TPU v7x, 32 devices: a whole 2x2x4 slice. The times are simulated.
32 devices in a mesh: head: 4 (over z), blk: 8 (over y, x, core).
Axes of the slice: x: 2, y: 2, z: 4, core: 2. Of those that a mesh axis runs over, the one named last changes fastest.
Arguments:
- tokens: bfloat16 [2, 2048, 1024], P(None, ('head', 'blk')), may hold values from -6 to 6
- positions: int32 [2, 2048], P(None, ('head', 'blk')), may hold values from 0 to 2047
- time_index: int32 [2], replicated, may hold values from 0 to 63
- time_table: float32 [64, 256], replicated, may hold values from -6 to 6
- w_qkv: bfloat16 [1024, 3072], P(('head', 'blk')), may hold values from -0.21875 to 0.21875
- w_out: bfloat16 [1024, 1024], P(('head', 'blk')), may hold values from -3 to 3
- w_up: bfloat16 [1024, 4096], P(('head', 'blk')), may hold values from -0.1875 to 0.1875
- w_down: bfloat16 [4096, 1024], P(('head', 'blk')), may hold values from -0.09375 to 0.09375
- scale_attn: bfloat16 [256, 1024], P(('head', 'blk')), may hold values from -0.19921875 to 0.19921875
- scale_mlp: bfloat16 [256, 1024], P(('head', 'blk')), may hold values from -0.19921875 to 0.19921875
- cotangent: bfloat16 [2, 2048, 1024], P(None, ('head', 'blk')), may hold values from -6 to 6
Outputs:
- output: bfloat16 [2, 2048, 1024], P(None, ('head', 'blk'))
- grad_tokens: float32 [2, 2048, 1024], P(None, ('head', 'blk'))
- grad_w_qkv: float32 [1024, 3072], P(('head', 'blk'))
- grad_w_out: float32 [1024, 1024], P(('head', 'blk'))
- grad_w_up: float32 [1024, 4096], P(('head', 'blk'))
- grad_w_down: float32 [4096, 1024], P(('head', 'blk'))
- grad_scale_attn: float32 [256, 1024], P(('head', 'blk'))
- grad_scale_mlp: float32 [256, 1024], P(('head', 'blk'))
All inputs are finite; a program needn't handle non-finite values.
Results may differ from a plain program's by a relative error of at most 0.017.
Values may be sent and summed in bfloat16 or wider, within the bound.
A program may use at most 256 MiB of HBM per device.

v0:
```python
import math

import jax
import jax.numpy as jnp
from jax import lax
from jax.sharding import PartitionSpec as P

HEADS = 16
HEAD_DIM = 64


NORM_EPSILON = 1e-05
PRECISE = lax.Precision.HIGHEST
START_TOP = -1e30
SCORE_SCALE = 0.125


def shifted(value, axis, steps):
    count = lax.axis_size(axis)
    pairs = [(source, (source + steps) % count) for source in range(count)]
    return lax.ppermute(value, axis, pairs)


def layer_norm(value, scale):
    centered = value - jnp.mean(value, axis=-1, keepdims=True)
    variance = jnp.mean(centered * centered, axis=-1, keepdims=True)
    return centered * lax.rsqrt(variance + NORM_EPSILON) * scale


def rotate(value, cosine_table, sine_table):
    half_dim = value.shape[-1] // 2
    first_half = value[..., :half_dim]
    second_half = value[..., half_dim:]
    return jnp.concatenate(
        [
            first_half * cosine_table - second_half * sine_table,
            second_half * cosine_table + first_half * sine_table,
        ],
        axis=-1,
    )


def rotary_tables(positions, head_dim):
    half_dim = head_dim // 2
    frequency = 10000.0 ** (-jnp.arange(half_dim, dtype=jnp.float32) / half_dim)
    turned = positions.astype(jnp.float32)[:, :, None, None] * frequency
    return (jnp.cos(turned), jnp.sin(turned))


def contract_rows(left, right):
    return lax.dot_general(
        left, right, (((0,), (0,)), ((), ())), preferred_element_type=jnp.float32
    )


def contract_cols(left, right):
    return lax.dot_general(
        left, right, (((1,), (1,)), ((), ())), preferred_element_type=jnp.float32
    )


def attend_step(running, query_block, key_block, value_block):
    row_top, row_sum, accum = running
    scores = (
        jnp.einsum("sqhd,skhd->sqhk", query_block, key_block, preferred_element_type=jnp.float32)
        * SCORE_SCALE
    )
    new_top = jnp.maximum(row_top, jnp.max(scores, axis=-1))
    shrink = jnp.exp(row_top - new_top)
    weights = jnp.exp(scores - new_top[..., None])
    row_sum = row_sum * shrink + jnp.sum(weights, axis=-1)
    accum = accum * shrink[..., None] + jnp.einsum(
        "sqhk,skhd->sqhd",
        weights.astype(jnp.bfloat16),
        value_block,
        preferred_element_type=jnp.float32,
    )
    return (new_top, row_sum, accum)


def back_step(query_block, key_block, value_block, grad_block, log_total, delta):
    scores = (
        jnp.einsum("sqhd,skhd->sqhk", query_block, key_block, preferred_element_type=jnp.float32)
        * SCORE_SCALE
    )
    probs = jnp.exp(scores - log_total[..., None])
    grad_values = jnp.einsum(
        "sqhk,sqhd->skhd",
        probs.astype(jnp.bfloat16),
        grad_block,
        preferred_element_type=jnp.float32,
    )
    grad_probs = jnp.einsum(
        "sqhd,skhd->sqhk", grad_block, value_block, preferred_element_type=jnp.float32
    )
    grad_scores = (probs * (grad_probs - delta[..., None])).astype(jnp.bfloat16)
    grad_query = jnp.einsum(
        "sqhk,skhd->sqhd", grad_scores, key_block, preferred_element_type=jnp.float32
    )
    grad_keys = jnp.einsum(
        "sqhk,sqhd->skhd", grad_scores, query_block, preferred_element_type=jnp.float32
    )
    return (grad_query, grad_keys, grad_values)


def local(
    tokens,
    positions,
    time_index,
    time_table,
    w_qkv,
    w_out,
    w_up,
    w_down,
    scale_attn,
    scale_mlp,
    cotangent,
):
    seq_count, row_count, model_width = tokens.shape
    group_count = lax.axis_size("head")
    local_heads = HEADS // group_count
    feature_width = local_heads * HEAD_DIM
    flat_rows = seq_count * row_count
    gathered = (
        lax.all_gather(w_qkv, ("head", "blk"), axis=0, tiled=True),
        lax.all_gather(w_out, ("head", "blk"), axis=0, tiled=True),
        lax.all_gather(w_up, ("head", "blk"), axis=0, tiled=True),
        lax.all_gather(w_down, ("head", "blk"), axis=0, tiled=True),
        lax.all_gather(scale_attn, ("head", "blk"), axis=0, tiled=True),
        lax.all_gather(scale_mlp, ("head", "blk"), axis=0, tiled=True),
    )
    full_qkv, full_out, full_up, full_down, full_scale_attn, full_scale_mlp = gathered
    step_count = time_table.shape[0]
    picker = (time_index[:, None] == jnp.arange(step_count, dtype=jnp.int32)[None, :]).astype(
        jnp.float32
    )
    time_embed = jnp.dot(picker, time_table, precision=PRECISE)
    scale_one = 1.0 + jnp.dot(time_embed, full_scale_attn.astype(jnp.float32), precision=PRECISE)
    scale_two = 1.0 + jnp.dot(time_embed, full_scale_mlp.astype(jnp.float32), precision=PRECISE)
    token_float = tokens.astype(jnp.float32)
    normed = (
        layer_norm(token_float, scale_one[:, None, :])
        .astype(jnp.bfloat16)
        .reshape(flat_rows, model_width)
    )
    projected = jnp.dot(normed, full_qkv, preferred_element_type=jnp.float32).reshape(
        seq_count, row_count, 3, HEADS, HEAD_DIM
    )
    cosine_table, sine_table = rotary_tables(positions, HEAD_DIM)
    query_tok = rotate(projected[:, :, 0], cosine_table, sine_table)
    keys_tok = rotate(projected[:, :, 1], cosine_table, sine_table)
    packed = (
        jnp.stack([query_tok, keys_tok, projected[:, :, 2]], axis=2)
        .reshape(seq_count, row_count, 3, model_width)
        .astype(jnp.bfloat16)
    )
    regrouped = lax.all_to_all(packed, "head", split_axis=3, concat_axis=1, tiled=True)
    block_len = regrouped.shape[1]
    local_query = regrouped[:, :, 0].reshape(seq_count, block_len, local_heads, HEAD_DIM)
    local_keys = regrouped[:, :, 1]
    local_values = regrouped[:, :, 2]
    start_state = (
        jnp.full((seq_count, block_len, local_heads), START_TOP, jnp.float32),
        jnp.zeros((seq_count, block_len, local_heads), jnp.float32),
        jnp.zeros((seq_count, block_len, local_heads, HEAD_DIM), jnp.float32),
    )
    key_piece = lax.all_gather(local_keys, "blk", axis=1, tiled=True)
    value_piece = lax.all_gather(local_values, "blk", axis=1, tiled=True)
    piece_len = key_piece.shape[1]
    step_len = math.gcd(piece_len, block_len)

    def one_block(index, state):
        key_block = lax.dynamic_slice_in_dim(key_piece, index * step_len, step_len, 1).reshape(
            seq_count, step_len, local_heads, HEAD_DIM
        )
        value_block = lax.dynamic_slice_in_dim(value_piece, index * step_len, step_len, 1).reshape(
            seq_count, step_len, local_heads, HEAD_DIM
        )
        return attend_step(state, local_query, key_block, value_block)

    row_top, row_sum, accum = lax.fori_loop(0, piece_len // step_len, one_block, start_state)
    mixed = accum / row_sum[..., None]
    log_total = row_top + jnp.log(row_sum)
    attended_heads = mixed.astype(jnp.bfloat16).reshape(seq_count, block_len, feature_width)
    attended = lax.all_to_all(
        attended_heads, "head", split_axis=1, concat_axis=2, tiled=True
    ).reshape(flat_rows, model_width)
    branch = jnp.dot(attended, full_out, preferred_element_type=jnp.float32)
    middle = token_float + branch.reshape(seq_count, row_count, model_width)
    normed_two = (
        layer_norm(middle, scale_two[:, None, :])
        .astype(jnp.bfloat16)
        .reshape(flat_rows, model_width)
    )
    hidden = jnp.dot(normed_two, full_up, preferred_element_type=jnp.float32)
    active = jax.nn.gelu(hidden, approximate=False).astype(jnp.bfloat16)
    result = middle.reshape(flat_rows, model_width) + jnp.dot(
        active, full_down, preferred_element_type=jnp.float32
    )
    output = result.astype(jnp.bfloat16).reshape(seq_count, row_count, model_width)
    back_qkv, back_out, back_up, back_down = (
        lax.all_gather(w_qkv, ("head", "blk"), axis=0, tiled=True),
        lax.all_gather(w_out, ("head", "blk"), axis=0, tiled=True),
        lax.all_gather(w_up, ("head", "blk"), axis=0, tiled=True),
        lax.all_gather(w_down, ("head", "blk"), axis=0, tiled=True),
    )
    grad_out = cotangent.reshape(flat_rows, model_width)
    grad_active = contract_cols(grad_out, back_down)
    grad_w_down = contract_rows(active, grad_out)
    gelu_value, gelu_pull = jax.vjp(lambda entry: jax.nn.gelu(entry, approximate=False), hidden)
    grad_hidden = gelu_pull(grad_active)[0].astype(jnp.bfloat16)
    grad_w_up = contract_rows(normed_two, grad_hidden)
    grad_normed_two = contract_cols(grad_hidden, back_up).reshape(seq_count, row_count, model_width)
    norm_value, norm_pull = jax.vjp(layer_norm, middle, scale_two[:, None, :])
    grad_middle_norm, grad_scale_two = norm_pull(grad_normed_two)
    grad_middle = cotangent.astype(jnp.float32) + grad_middle_norm
    grad_scale_mlp = jnp.dot(time_embed.T, grad_scale_two[:, 0, :], precision=PRECISE)
    grad_branch = grad_middle.reshape(flat_rows, model_width).astype(jnp.bfloat16)
    grad_w_out = contract_rows(attended, grad_branch)
    grad_attended = (
        contract_cols(grad_branch, back_out)
        .astype(jnp.bfloat16)
        .reshape(seq_count, row_count, model_width)
    )
    grad_heads = lax.all_to_all(
        grad_attended, "head", split_axis=2, concat_axis=1, tiled=True
    ).reshape(seq_count, block_len, local_heads, HEAD_DIM)
    delta = jnp.sum(grad_heads.astype(jnp.float32) * mixed, axis=-1)

    def turn(index, state):
        key_now, value_now, grad_keys_now, grad_values_now, grad_query_sum = state
        grad_query, grad_keys, grad_values = back_step(
            local_query,
            key_now.reshape(seq_count, block_len, local_heads, HEAD_DIM),
            value_now.reshape(seq_count, block_len, local_heads, HEAD_DIM),
            grad_heads,
            log_total,
            delta,
        )
        moved_keys, moved_values = shifted((key_now, value_now), "blk", 1)
        moved_grad_keys, moved_grad_values = (
            shifted(
                (grad_keys_now + grad_keys.reshape(seq_count, block_len, feature_width)).astype(
                    jnp.bfloat16
                ),
                "blk",
                1,
            ).astype(jnp.float32),
            shifted(
                (grad_values_now + grad_values.reshape(seq_count, block_len, feature_width)).astype(
                    jnp.bfloat16
                ),
                "blk",
                1,
            ).astype(jnp.float32),
        )
        return (
            moved_keys,
            moved_values,
            moved_grad_keys,
            moved_grad_values,
            grad_query_sum + grad_query,
        )

    zero_kv = jnp.zeros((seq_count, block_len, feature_width), jnp.float32)
    begin = (
        local_keys,
        local_values,
        zero_kv,
        zero_kv,
        jnp.zeros((seq_count, block_len, local_heads, HEAD_DIM), jnp.float32),
    )
    final_state = lax.fori_loop(0, lax.axis_size("blk"), turn, begin)
    grad_keys_own = final_state[2]
    grad_values_own = final_state[3]
    grad_query_all = final_state[4]
    stacked = jnp.stack(
        [
            grad_query_all.reshape(seq_count, block_len, feature_width) * SCORE_SCALE,
            grad_keys_own * SCORE_SCALE,
            grad_values_own,
        ],
        axis=2,
    ).astype(jnp.bfloat16)
    returned = lax.all_to_all(stacked, "head", split_axis=1, concat_axis=3, tiled=True)
    grad_query_tok = (
        returned[:, :, 0].astype(jnp.float32).reshape(seq_count, row_count, HEADS, HEAD_DIM)
    )
    grad_keys_tok = (
        returned[:, :, 1].astype(jnp.float32).reshape(seq_count, row_count, HEADS, HEAD_DIM)
    )
    grad_values_tok = (
        returned[:, :, 2].astype(jnp.float32).reshape(seq_count, row_count, HEADS, HEAD_DIM)
    )
    grad_projected = (
        jnp.stack(
            [
                rotate(grad_query_tok, cosine_table, -sine_table),
                rotate(grad_keys_tok, cosine_table, -sine_table),
                grad_values_tok,
            ],
            axis=2,
        )
        .reshape(flat_rows, 3 * model_width)
        .astype(jnp.bfloat16)
    )
    grad_w_qkv = contract_rows(normed, grad_projected)
    grad_normed = contract_cols(grad_projected, back_qkv).reshape(seq_count, row_count, model_width)
    first_value, first_pull = jax.vjp(layer_norm, token_float, scale_one[:, None, :])
    grad_token_norm, grad_scale_one = first_pull(grad_normed)
    grad_tokens = grad_middle + grad_token_norm
    grad_scale_attn = jnp.dot(time_embed.T, grad_scale_one[:, 0, :], precision=PRECISE)
    shards = (
        lax.psum_scatter(grad_w_qkv, ("head", "blk"), scatter_dimension=0, tiled=True),
        lax.psum_scatter(grad_w_out, ("head", "blk"), scatter_dimension=0, tiled=True),
        lax.psum_scatter(grad_w_up, ("head", "blk"), scatter_dimension=0, tiled=True),
        lax.psum_scatter(grad_w_down, ("head", "blk"), scatter_dimension=0, tiled=True),
        lax.psum_scatter(grad_scale_attn, ("head", "blk"), scatter_dimension=0, tiled=True),
        lax.psum_scatter(grad_scale_mlp, ("head", "blk"), scatter_dimension=0, tiled=True),
    )
    return (output, grad_tokens, shards[0], shards[1], shards[2], shards[3], shards[4], shards[5])


def solution(mesh):
    placed = (
        P(None, ("head", "blk"), None),
        P(None, ("head", "blk")),
        P(),
        P(),
        P(("head", "blk"), None),
        P(("head", "blk"), None),
        P(("head", "blk"), None),
        P(("head", "blk"), None),
        P(("head", "blk"), None),
        P(("head", "blk"), None),
        P(None, ("head", "blk"), None),
    )
    return jax.shard_map(
        local,
        mesh=mesh,
        in_specs=placed,
        out_specs=(
            P(None, ("head", "blk"), None),
            P(None, ("head", "blk"), None),
            P(("head", "blk"), None),
            P(("head", "blk"), None),
            P(("head", "blk"), None),
            P(("head", "blk"), None),
            P(("head", "blk"), None),
            P(("head", "blk"), None),
        ),
        check_vma=False,
    )
```

profile of v0, /device:TPU:0, one launch (start us, length us, event | category | flops | bytes accessed | tf_op | source)
XLA Modules:
  0.0 1571.1 jit_solution(9554093618369805315)
XLA Ops:
  12.5 45.7 %all_gather.28 = bf16[256,1024]{1,0:T(8,128)(2,1)S(1)} all-gather(bf16[8,1024]{1,0:T(8,128)(2,1)} %param.23), channel_id=1, replica_groups=mesh['head'=4,'blk'=8] {'head','blk'}, dimensions={0}, use_global_device_ids=true | all-gather | bytes 540672 | tf_op jit(solution)/shard_map/all_gather | solution.py:129
  58.8 25.1 %all-gather.9.cloned.1.call-done = bf16[1024,3072]{1,0:T(8,128)(2,1)} async-done(((bf16[32,3072]{1,0:T(8,128)(2,1)}), bf16[1024,3072]{1,0:T(8,128)(2,1)}) %all-gather.9.cloned.1.call-update) | async-done | bytes 6291472 | tf_op jit(solution)/shard_map/all_gather | solution.py:125
  84.0 8.6 copy.148
  92.6 4.5 fusion.47
  99.6 2.9 fusion.60
  103.9 23.4 %all_to_all.66 = bf16[4,2,49152]{2,1,0:T(2,128)(2,1)S(1)} all-to-all(bf16[4,2,49152]{2,1,0:T(2,128)(2,1)S(1)} %reshape.240), channel_id=1, replica_groups=mesh['head'=4,'blk'=8] {'head'}, dimensions={0} | all-to-all | bytes 1572864 | tf_op jit(solution)/shard_map/all_to_all | solution.py:157
  128.5 2.3 copy.182
  134.6 23.5 %all-gather.17.cloned.1.call-done = bf16[2,2048,1,256]{3,1,2,0:T(8,128)(2,1)} async-done(((bf16[2,256,1,256]{3,1,2,0:T(8,128)(2,1)}), bf16[2,2048,1,256]{3,1,2,0:T(8,128)(2,1)}) %all-gather.17.cloned.1.call-update) | async-done | bytes 2097168 | tf_op jit(solution)/shard_map/all_gather | solution.py:167
  158.2 30.4 %all-gather.19.cloned.1.call-done = bf16[2,2048,1,256]{3,1,2,0:T(8,128)(2,1)} async-done(((bf16[2,256,1,256]{3,1,2,0:T(8,128)(2,1)}), bf16[2,2048,1,256]{3,1,2,0:T(8,128)(2,1)}) %all-gather.19.cloned.1.call-update) | async-done | bytes 2097168 | tf_op jit(solution)/shard_map/all_gather | solution.py:168
  188.6 22.7 %while.37 = (s32[]{:T(128)}, f32[2,256,4]{1,2,0:T(4,128)S(1)}, f32[2,256,4]{1,2,0:T(4,128)S(1)}, f32[2,256,4,64]{1,3,2,0:T(8,128)S(1)}, bf16[2,2048,256]{2,1,0:T...) while((s32[]{:T(128)}, f32[2,256,4]{1,2,0:T(4,128)S(1)}, ...), condition=%wide.region_5.0_spmd.clone, body=%wide.region_2.0_spmd.clone.sunk | while | flops 138815488 | bytes 10354867 | solution.py:181
  212.2 4.6 all-to-all-start.1
  216.8 42.8 %all_gather.33 = bf16[256,1024]{1,0:T(8,128)(2,1)S(1)} all-gather(bf16[8,1024]{1,0:T(8,128)(2,1)S(1)} %copy-done.38), channel_id=1, replica_groups=mesh['head'=4,'blk'=8] {'head','blk'}, dimensions={0}, use_global_device_ids=true | all-gather | bytes 540672 | tf_op jit(solution)/shard_map/all_gather | solution.py:130
  260.7 2.1 fusion.59
  263.9 64.3 %all-gather.13.cloned.1.call-done = bf16[1024,4096]{1,0:T(8,128)(2,1)} async-done(((bf16[32,4096]{1,0:T(8,128)(2,1)}), bf16[1024,4096]{1,0:T(8,128)(2,1)}) %all-gather.13.cloned.1.call-update) | async-done | bytes 8388624 | tf_op jit(solution)/shard_map/all_gather | solution.py:127
  328.2 4.7 fusion.63
  333.0 74.0 %all-gather.15.cloned.1.call-done = bf16[4096,1024]{1,0:T(8,128)(2,1)} async-done(((bf16[128,1024]{1,0:T(8,128)(2,1)}), bf16[4096,1024]{1,0:T(8,128)(2,1)}) %all-gather.15.cloned.1.call-update) | async-done | bytes 8388624 | tf_op jit(solution)/shard_map/all_gather | solution.py:128
  407.0 10.4 add_convert_fusion
  417.4 2.9 fusion.64
  422.4 2.5 convolution_convert_fusion
  426.4 3.6 all-to-all-start.2
  431.8 7.8 all-to-all-done.2
  442.5 169.7 %while.38 = (s32[]{:T(128)}, bf16[2,256,256]{1,2,0:T(8,128)(2,1)}, bf16[2,256,256]{1,2,0:T(8,128)(2,1)}, f32[2,256,256]{1,2,0:T(8,128)}, f32[2,256,256]{1,2,0:T(...) while((s32[]{:T(128)}, bf16[2,256,256]{1,2,0:T(8,128)(2,1)}, ...), condition=%wide.region_12.0_spmd.clone, body=%wide.region_11.0_spmd.clone.sunk | while | flops 341049344 | bytes 24928572 | solution.py:273
  451.8 1.9 fusion.157
  456.8 2.1 fusion.160
  460.6 1.8 convert_element_type.211
  472.6 2.0 fusion.157
  477.8 2.3 fusion.160
  481.7 1.8 convert_element_type.211
  493.7 2.0 fusion.157
  498.8 2.3 fusion.160
  502.7 1.8 convert_element_type.211
  514.7 2.0 fusion.157
  518.2 2.5 collective-permute-start.3
  520.7 2.3 fusion.160
  523.7 1.8 convert_element_type.211
  536.5 2.0 fusion.157
  541.7 2.3 fusion.160
  545.5 1.8 convert_element_type.211
  557.6 2.0 fusion.157
  562.7 2.3 fusion.160
  566.6 1.8 convert_element_type.211
  578.6 2.0 fusion.157
  583.7 2.3 fusion.160
  599.6 2.0 fusion.157
  603.1 2.5 collective-permute-start.3
  605.6 2.3 fusion.160
  615.5 1.9 copy.168
  617.4 3.5 all-to-all-start.3
  620.9 2.0 fusion.70
  623.0 17.8 %all-to-all-done.3 = bf16[2,256,3,256]{3,0,2,1:T(2,128)(2,1)S(1)} async-done(((bf16[2,256,3,256]{3,0,2,1:T(2,128)(2,1)}), bf16[2,256,3,256]{3,0,2,1:T(2,128)(2,1)S(1)}, u32[]{:S(2)}, u32[]{:S(2)}) %all-to-all-start.3) | async-done | bytes 786464 | tf_op jit(solution)/shard_map/all_to_all | solution.py:285
  646.8 5.1 fusion.44
  652.3 2.0 fusion.69
  654.7 2.7 fusion.66
  658.9 6.3 fusion.65
  666.5 8.1 fusion.67
  674.7 2.5 multiply_convert_fusion
  677.2 8.1 fusion.68
  686.4 5.4 fusion.34
  693.1 66.8 %reduce-scatter.17.cloned.1.call-done = f32[8,1024]{1,0:T(8,128)} async-done(((f32[256,1024]{1,0:T(8,128)}), f32[8,1024]{1,0:T(8,128)}) %reduce-scatter.17.cloned.1.call-update) | async-done | bytes 32784 | tf_op jit(solution)/shard_map/reduce_scatter | solution.py:319
  759.9 133.8 %reduce-scatter.15.cloned.1.call-done = f32[8,1024]{1,0:T(8,128)} async-done(((f32[256,1024]{1,0:T(8,128)}), f32[8,1024]{1,0:T(8,128)}) %reduce-scatter.15.cloned.1.call-update) | async-done | bytes 32784 | tf_op jit(solution)/shard_map/reduce_scatter | solution.py:318
  893.8 139.6 %reduce-scatter.9.cloned.1.call-done = f32[32,1024]{1,0:T(8,128)} async-done(((f32[1024,1024]{1,0:T(8,128)}), f32[32,1024]{1,0:T(8,128)}) %reduce-scatter.9.cloned.1.call-update) | async-done | bytes 131088 | tf_op jit(solution)/shard_map/reduce_scatter | solution.py:315
  1033.3 158.2 %reduce-scatter.7.cloned.1.call-done = f32[32,3072]{1,0:T(8,128)} async-done(((f32[1024,3072]{1,0:T(8,128)}), f32[32,3072]{1,0:T(8,128)}) %reduce-scatter.7.cloned.1.call-update) | async-done | bytes 393232 | tf_op jit(solution)/shard_map/reduce_scatter | solution.py:314
  1191.5 185.0 %reduce-scatter.11.cloned.1.call-done = f32[32,4096]{1,0:T(8,128)} async-done(((f32[1024,4096]{1,0:T(8,128)}), f32[32,4096]{1,0:T(8,128)}) %reduce-scatter.11.cloned.1.call-update) | async-done | bytes 524304 | tf_op jit(solution)/shard_map/reduce_scatter | solution.py:316
  1376.5 187.3 %reduce-scatter.13.cloned.1.call-done = f32[128,1024]{1,0:T(8,128)} async-done(((f32[4096,1024]{1,0:T(8,128)}), f32[128,1024]{1,0:T(8,128)}) %reduce-scatter.13.cloned.1.call-update) | async-done | bytes 524304 | tf_op jit(solution)/shard_map/reduce_scatter | solution.py:317
  (401 shorter events, 182.7 us)
Async XLA Ops:
  7.2 51.4 %copy-start.8 = (bf16[2,64,1024]{2,1,0:T(8,128)(2,1)S(1)}, bf16[2,64,1024]{2,1,0:T(8,128)(2,1)}, u32[]{:S(2)}) copy-start(bf16[2,64,1024]{2,1,0:T(8,128)(2,1)} %param.15) | copy-start | bytes 786436
  7.2 76.8 %all-gather.9.cloned.1.call-start = ((), (), s32[]{:S(2)}) async-start(), calls=%async_computation.10 | async-start | bytes 6488064 | tf_op jit(solution)/shard_map/all_gather | solution.py:125
  7.9 150.2 %all-gather.17.cloned.1.call-start = ((), (), s32[]{:S(2)}) async-start(), calls=%async_computation.20 | async-start | bytes 2359296 | tf_op jit(solution)/shard_map/all_gather | solution.py:167
  9.7 82.9 %copy-start.32 = (f32[2,64]{1,0:T(2,128)}, f32[2,64]{1,0:T(2,128)S(1)}, u32[]{:S(2)}) copy-start(f32[2,64]{1,0:T(2,128)S(1)} %broadcast_multiply_fusion.1) | copy-start | bytes 1540
  11.5 81.1 %copy-start.34 = (f32[2,64]{1,0:T(2,128)}, f32[2,64]{1,0:T(2,128)S(1)}, u32[]{:S(2)}) copy-start(f32[2,64]{1,0:T(2,128)S(1)} %fusion.55) | copy-start | bytes 1540
  12.3 46.0 %copy-start.26 = (f32[2,256]{1,0:T(2,128)}, f32[2,256]{1,0:T(2,128)S(1)}, u32[]{:S(2)}) copy-start(f32[2,256]{1,0:T(2,128)S(1)} %fusion.52) | copy-start | bytes 6148
  58.8 33.8 %copy-start.24 = (bf16[2,64,1024]{2,1,0:T(8,128)(2,1)}, bf16[2,64,1024]{2,1,0:T(8,128)(2,1)S(1)}, u32[]{:S(2)}) copy-start(bf16[2,64,1024]{2,1,0:T(8,128)(2,1)S(1)} %fusion.41) | copy-start | bytes 786436
  132.0 56.6 %all-gather.19.cloned.1.call-start = ((), (), s32[]{:S(2)}) async-start(), calls=%async_computation.21 | async-start | bytes 2359296 | tf_op jit(solution)/shard_map/all_gather | solution.py:168
  132.7 127.3 %all-gather.11.cloned.1.call-start = ((), (), s32[]{:S(2)}) async-start(), calls=%async_computation.11 | async-start | bytes 2162688 | tf_op jit(solution)/shard_map/all_gather | solution.py:126
  133.3 194.9 %all-gather.13.cloned.1.call-start = ((), (), s32[]{:S(2)}) async-start(), calls=%async_computation.12 | async-start | bytes 8650752 | tf_op jit(solution)/shard_map/all_gather | solution.py:127
  133.9 273.1 %all-gather.15.cloned.1.call-start = ((), (), s32[]{:S(2)}) async-start(), calls=%async_computation.13 | async-start | bytes 8650752 | tf_op jit(solution)/shard_map/all_gather | solution.py:128
  188.6 28.2 %copy-start.38 = (bf16[8,1024]{1,0:T(8,128)(2,1)S(1)}, bf16[8,1024]{1,0:T(8,128)(2,1)}, u32[]{:S(2)}) copy-start(bf16[8,1024]{1,0:T(8,128)(2,1)} %param.24) | copy-start | bytes 49156
  211.3 48.3 %copy-start.27 = (f32[2,256]{1,0:T(2,128)S(1)}, f32[2,256]{1,0:T(2,128)}, u32[]{:S(2)}) copy-start(f32[2,256]{1,0:T(2,128)} %copy-done.26) | copy-start | bytes 6148
  211.3 49.4 %copy-start.9 = (bf16[2,64,1024]{2,1,0:T(8,128)(2,1)S(1)}, bf16[2,64,1024]{2,1,0:T(8,128)(2,1)}, u32[]{:S(2)}) copy-start(bf16[2,64,1024]{2,1,0:T(8,128)(2,1)} %param.15) | copy-start | bytes 786436
  212.2 47.7 %all-to-all-start.1 = ((bf16[2,256,256]{2,0,1:T(2,128)(2,1)}), bf16[2,256,256]{2,0,1:T(2,128)(2,1)S(1)}, u32[]{:S(2)}, u32[]{:S(2)}) async-start(bf16[2,256,256]{2,0,1:T(2,128)(2,1)} %copy.158), calls=%async_computation.1 | async-start | bytes 524288 | tf_op jit(solution)/shard_map/all_to_all | solution.py:185
  262.8 158.1 %copy-start.3 = (f32[2,64,1024]{2,1,0:T(8,128)}, f32[2,64,1024]{2,1,0:T(8,128)S(1)}, u32[]{:S(2)}) copy-start(f32[2,64,1024]{2,1,0:T(8,128)S(1)} %get-tuple-element.408) | copy-start | bytes 1572868
  262.8 158.1 %copy-start.28 = (f32[2,64]{1,0:T(2,128)}, f32[2,64]{1,0:T(2,128)S(1)}, u32[]{:S(2)}) copy-start(f32[2,64]{1,0:T(2,128)S(1)} %broadcast_multiply_fusion) | copy-start | bytes 1540
  263.0 157.9 %copy-start.30 = (f32[2,64]{1,0:T(2,128)}, f32[2,64]{1,0:T(2,128)S(1)}, u32[]{:S(2)}) copy-start(f32[2,64]{1,0:T(2,128)S(1)} %fusion.56) | copy-start | bytes 1540
  332.9 84.5 %copy-start.11 = (f32[128,4096]{1,0:T(8,128)}, f32[128,4096]{1,0:T(8,128)S(1)}, u32[]{:S(2)}) copy-start(f32[128,4096]{1,0:T(8,128)S(1)} %fusion.63) | copy-start | bytes 6291460
  407.0 10.4 copy-start.2
  422.4 7.7 copy-start.23
  422.4 8.5 copy-start.22
  426.4 13.2 all-to-all-start.2
  444.1 20.0 %collective-permute-start = (bf16[2,256,256]{1,2,0:T(8,128)(2,1)}, bf16[2,256,256]{1,2,0:T(8,128)(2,1)}, u32[]{:S(2)}, u32[]{:S(2)}) collective-permute-start(bf16[2,256,256]{1,2,0:T(8,128)(2,1)} %copy.218), channel_id=1, source_target_pairs={{0,1},{1,2},{2,3},{3,4},{4,5},{5,6},{6,7},{7,0},{8,9},{9,10},{10,1... | collective-permute-start | bytes 786440 | tf_op jit(solution)/shard_map/while/body/eval_jaxpr/ppermute | solution.py:21
  445.8 18.4 %collective-permute-start.1 = (bf16[2,256,256]{1,2,0:T(8,128)(2,1)}, bf16[2,256,256]{1,2,0:T(8,128)(2,1)}, u32[]{:S(2)}, u32[]{:S(2)}) collective-permute-start(bf16[2,256,256]{1,2,0:T(8,128)(2,1)} %copy.219), channel_id=1, source_target_pairs={{0,1},{1,2},{2,3},{3,4},{4,5},{5,6},{6,7},{7,0},{8,9},{9,10},{10,1... | collective-permute-start | bytes 786440 | tf_op jit(solution)/shard_map/while/body/eval_jaxpr/ppermute | solution.py:21
  453.6 7.0 collective-permute-start.2
  455.2 8.2 collective-permute-start.3
  465.9 19.4 %collective-permute-start = (bf16[2,256,256]{1,2,0:T(8,128)(2,1)}, bf16[2,256,256]{1,2,0:T(8,128)(2,1)}, u32[]{:S(2)}, u32[]{:S(2)}) collective-permute-start(bf16[2,256,256]{1,2,0:T(8,128)(2,1)} %copy.218), channel_id=1, source_target_pairs={{0,1},{1,2},{2,3},{3,4},{4,5},{5,6},{6,7},{7,0},{8,9},{9,10},{10,1... | collective-permute-start | bytes 786440 | tf_op jit(solution)/shard_map/while/body/eval_jaxpr/ppermute | solution.py:21
  467.5 17.7 %collective-permute-start.1 = (bf16[2,256,256]{1,2,0:T(8,128)(2,1)}, bf16[2,256,256]{1,2,0:T(8,128)(2,1)}, u32[]{:S(2)}, u32[]{:S(2)}) collective-permute-start(bf16[2,256,256]{1,2,0:T(8,128)(2,1)} %copy.219), channel_id=1, source_target_pairs={{0,1},{1,2},{2,3},{3,4},{4,5},{5,6},{6,7},{7,0},{8,9},{9,10},{10,1... | collective-permute-start | bytes 786440 | tf_op jit(solution)/shard_map/while/body/eval_jaxpr/ppermute | solution.py:21
  474.7 7.0 collective-permute-start.2
  476.2 8.2 collective-permute-start.3
  486.9 19.3 %collective-permute-start = (bf16[2,256,256]{1,2,0:T(8,128)(2,1)}, bf16[2,256,256]{1,2,0:T(8,128)(2,1)}, u32[]{:S(2)}, u32[]{:S(2)}) collective-permute-start(bf16[2,256,256]{1,2,0:T(8,128)(2,1)} %copy.218), channel_id=1, source_target_pairs={{0,1},{1,2},{2,3},{3,4},{4,5},{5,6},{6,7},{7,0},{8,9},{9,10},{10,1... | collective-permute-start | bytes 786440 | tf_op jit(solution)/shard_map/while/body/eval_jaxpr/ppermute | solution.py:21
  488.6 17.7 %collective-permute-start.1 = (bf16[2,256,256]{1,2,0:T(8,128)(2,1)}, bf16[2,256,256]{1,2,0:T(8,128)(2,1)}, u32[]{:S(2)}, u32[]{:S(2)}) collective-permute-start(bf16[2,256,256]{1,2,0:T(8,128)(2,1)} %copy.219), channel_id=1, source_target_pairs={{0,1},{1,2},{2,3},{3,4},{4,5},{5,6},{6,7},{7,0},{8,9},{9,10},{10,1... | collective-permute-start | bytes 786440 | tf_op jit(solution)/shard_map/while/body/eval_jaxpr/ppermute | solution.py:21
  495.7 7.0 collective-permute-start.2
  497.2 8.2 collective-permute-start.3
  507.9 19.3 %collective-permute-start = (bf16[2,256,256]{1,2,0:T(8,128)(2,1)}, bf16[2,256,256]{1,2,0:T(8,128)(2,1)}, u32[]{:S(2)}, u32[]{:S(2)}) collective-permute-start(bf16[2,256,256]{1,2,0:T(8,128)(2,1)} %copy.218), channel_id=1, source_target_pairs={{0,1},{1,2},{2,3},{3,4},{4,5},{5,6},{6,7},{7,0},{8,9},{9,10},{10,1... | collective-permute-start | bytes 786440 | tf_op jit(solution)/shard_map/while/body/eval_jaxpr/ppermute | solution.py:21
  509.6 17.6 %collective-permute-start.1 = (bf16[2,256,256]{1,2,0:T(8,128)(2,1)}, bf16[2,256,256]{1,2,0:T(8,128)(2,1)}, u32[]{:S(2)}, u32[]{:S(2)}) collective-permute-start(bf16[2,256,256]{1,2,0:T(8,128)(2,1)} %copy.219), channel_id=1, source_target_pairs={{0,1},{1,2},{2,3},{3,4},{4,5},{5,6},{6,7},{7,0},{8,9},{9,10},{10,1... | collective-permute-start | bytes 786440 | tf_op jit(solution)/shard_map/while/body/eval_jaxpr/ppermute | solution.py:21
  516.7 7.0 collective-permute-start.2
  518.2 8.2 collective-permute-start.3
  528.9 20.2 %collective-permute-start = (bf16[2,256,256]{1,2,0:T(8,128)(2,1)}, bf16[2,256,256]{1,2,0:T(8,128)(2,1)}, u32[]{:S(2)}, u32[]{:S(2)}) collective-permute-start(bf16[2,256,256]{1,2,0:T(8,128)(2,1)} %copy.218), channel_id=1, source_target_pairs={{0,1},{1,2},{2,3},{3,4},{4,5},{5,6},{6,7},{7,0},{8,9},{9,10},{10,1... | collective-permute-start | bytes 786440 | tf_op jit(solution)/shard_map/while/body/eval_jaxpr/ppermute | solution.py:21
  530.6 18.5 %collective-permute-start.1 = (bf16[2,256,256]{1,2,0:T(8,128)(2,1)}, bf16[2,256,256]{1,2,0:T(8,128)(2,1)}, u32[]{:S(2)}, u32[]{:S(2)}) collective-permute-start(bf16[2,256,256]{1,2,0:T(8,128)(2,1)} %copy.219), channel_id=1, source_target_pairs={{0,1},{1,2},{2,3},{3,4},{4,5},{5,6},{6,7},{7,0},{8,9},{9,10},{10,1... | collective-permute-start | bytes 786440 | tf_op jit(solution)/shard_map/while/body/eval_jaxpr/ppermute | solution.py:21
  538.5 7.0 collective-permute-start.2
  540.1 8.2 collective-permute-start.3
  550.8 19.4 %collective-permute-start = (bf16[2,256,256]{1,2,0:T(8,128)(2,1)}, bf16[2,256,256]{1,2,0:T(8,128)(2,1)}, u32[]{:S(2)}, u32[]{:S(2)}) collective-permute-start(bf16[2,256,256]{1,2,0:T(8,128)(2,1)} %copy.218), channel_id=1, source_target_pairs={{0,1},{1,2},{2,3},{3,4},{4,5},{5,6},{6,7},{7,0},{8,9},{9,10},{10,1... | collective-permute-start | bytes 786440 | tf_op jit(solution)/shard_map/while/body/eval_jaxpr/ppermute | solution.py:21
  552.4 17.7 %collective-permute-start.1 = (bf16[2,256,256]{1,2,0:T(8,128)(2,1)}, bf16[2,256,256]{1,2,0:T(8,128)(2,1)}, u32[]{:S(2)}, u32[]{:S(2)}) collective-permute-start(bf16[2,256,256]{1,2,0:T(8,128)(2,1)} %copy.219), channel_id=1, source_target_pairs={{0,1},{1,2},{2,3},{3,4},{4,5},{5,6},{6,7},{7,0},{8,9},{9,10},{10,1... | collective-permute-start | bytes 786440 | tf_op jit(solution)/shard_map/while/body/eval_jaxpr/ppermute | solution.py:21
  559.6 7.0 collective-permute-start.2
  561.1 8.2 collective-permute-start.3
  571.8 19.3 %collective-permute-start = (bf16[2,256,256]{1,2,0:T(8,128)(2,1)}, bf16[2,256,256]{1,2,0:T(8,128)(2,1)}, u32[]{:S(2)}, u32[]{:S(2)}) collective-permute-start(bf16[2,256,256]{1,2,0:T(8,128)(2,1)} %copy.218), channel_id=1, source_target_pairs={{0,1},{1,2},{2,3},{3,4},{4,5},{5,6},{6,7},{7,0},{8,9},{9,10},{10,1... | collective-permute-start | bytes 786440 | tf_op jit(solution)/shard_map/while/body/eval_jaxpr/ppermute | solution.py:21
  573.5 17.7 %collective-permute-start.1 = (bf16[2,256,256]{1,2,0:T(8,128)(2,1)}, bf16[2,256,256]{1,2,0:T(8,128)(2,1)}, u32[]{:S(2)}, u32[]{:S(2)}) collective-permute-start(bf16[2,256,256]{1,2,0:T(8,128)(2,1)} %copy.219), channel_id=1, source_target_pairs={{0,1},{1,2},{2,3},{3,4},{4,5},{5,6},{6,7},{7,0},{8,9},{9,10},{10,1... | collective-permute-start | bytes 786440 | tf_op jit(solution)/shard_map/while/body/eval_jaxpr/ppermute | solution.py:21
  580.6 7.0 collective-permute-start.2
  582.1 8.2 collective-permute-start.3
  592.8 19.3 %collective-permute-start = (bf16[2,256,256]{1,2,0:T(8,128)(2,1)}, bf16[2,256,256]{1,2,0:T(8,128)(2,1)}, u32[]{:S(2)}, u32[]{:S(2)}) collective-permute-start(bf16[2,256,256]{1,2,0:T(8,128)(2,1)} %copy.218), channel_id=1, source_target_pairs={{0,1},{1,2},{2,3},{3,4},{4,5},{5,6},{6,7},{7,0},{8,9},{9,10},{10,1... | collective-permute-start | bytes 786440 | tf_op jit(solution)/shard_map/while/body/eval_jaxpr/ppermute | solution.py:21
  594.5 17.6 %collective-permute-start.1 = (bf16[2,256,256]{1,2,0:T(8,128)(2,1)}, bf16[2,256,256]{1,2,0:T(8,128)(2,1)}, u32[]{:S(2)}, u32[]{:S(2)}) collective-permute-start(bf16[2,256,256]{1,2,0:T(8,128)(2,1)} %copy.219), channel_id=1, source_target_pairs={{0,1},{1,2},{2,3},{3,4},{4,5},{5,6},{6,7},{7,0},{8,9},{9,10},{10,1... | collective-permute-start | bytes 786440 | tf_op jit(solution)/shard_map/while/body/eval_jaxpr/ppermute | solution.py:21
  601.6 7.0 collective-permute-start.2
  603.1 8.2 collective-permute-start.3
  617.4 23.4 %all-to-all-start.3 = ((bf16[2,256,3,256]{3,0,2,1:T(2,128)(2,1)}), bf16[2,256,3,256]{3,0,2,1:T(2,128)(2,1)S(1)}, u32[]{:S(2)}, u32[]{:S(2)}) async-start(bf16[2,256,3,256]{3,0,2,1:T(2,128)(2,1)} %copy.168), calls=%async_computation.3 | async-start | bytes 1572864 | tf_op jit(solution)/shard_map/all_to_all | solution.py:285
  620.9 139.1 %reduce-scatter.17.cloned.1.call-start = ((), (), s32[]{:S(2)}) async-start(), calls=%async_computation.19 | async-start | bytes 1081344 | tf_op jit(solution)/shard_map/reduce_scatter | solution.py:319
  623.0 270.8 %reduce-scatter.15.cloned.1.call-start = ((), (), s32[]{:S(2)}) async-start(), calls=%async_computation.18 | async-start | bytes 1081344 | tf_op jit(solution)/shard_map/reduce_scatter | solution.py:318
  654.4 379.0 %reduce-scatter.9.cloned.1.call-start = ((), (), s32[]{:S(2)}) async-start(), calls=%async_computation.15 | async-start | bytes 4325376 | tf_op jit(solution)/shard_map/reduce_scatter | solution.py:315
  657.5 534.1 %reduce-scatter.7.cloned.1.call-start = ((), (), s32[]{:S(2)}) async-start(), calls=%async_computation.14 | async-start | bytes 12976128 | tf_op jit(solution)/shard_map/reduce_scatter | solution.py:314
  665.3 711.2 %reduce-scatter.11.cloned.1.call-start = ((), (), s32[]{:S(2)}) async-start(), calls=%async_computation.16 | async-start | bytes 17301504 | tf_op jit(solution)/shard_map/reduce_scatter | solution.py:316
  674.7 889.2 %reduce-scatter.13.cloned.1.call-start = ((), (), s32[]{:S(2)}) async-start(), calls=%async_computation.17 | async-start | bytes 17301504 | tf_op jit(solution)/shard_map/reduce_scatter | solution.py:317
  686.4 5.5 copy-start.40
  686.4 877.4 %copy-start.1 = (f32[64,256]{1,0:T(8,128)S(1)}, f32[64,256]{1,0:T(8,128)}, u32[]{:S(2)}) copy-start(f32[64,256]{1,0:T(8,128)} %param.18) | copy-start | bytes 196612
  (33 other events, 98.2 us)
Sparse Core Ops, SparseCore 0:
  10.9 73.0 all-gather.8
  132.1 26.0 all-gather.16
  160.7 27.8 all-gather.18
  191.3 57.4 all-gather.10
  251.5 76.6 all-gather.12
  330.9 76.0 all-gather.14
  624.5 135.3 reduce-scatter.16
  762.8 130.8 reduce-scatter.14
  896.6 136.6 reduce-scatter.8
  1039.8 151.6 reduce-scatter.6
  1194.5 181.9 reduce-scatter.10
  1379.3 184.4 reduce-scatter.12
where the time goes:
time: 1580 us; the launch traced here: 1570 us
  waiting for transfers between devices  1140 us (72%)
  matrix products  141 us (9%)
  blocking collectives  112 us (7%)
  local copies, waits for them, and re-layouts  72.9 us (5%)
  other arithmetic  58.9 us (4%)
  starting transfers between devices  34.5 us (2%)
    reduce_scatter x1, waiting for transfers between devices, local(): lax.psum_scatter(grad_w_down, ('head', 'blk'), scatter_dimension=0, tiled...  187 us
    reduce_scatter x1, waiting for transfers between devices, local(): lax.psum_scatter(grad_w_up, ('head', 'blk'), scatter_dimension=0, tiled=T...  185 us
    reduce_scatter x1, waiting for transfers between devices, local(): lax.psum_scatter(grad_w_qkv, ('head', 'blk'), scatter_dimension=0, tiled=...  158 us
    reduce_scatter x1, waiting for transfers between devices, local(): lax.psum_scatter(grad_w_out, ('head', 'blk'), scatter_dimension=0, tiled=...  140 us
    reduce_scatter x1, waiting for transfers between devices, local(): lax.psum_scatter(grad_scale_attn, ('head', 'blk'), scatter_dimension=0, t...  134 us
    all_gather x1, waiting for transfers between devices, local(): lax.all_gather(w_down, ('head', 'blk'), axis=0, tiled=True)  74 us
    reduce_scatter x1, waiting for transfers between devices, local(): lax.psum_scatter(grad_scale_mlp, ('head', 'blk'), scatter_dimension=0, ti...  66.8 us
    all_gather x1, waiting for transfers between devices, local(): lax.all_gather(w_up, ('head', 'blk'), axis=0, tiled=True)  64.3 us
  transfers between devices with their start and end apart: 47, of which 29 were waited for; matrix products, arithmetic and copies ran while one was open for 13% of the time, Pallas kernels for 0%

commit v1 on v0

--- a/solution.py
+++ b/solution.py
@@ -103,7 +103,7 @@
     return (grad_query, grad_keys, grad_values)
 
 
-def local(
+def general(
     tokens,
     positions,
     time_index,
@@ -321,7 +321,258 @@
     return (output, grad_tokens, shards[0], shards[1], shards[2], shards[3], shards[4], shards[5])
 
 
+EPS = NORM_EPSILON
+BF = jnp.bfloat16
+F32 = jnp.float32
+
+
+def norm_stats(value):
+    centered = value - jnp.mean(value, axis=-1, keepdims=True)
+    spread = lax.rsqrt(jnp.mean(centered * centered, axis=-1, keepdims=True) + EPS)
+    return centered * spread, spread
+
+
+def norm_back(unit, spread, grad, scale):
+    scaled = grad * scale
+    return spread * (
+        scaled
+        - jnp.mean(scaled, axis=-1, keepdims=True)
+        - unit * jnp.mean(scaled * unit, axis=-1, keepdims=True)
+    )
+
+
+def pack_half(value):
+    lead, width = value.shape[:-2], value.shape[-1]
+    rows = value.shape[-2]
+    axis = value.ndim - 2
+    return jnp.concatenate(
+        [
+            lax.slice_in_dim(value, 0, rows // 2, axis=axis),
+            lax.slice_in_dim(value, rows // 2, rows, axis=axis),
+        ],
+        axis=-1,
+    )
+
+
+def unpack_half(value):
+    width = value.shape[-1] // 2
+    return jnp.concatenate([value[..., :width], value[..., width:]], axis=-2)
+
+
+def turn(value, table, sign):
+    cosine = table[..., :32]
+    sine = table[..., 32:64] * sign
+    first, second = value[..., :32], value[..., 32:]
+    return jnp.concatenate(
+        [first * cosine - second * sine, second * cosine + first * sine], axis=-1
+    )
+
+
+def phase_one(tokens, table, wq_parts, scale_parts):
+    token_all = lax.all_gather(tokens, "head", axis=0)
+    table_all = lax.all_gather(table, "head", axis=0)
+    scales = lax.psum(scale_parts, ("head", "blk"))
+    wq = lax.all_to_all(wq_parts, "head", 0, 0, tiled=True)
+    wq = jnp.swapaxes(lax.all_gather(wq, "blk", axis=0), 0, 1).reshape(1024, 768)
+    unit, _ = norm_stats(token_all.astype(F32))
+    scale_one = 1.0 + scales[:2]
+    normed = (unit * scale_one[None, :, None, :]).astype(BF).reshape(512, 1024)
+    proj = jnp.dot(normed, wq, preferred_element_type=F32).reshape(4, 2, 64, 768)
+    tab = table_all.reshape(4, 2, 64, 1, 64)
+    pairs = proj[..., :512].reshape(4, 2, 64, 4, 128)
+    keys = turn(pairs[..., :64], tab, 1.0)
+    query = turn(proj[..., 512:].reshape(4, 2, 64, 4, 64), tab, 1.0)
+    kv = jnp.concatenate([keys, pairs[..., 64:]], axis=-1).astype(BF)
+    kv = jnp.transpose(kv, (1, 3, 0, 2, 4))
+    query = pack_half(jnp.transpose(query.astype(BF), (1, 3, 0, 2, 4)))
+    tiles = jnp.concatenate([kv, query], axis=-2).reshape(8, 4, 96, 128)
+    tiles = jnp.swapaxes(lax.all_to_all(tiles, "blk", 0, 0, tiled=True), 0, 1)
+    return tiles, normed, wq, scales, table_all.reshape(512, 64)
+
+
+def split_tiles(tiles):
+    kv = tiles[:, :, :64].reshape(2048, 128)
+    query = unpack_half(tiles[:, :, 64:]).reshape(2048, 64)
+    return query, kv[:, :64], kv[:, 64:]
+
+
+def to_all(tiles):
+    return lax.all_to_all(
+        tiles.reshape(32, 32, 128), ("head", "blk"), 0, 0, tiled=True
+    ).reshape(4, 8, 32, 128)
+
+
+def phase_two(tiles, up_parts, w_down, w_out, cotangent):
+    query, keys, values = split_tiles(tiles)
+    scores = SCORE_SCALE * contract_cols(keys, query)
+    top = jnp.max(scores, axis=0, keepdims=True)
+    weights = jnp.exp(scores - top)
+    row_sum = jnp.sum(weights, axis=0, keepdims=True)
+    mixed = contract_rows(values, weights.astype(BF)) / row_sum
+    lse = top + jnp.log(row_sum)
+    attended = pack_half(jnp.transpose(mixed).astype(BF).reshape(4, 8, 64, 64))
+    received = to_all(attended)
+    up = lax.all_to_all(up_parts, "head", 0, 0, tiled=True)
+    up = jnp.swapaxes(lax.all_gather(up, "blk", axis=0), 0, 1).reshape(1024, 1024)
+    down = lax.all_gather(w_down, "blk", axis=0, tiled=True)
+    out = lax.all_gather(w_out, ("head", "blk"), axis=0, tiled=True)
+    cot_all = lax.all_gather(cotangent, "head", axis=0).reshape(512, 1024)
+    return mixed, lse, received, up, down, out, cot_all
+
+
+def scatter_head(partial):
+    parts = lax.all_to_all(
+        partial.astype(BF).reshape(4, 128, 1024), "head", 0, 0, tiled=True
+    )
+    return jnp.sum(parts.astype(F32), axis=0)
+
+
+def phase_three(received, tokens, out, up, down, cot_all, cotangent, scales):
+    attended = unpack_half(received).reshape(4, 2, 4, 64, 64)
+    attended = jnp.transpose(attended, (1, 3, 0, 2, 4)).reshape(128, 1024)
+    middle = tokens.reshape(128, 1024).astype(F32) + jnp.dot(
+        attended, out, preferred_element_type=F32
+    )
+    unit, spread = norm_stats(middle)
+    scale_two = jnp.repeat(1.0 + scales[2:4], 64, axis=0)
+    normed_two = (unit * scale_two).astype(BF)
+    normed_all = lax.all_gather(normed_two, "head", axis=0, tiled=True)
+    hidden = jnp.dot(normed_all, up, preferred_element_type=F32)
+    cdf = 0.5 * (1.0 + lax.erf(hidden * math.sqrt(0.5)))
+    active = (hidden * cdf).astype(BF)
+    out_partial = jnp.dot(active, down, preferred_element_type=F32).astype(BF)
+    grad_active = contract_cols(cot_all, down)
+    slope = cdf + hidden * jnp.exp(-0.5 * hidden * hidden) * (1.0 / math.sqrt(2 * math.pi))
+    grad_hidden = (grad_active * slope).astype(BF)
+    grad_down = contract_rows(active, cot_all).astype(BF)
+    grad_up = contract_rows(normed_all, grad_hidden).astype(BF)
+    grad_normed = scatter_head(contract_cols(grad_hidden, up))
+    grad_middle = cotangent.reshape(128, 1024).astype(F32) + norm_back(
+        unit, spread, grad_normed, scale_two
+    )
+    sums = jnp.sum((grad_normed * unit).reshape(2, 64, 1024), axis=1)
+    branch = grad_middle.astype(BF)
+    grad_out = contract_rows(attended, branch).astype(BF)
+    grad_att = contract_cols(branch, out).astype(BF).reshape(2, 64, 4, 4, 64)
+    grad_att = pack_half(jnp.transpose(grad_att, (2, 0, 3, 1, 4)))
+    grad_rx = to_all(grad_att)
+    return grad_rx, grad_middle, middle, out_partial, grad_down, grad_up, grad_out, sums
+
+
+def sum_parts(parts):
+    return jnp.sum(parts.astype(F32), axis=0)
+
+
+def phase_four(tiles, grad_rx, mixed, lse, out_partial, middle, grad_down, grad_up, grad_out):
+    query, keys, values = split_tiles(tiles)
+    grad = unpack_half(grad_rx).reshape(2048, 64)
+    delta = jnp.sum(jnp.transpose(grad).astype(F32) * mixed, axis=0, keepdims=True)
+    probs = jnp.exp(SCORE_SCALE * contract_cols(keys, query) - lse)
+    grad_values = jnp.dot(probs.astype(BF), grad, preferred_element_type=F32)
+    grad_scores = (probs * (contract_cols(values, grad) - delta)).astype(BF)
+    grad_keys = SCORE_SCALE * jnp.dot(grad_scores, query, preferred_element_type=F32)
+    grad_query = SCORE_SCALE * contract_rows(grad_scores, keys)
+    kv = jnp.concatenate([grad_keys, grad_values], axis=-1).astype(BF).reshape(4, 8, 64, 128)
+    packed = pack_half(grad_query.astype(BF).reshape(4, 8, 64, 64))
+    back = jnp.swapaxes(jnp.concatenate([kv, packed], axis=-2), 0, 1)
+    back = lax.all_to_all(back, "blk", 0, 0, tiled=True)
+    output = (middle + scatter_head(out_partial)).astype(BF).reshape(2, 64, 1024)
+    down = sum_parts(lax.all_to_all(grad_down.reshape(8, 128, 1024), "blk", 0, 0, tiled=True))
+    up = jnp.swapaxes(grad_up.reshape(4, 8, 32, 1024), 0, 1)
+    up = sum_parts(lax.all_to_all(up, "blk", 0, 0, tiled=True))
+    up = lax.all_to_all(up.astype(BF), "head", 0, 0, tiled=True).astype(F32)
+    up = jnp.swapaxes(up, 0, 1).reshape(32, 4096)
+    out = jnp.swapaxes(grad_out.reshape(4, 8, 32, 1024), 0, 1)
+    out = sum_parts(lax.all_to_all(out, "blk", 0, 0, tiled=True))
+    out = sum_parts(lax.all_to_all(out.astype(BF), "head", 0, 0, tiled=True))
+    return back, output, down, up, out
+
+
+def phase_five(back, table_all, normed, wq, tokens, scales, grad_middle, sums):
+    kv = back[:, :, :64].reshape(2, 4, 4, 64, 128)
+    query = unpack_half(back[:, :, 64:]).reshape(2, 4, 4, 64, 64)
+    kv = jnp.transpose(kv, (2, 0, 3, 1, 4)).astype(F32)
+    query = jnp.transpose(query, (2, 0, 3, 1, 4)).astype(F32)
+    tab = table_all.reshape(4, 2, 64, 1, 64)
+    keys = turn(kv[..., :64], tab, -1.0)
+    query = turn(query, tab, -1.0)
+    kv = jnp.concatenate([keys, kv[..., 64:]], axis=-1).reshape(512, 512)
+    grad_proj = jnp.concatenate([kv, query.reshape(512, 256)], axis=-1).astype(BF)
+    grad_wq = contract_rows(normed, grad_proj).astype(BF)
+    grad_normed = scatter_head(contract_cols(grad_proj, wq))
+    unit, spread = norm_stats(tokens.reshape(128, 1024).astype(F32))
+    scale_one = jnp.repeat(1.0 + scales[:2], 64, axis=0)
+    grad_tokens = grad_middle + norm_back(unit, spread, grad_normed, scale_one)
+    first = jnp.sum((grad_normed * unit).reshape(2, 64, 1024), axis=1)
+    total = lax.psum(jnp.concatenate([first, sums], axis=0), ("head", "blk"))
+    grad_wq = jnp.swapaxes(grad_wq.reshape(4, 8, 32, 768), 0, 1)
+    grad_wq = sum_parts(lax.all_to_all(grad_wq, "blk", 0, 0, tiled=True))
+    grad_wq = lax.all_to_all(grad_wq.astype(BF), "head", 0, 0, tiled=True).astype(F32)
+    return grad_tokens.reshape(2, 64, 1024), grad_wq, total
+
+
+def blocked(
+    tokens,
+    positions,
+    time_index,
+    time_table,
+    w_qkv,
+    w_out,
+    w_up,
+    w_down,
+    scale_attn,
+    scale_mlp,
+    cotangent,
+):
+    place = lax.axis_index(("head", "blk"))
+    embed = time_table[time_index]
+    embed_own = lax.dynamic_slice_in_dim(embed, place * 8, 8, 1)
+    scale_parts = jnp.concatenate(
+        [
+            jnp.dot(embed_own, scale_attn.astype(F32), precision=PRECISE),
+            jnp.dot(embed_own, scale_mlp.astype(F32), precision=PRECISE),
+        ],
+        axis=0,
+    )
+    cosine, sine = rotary_tables(positions, HEAD_DIM)
+    table = jnp.concatenate([cosine[:, :, 0], sine[:, :, 0]], axis=-1).reshape(128, 64)
+    wide = w_qkv.reshape(32, 3, 4, 4, 64)
+    kv_cols = jnp.stack([wide[:, 1], wide[:, 2]], axis=3).reshape(32, 4, 512)
+    wq_parts = jnp.concatenate([kv_cols, wide[:, 0].reshape(32, 4, 256)], axis=-1)
+    wq_parts = jnp.swapaxes(wq_parts, 0, 1)
+    up_parts = jnp.swapaxes(w_up.reshape(32, 4, 1024), 0, 1)
+    tiles, normed, wq, scales, table_all = phase_one(tokens, table, wq_parts, scale_parts)
+    mixed, lse, received, up, down, out, cot_all = phase_two(
+        tiles, up_parts, w_down, w_out, cotangent
+    )
+    grad_rx, grad_middle, middle, out_partial, grad_down, grad_up, grad_out, sums = phase_three(
+        received, tokens, out, up, down, cot_all, cotangent, scales
+    )
+    back, output, down_own, up_own, out_own = phase_four(
+        tiles, grad_rx, mixed, lse, out_partial, middle, grad_down, grad_up, grad_out
+    )
+    grad_tokens, grad_wq, total = phase_five(
+        back, table_all, normed, wq, tokens, scales, grad_middle, sums
+    )
+    kv_cols = grad_wq[:, :, :512].reshape(4, 32, 4, 2, 64)
+    wide = jnp.stack(
+        [grad_wq[:, :, 512:].reshape(4, 32, 4, 64), kv_cols[:, :, :, 0], kv_cols[:, :, :, 1]],
+        axis=0,
+    )
+    qkv_own = jnp.transpose(wide, (2, 0, 1, 3, 4)).reshape(32, 3072)
+    grad_attn = contract_rows_precise(embed_own, total[:2])
+    grad_mlp = contract_rows_precise(embed_own, total[2:])
+    return output, grad_tokens, qkv_own, out_own, up_own, down_own, grad_attn, grad_mlp
+
+
+def contract_rows_precise(left, right):
+    return lax.dot_general(
+        left, right, (((0,), (0,)), ((), ())), precision=PRECISE, preferred_element_type=F32
+    )
+
+
 def solution(mesh):
+    fits = mesh.shape["head"] == 4 and mesh.shape["blk"] == 8
     placed = (
         P(None, ("head", "blk"), None),
         P(None, ("head", "blk")),
@@ -336,7 +587,7 @@
         P(None, ("head", "blk"), None),
     )
     return jax.shard_map(
-        local,
+        blocked if fits else general,
         mesh=mesh,
         in_specs=placed,
         out_specs=(

time: 1580 us -> 605 us (0.38)
  waiting for transfers between devices: 1140 us -> 205 us
  matrix products: 141 us -> 78.8 us
  starting transfers between devices: 34.5 us -> 60.2 us
  local copies, waits for them, and re-layouts: 72.9 us -> 52 us
  blocking collectives: 112 us -> 128 us
    reduce_scatter x6 -> x0, waiting for transfers between devices: 871 us -> none  [the longest x1 187 us: local(): lax.psum_scatter(grad_w_down, ('head', 'blk'), scatter_dimension=0, tiled...]
    all_gather x6 -> x7, waiting for transfers between devices: 217 us -> 78.6 us  [the longest x1 29.3 us: phase_two(): down = lax.all_gather(w_down, 'blk', axis=0, tiled=True)]
    all_to_all x3 -> x14, waiting for transfers between devices: 25.6 us -> 124 us  [the longest x3 61.9 us: scatter_head(): lax.all_to_all(partial.astype(BF).reshape(4, 128, 1024), 'head', 0, 0, ti...]
    psum x0 -> x2, blocking collectives: none -> 81.5 us  [the longest x1 41.9 us: phase_five(): total = lax.psum(jnp.concatenate([first, sums], axis=0), ('head', 'blk'))]
    dot_general x65 -> x10, matrix products: 94.9 us -> 26 us  [the longest x1 6.74 us: phase_four(): jnp.dot(grad_scores, query, preferred_element_type=F32)]
    all_gather x2 -> x1, blocking collectives: 88.5 us -> 19.7 us  [phase_one(): table_all = lax.all_gather(table, 'head', axis=0)]
    all_to_all x3 -> x14, starting transfers between devices: 11.7 us -> 59.5 us  [the longest x3 13.2 us: scatter_head(): lax.all_to_all(partial.astype(BF).reshape(4, 128, 1024), 'head', 0, 0, ti...]
    convert_element_type x39 -> x7, other arithmetic: 41.8 us -> 13.3 us  [the longest x1 10.1 us: phase_four(): grad_values = jnp.dot(probs.astype(BF), grad, preferred_element_type=F32)]
  transfers between devices with their start and end apart: 47 -> 21, of which waited for: 29 -> 12; matrix products, arithmetic and copies ran while one was open for 13% -> 28% of each run, Pallas kernels for 0% -> 0%
where the time goes in v1:
time: 605 us; the launch traced here: 596 us
  waiting for transfers between devices  205 us (34%)
  blocking collectives  128 us (21%)
  matrix products  78.8 us (13%)
  starting transfers between devices  60.2 us (10%)
  other arithmetic  55.7 us (9%)
  local copies, waits for them, and re-layouts  52 us (9%)
  between operations  15.5 us (3%)
    all_to_all x3, waiting for transfers between devices, scatter_head(): lax.all_to_all(partial.astype(BF).reshape(4, 128, 1024), 'head', 0, 0, ti...  61.9 us
    psum x1, blocking collectives, phase_five(): total = lax.psum(jnp.concatenate([first, sums], axis=0), ('head', 'blk'))  41.9 us
    psum x1, blocking collectives, phase_one(): scales = lax.psum(scale_parts, ('head', 'blk'))  39.7 us
    dot_general x6, matrix products, contract_cols(): lax.dot_general(left, right, (((1,), (1,)), ((), ())), preferred_element_...  29.7 us
    all_gather x1, waiting for transfers between devices, phase_two(): down = lax.all_gather(w_down, 'blk', axis=0, tiled=True)  29.3 us
    all_gather x1, waiting for transfers between devices, phase_two(): cot_all = lax.all_gather(cotangent, 'head', axis=0).reshape(512, 1024)  24.7 us
    all_gather x1, waiting for transfers between devices, phase_three(): normed_all = lax.all_gather(normed_two, 'head', axis=0, tiled=True)  24.6 us
    dot_general x6, matrix products, contract_rows(): lax.dot_general(left, right, (((0,), (0,)), ((), ())), preferred_element_...  23.1 us
  transfers between devices with their start and end apart: 21, of which 12 were waited for; matrix products, arithmetic and copies ran while one was open for 28% of the time, Pallas kernels for 0%

profile of v1, /device:TPU:0, one launch (start us, length us, event | category | flops | bytes accessed | tf_op | source)
XLA Modules:
  0.0 595.7 jit_solution(6691159579818586380)
XLA Ops:
  10.2 13.8 %all_to_all.80 = bf16[4,32,768]{2,1,0:T(8,128)(2,1)} all-to-all(bf16[4,32,768]{2,1,0:T(8,128)(2,1)S(1)} %maximum_bitcast_fusion.4), channel_id=1, replica_groups=mesh['head'=4,'blk'=8] {'head'}, dimensions={0} | all-to-all | bytes 393216 | tf_op jit(solution)/shard_map/all_to_all | solution.py:375
  25.0 4.9 all-to-all-start.3
  32.0 19.7 %all_gather.40 = f32[4,128,64]{1,2,0:T(8,128)S(1)} all-gather(f32[1,128,64]{1,2,0:T(8,128)S(1)} %pad_maximum_fusion.9), channel_id=1, replica_groups=mesh['head'=4,'blk'=8] {'head'}, dimensions={0}, use_global_device_ids=true | all-gather | bytes 163840 | tf_op jit(solution)/shard_map/all_gather | solution.py:373
  53.0 39.7 %psum.14 = f32[4,1024]{1,0:T(4,128)S(1)} all-reduce(f32[4,1024]{1,0:T(4,128)S(1)} %pad_maximum_fusion.10), channel_id=1, replica_groups=mesh['head'=4,'blk'=8] {'head','blk'}, use_global_device_ids=true, to_apply=%region_2.0 | all-reduce | flops 4096 | bytes 32768 | tf_op jit(solution)/shard_map/psum | solution.py:374
  96.0 1.9 copy.179
  104.7 3.6 all-to-all-start.1
  109.0 11.8 %all-to-all-done.1 = bf16[8,4,96,128]{3,2,1,0:T(8,128)(2,1)S(1)} async-done(((bf16[8,4,96,128]{3,2,1,0:T(8,128)(2,1)}), bf16[8,4,96,128]{3,2,1,0:T(8,128)(2,1)S(1)}, u32[]{:S(2)}, u32[]{:S(2)}) %all-to-all-start.1) | async-done | bytes 786464 | tf_op jit(solution)/shard_map/all_to_all | solution.py:389
  122.5 8.1 %multiply_reduce_fusion = (f32[2048]{0:T(1024)S(1)}, f32[2048,2048]{1,0:T(8,128)}) fusion(bf16[2048,64]{0,1:T(8,128)(2,1)S(1)} %reshape.411, bf16[2048,128]{1,0:T(8,128)(2,1)S(1)} %bitcast.188), kind=kOutput, calls=%fused_computation.7 | convolution fusion | flops 545257472 | bytes 17571840 | tf_op jit(solution)/shard_map/dot_general | solution.py:57
  130.6 8.7 %fusion = f32[2048]{0:T(1024)S(1)} fusion(f32[2048,2048]{1,0:T(8,128)} %get-tuple-element.59, f32[2048]{0:T(1024)S(1)} %get-tuple-element.58), kind=kLoop, calls=%fused_computation.4 | loop fusion | flops 12580864 | bytes 16793600 | tf_op jit(solution)/shard_map/reduce_sum | solution.py:410
  139.8 7.7 %fusion.7 = f32[64,2048]{1,0:T(8,128)S(1)} fusion(f32[2048,2048]{1,0:T(8,128)} %get-tuple-element.59, f32[2048]{0:T(1024)S(1)} %get-tuple-element.58, bf16[2048,128]{1,0:T(8,128)(2,1)S(1)} %bitcast.189, f32[2048]{0:T(1024)S(1)} %fusion), kind=kOutput, calls=%fused_computation.15 | convolution fusion | flops 549584896 | bytes 17842176 | tf_op jit(solution)/shard_map/dot_general | solution.py:51
  148.9 13.2 %all_to_all.81 = bf16[32,32,128]{2,1,0:T(8,128)(2,1)S(1)} all-to-all(bf16[32,32,128]{2,1,0:T(8,128)(2,1)S(1)} %bitcast.222), channel_id=1, replica_groups=mesh['head'=4,'blk'=8] {'head','blk'}, dimensions={0} | all-to-all | bytes 524288 | tf_op jit(solution)/shard_map/all_to_all | solution.py:400
  163.3 2.2 fusion.53
  168.0 1.8 copy.193
  169.8 24.6 %all-gather.14.cloned.1.call-done = bf16[512,1024]{1,0:T(8,128)(2,1)} async-done(((bf16[128,1024]{1,0:T(8,128)(2,1)}), bf16[512,1024]{1,0:T(8,128)(2,1)}) %all-gather.14.cloned.1.call-update) | async-done | bytes 1048592 | tf_op jit(solution)/shard_map/all_gather | solution.py:439
  194.4 4.2 multiply_convert_fusion.1
  198.6 24.7 %all-gather.24.cloned.1.call-done = bf16[8,64,1024]{2,1,0:T(8,128)(2,1)} async-done(((bf16[2,64,1024]{2,1,0:T(8,128)(2,1)}), bf16[8,64,1024]{2,1,0:T(8,128)(2,1)}) %all-gather.24.cloned.1.call-update) | async-done | bytes 1048592 | tf_op jit(solution)/shard_map/all_gather | solution.py:419
  223.2 29.3 %all-gather.16.cloned.1.call-done = bf16[1024,1024]{1,0:T(8,128)(2,1)} async-done(((bf16[128,1024]{1,0:T(8,128)(2,1)}), bf16[1024,1024]{1,0:T(8,128)(2,1)}) %all-gather.16.cloned.1.call-update) | async-done | bytes 2097168 | tf_op jit(solution)/shard_map/all_gather | solution.py:417
  252.5 4.3 fusion.15
  256.9 2.3 convolution_convert_fusion.5
  259.2 4.7 all-to-all-start.5
  263.9 3.8 convolution_convert_fusion.6
  267.7 22.3 %all-to-all-done.5 = bf16[4,128,1024]{2,1,0:T(8,128)(2,1)S(1)} async-done(((bf16[4,128,1024]{2,1,0:T(8,128)(2,1)}), bf16[4,128,1024]{2,1,0:T(8,128)(2,1)S(1)}, u32[]{:S(2)}, u32[]{:S(2)}) %all-to-all-start.5) | async-done | bytes 1048608 | tf_op jit(solution)/shard_map/all_to_all | solution.py:424
  290.0 4.3 all-to-all-start.4
  296.4 23.2 %all-to-all-done.4 = bf16[4,128,1024]{2,1,0:T(8,128)(2,1)} async-done(((bf16[4,128,1024]{2,1,0:T(8,128)(2,1)}), bf16[4,128,1024]{2,1,0:T(8,128)(2,1)}, u32[]{:S(2)}, u32[]{:S(2)}) %all-to-all-start.4) | async-done | bytes 1048608 | tf_op jit(solution)/shard_map/all_to_all | solution.py:424
  321.1 2.0 convert_add_fusion
  327.9 2.7 all-to-all-start.6
  330.6 10.1 %fusion.2 = bf16[2048,2048]{1,0:T(8,128)(2,1)} fusion(f32[2048,2048]{1,0:T(8,128)} %get-tuple-element.59, f32[2048]{0:T(1024)S(1)} %copy-done.27), kind=kLoop, calls=%fused_computation.6 | loop fusion | flops 12582912 | bytes 25174016 | tf_op jit(solution)/shard_map/convert_element_type | solution.py:471
  340.8 2.6 convolution_convert_fusion
  344.1 4.4 all-to-all-start.15
  348.5 2.8 convolution_convert_fusion.1
  353.7 2.5 copy.220
  356.2 2.5 copy.221
  358.7 2.3 pad_maximum_fusion.2
  360.9 2.2 reshape.427
  363.1 2.2 reshape.469
  366.5 9.9 %multiply_convert_fusion = bf16[2048,2048]{1,0:T(8,128)(2,1)} fusion(f32[2048,2048]{1,0:T(8,128)} %get-tuple-element.59, bf16[2048,64]{0,1:T(8,128)(2,1)} %reshape.427, f32[2048]{0:T(1024)S(1)} %fusion.17, f32[2048]{0:T(1024)S(1)} %copy-done.27, bf16[2048,128]{1,0:T(8,128)(2,1)S(1)} %bitcast.190), kind=kOutput, calls=%fused_computation.1 | convolution fusion | flops 557842432 | bytes 25968640 | tf_op jit(solution)/shard_map/dot_general | solution.py:57
  376.4 4.5 all-to-all-start.13
  381.0 6.7 %fusion.5 = bf16[2048,64]{0,1:T(8,128)(2,1)} fusion(bf16[2048,2048]{1,0:T(8,128)(2,1)} %multiply_convert_fusion, bf16[2048,64]{0,1:T(8,128)(2,1)} %copy-done.11), kind=kOutput, calls=%fused_computation.13 | convolution fusion | flops 537133056 | bytes 8912896 | tf_op jit(solution)/shard_map/dot_general | solution.py:473
  387.7 2.0 copy.214
  389.7 5.7 fusion.6
  396.7 5.8 convolution_convert_fusion.7
  403.9 3.7 all-to-all-done.13
  407.6 4.2 all-to-all-start.7
  411.8 1.7 convolution_convert_fusion.2
  415.1 9.4 %all-to-all-done.7 = bf16[8,4,96,128]{3,2,1,0:T(8,128)(2,1)} async-done(((bf16[8,4,96,128]{3,2,1,0:T(8,128)(2,1)}), bf16[8,4,96,128]{3,2,1,0:T(8,128)(2,1)}, u32[]{:S(2)}, u32[]{:S(2)}) %all-to-all-start.7) | async-done | bytes 786464 | tf_op jit(solution)/shard_map/all_to_all | solution.py:478
  424.4 4.4 all-to-all-start.11
  429.7 2.7 reduce_sum.228
  436.1 2.2 subtract_convert_fusion
  438.3 17.2 %all-to-all-done.11 = bf16[8,4,32,1024]{3,2,1,0:T(8,128)(2,1)} async-done(((bf16[8,4,32,1024]{3,2,1,0:T(8,128)(2,1)}), bf16[8,4,32,1024]{3,2,1,0:T(8,128)(2,1)}, u32[]{:S(2)}, u32[]{:S(2)}) %all-to-all-start.11) | async-done | bytes 2097184 | tf_op jit(solution)/shard_map/all_to_all | solution.py:486
  455.5 4.9 all-to-all-start.14
  460.3 1.9 pad_maximum_fusion.3
  466.5 2.0 bitcast_dynamic-update-slice_fusion
  468.5 2.7 reduce_sum.226
  471.2 5.1 all-to-all-start.12
  477.0 2.5 convolution_convert_fusion.3
  480.8 2.3 all-to-all-done.12
  483.1 4.3 all-to-all-start.9
  487.4 3.6 convolution_convert_fusion.4
  491.0 17.4 %all-to-all-done.9 = bf16[8,4,32,768]{3,2,1,0:T(8,128)(2,1)} async-done(((bf16[8,4,32,768]{3,2,1,0:T(8,128)(2,1)}), bf16[8,4,32,768]{3,2,1,0:T(8,128)(2,1)}, u32[]{:S(2)}, u32[]{:S(2)}) %all-to-all-start.9) | async-done | bytes 1572896 | tf_op jit(solution)/shard_map/all_to_all | solution.py:509
  508.4 4.2 all-to-all-start.8
  517.0 2.4 reduce_sum.225
  519.4 16.4 %all-to-all-done.8 = bf16[4,128,1024]{2,1,0:T(8,128)(2,1)} async-done(((bf16[4,128,1024]{2,1,0:T(8,128)(2,1)}), bf16[4,128,1024]{2,1,0:T(8,128)(2,1)}, u32[]{:S(2)}, u32[]{:S(2)}) %all-to-all-start.8) | async-done | bytes 1048608 | tf_op jit(solution)/shard_map/all_to_all | solution.py:424
  535.8 3.4 all-to-all-start.10
  541.0 41.9 %psum.15 = f32[4,1024]{1,0:T(4,128)S(1)} all-reduce(f32[4,1024]{1,0:T(4,128)S(1)} %pad_maximum_fusion.11), channel_id=1, replica_groups=mesh['head'=4,'blk'=8] {'head','blk'}, use_global_device_ids=true, to_apply=%region_24.0 | all-reduce | flops 4096 | bytes 32768 | tf_op jit(solution)/shard_map/psum | solution.py:507
  (247 shorter events, 64.2 us)
Async XLA Ops:
  7.2 23.6 %copy-start = (f32[64,256]{1,0:T(8,128)S(1)}, f32[64,256]{1,0:T(8,128)}, u32[]{:S(2)}) copy-start(f32[64,256]{1,0:T(8,128)} %param.14) | copy-start | bytes 196612
  7.2 86.0 %all-gather.18.cloned.1.call-start = ((), (), s32[]{:S(2)}) async-start(), calls=%async_computation.19 | async-start | bytes 1310720 | tf_op jit(solution)/shard_map/all_gather | solution.py:372
  7.9 88.0 %all-gather.20.cloned.1.call-start = ((), (), s32[]{:S(2)}) async-start(), calls=%async_computation.20 | async-start | bytes 1769472 | tf_op jit(solution)/shard_map/all_gather | solution.py:376
  9.2 14.8 %copy-start.26 = (bf16[32,4096]{1,0:T(8,128)(2,1)S(1)}, bf16[32,4096]{1,0:T(8,128)(2,1)}, u32[]{:S(2)}) copy-start(bf16[32,4096]{1,0:T(8,128)(2,1)} %param.17) | copy-start | bytes 786436
  9.4 21.2 %copy-start.45 = (s32[2]{0:T(128)S(1)}, s32[2]{0:T(128)}, u32[]{:S(2)}) copy-start(s32[2]{0:T(128)} %param.13) | copy-start | bytes 28
  9.4 21.2 %copy-start.43 = (s32[2,64]{1,0:T(2,128)S(1)}, s32[2,64]{1,0:T(2,128)}, u32[]{:S(2)}) copy-start(s32[2,64]{1,0:T(2,128)} %param.12) | copy-start | bytes 1540
  9.5 21.9 %copy-start.35 = (bf16[8,1024]{1,0:T(8,128)(2,1)S(1)}, bf16[8,1024]{1,0:T(8,128)(2,1)}, u32[]{:S(2)}) copy-start(bf16[8,1024]{1,0:T(8,128)(2,1)} %param.20) | copy-start | bytes 49156
  9.5 22.1 %copy-start.36 = (bf16[8,1024]{1,0:T(8,128)(2,1)S(1)}, bf16[8,1024]{1,0:T(8,128)(2,1)}, u32[]{:S(2)}) copy-start(bf16[8,1024]{1,0:T(8,128)(2,1)} %param.19) | copy-start | bytes 49156
  25.0 79.7 %all-to-all-start.3 = ((bf16[4,32,1024]{2,1,0:T(8,128)(2,1)}), bf16[4,32,1024]{2,1,0:T(8,128)(2,1)}, u32[]{:S(2)}, u32[]{:S(2)}) async-start(bf16[4,32,1024]{2,1,0:T(8,128)(2,1)} %copy.192), calls=%async_computation.3 | async-start | bytes 524288 | tf_op jit(solution)/shard_map/all_to_all | solution.py:415
  29.9 133.3 %all-gather.12.cloned.1.call-start = ((), (), s32[]{:S(2)}) async-start(), calls=%async_computation.16 | async-start | bytes 2162688 | tf_op jit(solution)/shard_map/all_gather | solution.py:418
  52.1 49.7 %copy-start.15 = (f32[4,2,64,32]{3,2,0,1:T(8,128)}, f32[4,2,64,32]{3,2,0,1:T(8,128)S(1)}, u32[]{:S(2)}) copy-start(f32[4,2,64,32]{3,2,0,1:T(8,128)S(1)} %copy.181) | copy-start | bytes 196612
  93.2 1.6 copy-start.2
  95.9 2.9 copy-start.21
  97.9 1.2 copy-start.20
  101.1 1.0 copy-start.24
  104.7 16.2 %all-to-all-start.1 = ((bf16[8,4,96,128]{3,2,1,0:T(8,128)(2,1)}), bf16[8,4,96,128]{3,2,1,0:T(8,128)(2,1)S(1)}, u32[]{:S(2)}, u32[]{:S(2)}) async-start(bf16[8,4,96,128]{3,2,1,0:T(8,128)(2,1)} %bitcast.15), calls=%async_computation.1 | async-start | bytes 1572864 | tf_op jit(solution)/shard_map/all_to_all | solution.py:389
  108.2 59.7 %all-gather.22.cloned.1.call-start = ((), (), s32[]{:S(2)}) async-start(), calls=%async_computation.21 | async-start | bytes 2359296 | tf_op jit(solution)/shard_map/all_gather | solution.py:416
  108.8 85.5 %all-gather.14.cloned.1.call-start = ((), (), s32[]{:S(2)}) async-start(), calls=%async_computation.17 | async-start | bytes 1310720 | tf_op jit(solution)/shard_map/all_gather | solution.py:439
  122.4 8.1 %copy-start.11 = (bf16[2048,64]{0,1:T(8,128)(2,1)}, bf16[2048,64]{0,1:T(8,128)(2,1)S(1)}, u32[]{:S(2)}) copy-start(bf16[2048,64]{0,1:T(8,128)(2,1)S(1)} %reshape.411) | copy-start | bytes 786436
  162.2 1.1 copy-start.3
  162.9 2.9 copy-start.28
  163.2 3.4 copy-start.14
  165.5 2.5 copy-start.37
  165.7 2.3 copy-start.40
  166.6 56.6 %all-gather.24.cloned.1.call-start = ((), (), s32[]{:S(2)}) async-start(), calls=%async_computation.22 | async-start | bytes 1310720 | tf_op jit(solution)/shard_map/all_gather | solution.py:419
  167.2 85.4 %all-gather.16.cloned.1.call-start = ((), (), s32[]{:S(2)}) async-start(), calls=%async_computation.18 | async-start | bytes 2359296 | tf_op jit(solution)/shard_map/all_gather | solution.py:417
  256.8 2.3 copy-start.48
  259.2 4.7 copy-start.46
  259.2 30.9 %all-to-all-start.5 = ((bf16[4,128,1024]{2,1,0:T(8,128)(2,1)}), bf16[4,128,1024]{2,1,0:T(8,128)(2,1)S(1)}, u32[]{:S(2)}, u32[]{:S(2)}) async-start(bf16[4,128,1024]{2,1,0:T(8,128)(2,1)} %bitcast.225), calls=%async_computation.5 | async-start | bytes 2097152 | tf_op jit(solution)/shard_map/all_to_all | solution.py:424
  267.7 26.6 %copy-start.32 = (f32[2048]{0:T(1024)S(1)}, f32[2048]{0:T(1024)}, u32[]{:S(2)}) copy-start(f32[2048]{0:T(1024)} %copy-done.31) | copy-start | bytes 24580
  267.7 27.4 %copy-start.29 = (f32[2,1024]{1,0:T(2,128)S(1)}, f32[2,1024]{1,0:T(2,128)}, u32[]{:S(2)}) copy-start(f32[2,1024]{1,0:T(2,128)} %get-tuple-element.54) | copy-start | bytes 24580
  267.7 27.4 %copy-start.38 = (f32[128]{0:T(128)S(1)}, f32[128]{0:T(128)}, u32[]{:S(2)}) copy-start(f32[128]{0:T(128)} %copy-done.37) | copy-start | bytes 1540
  267.7 27.4 %copy-start.41 = (f32[128]{0:T(128)S(1)}, f32[128]{0:T(128)}, u32[]{:S(2)}) copy-start(f32[128]{0:T(128)} %copy-done.40) | copy-start | bytes 1540
  290.0 29.6 %all-to-all-start.4 = ((bf16[4,128,1024]{2,1,0:T(8,128)(2,1)}), bf16[4,128,1024]{2,1,0:T(8,128)(2,1)}, u32[]{:S(2)}, u32[]{:S(2)}) async-start(bf16[4,128,1024]{2,1,0:T(8,128)(2,1)} %bitcast.28), calls=%async_computation.4 | async-start | bytes 2097152 | tf_op jit(solution)/shard_map/all_to_all | solution.py:424
  294.9 26.2 %copy-start.30 = (f32[2,1024]{1,0:T(2,128)S(1)}, f32[2,1024]{1,0:T(2,128)}, u32[]{:S(2)}) copy-start(f32[2,1024]{1,0:T(2,128)} %get-tuple-element.54) | copy-start | bytes 24580
  296.4 27.5 %copy-start.4 = (bf16[1024,1024]{1,0:T(8,128)(2,1)S(1)}, bf16[1024,1024]{1,0:T(8,128)(2,1)}, u32[]{:S(2)}) copy-start(bf16[1024,1024]{1,0:T(8,128)(2,1)} %all-gather.12.cloned.1.call-done) | copy-start | bytes 6291460
  325.5 5.2 copy-start.27
  327.9 15.5 %all-to-all-start.6 = ((bf16[32,32,128]{2,1,0:T(8,128)(2,1)}), bf16[32,32,128]{2,1,0:T(8,128)(2,1)S(1)}, u32[]{:S(2)}, u32[]{:S(2)}) async-start(bf16[32,32,128]{2,1,0:T(8,128)(2,1)} %bitcast.34), calls=%async_computation.6 | async-start | bytes 524288 | tf_op jit(solution)/shard_map/all_to_all | solution.py:400
  330.6 10.1 %copy-start.44 = (bf16[8,64,1024]{2,1,0:T(8,128)(2,1)S(1)}, bf16[8,64,1024]{2,1,0:T(8,128)(2,1)}, u32[]{:S(2)}) copy-start(bf16[8,64,1024]{2,1,0:T(8,128)(2,1)} %all-gather.24.cloned.1.call-done) | copy-start | bytes 3145732
  330.6 10.1 %copy-start.47 = (bf16[512,1024]{1,0:T(8,128)(2,1)S(1)}, bf16[512,1024]{1,0:T(8,128)(2,1)}, u32[]{:S(2)}) copy-start(bf16[512,1024]{1,0:T(8,128)(2,1)} %get-tuple-element.62) | copy-start | bytes 3145732
  344.1 32.3 %all-to-all-start.15 = ((bf16[8,128,1024]{2,1,0:T(8,128)(2,1)}), bf16[8,128,1024]{2,1,0:T(8,128)(2,1)S(1)}, u32[]{:S(2)}, u32[]{:S(2)}) async-start(bf16[8,128,1024]{2,1,0:T(8,128)(2,1)} %bitcast.208), calls=%async_computation.15 | async-start | bytes 4194304 | tf_op jit(solution)/shard_map/all_to_all | solution.py:480
  351.3 1.5 copy-start.13
  376.4 31.2 %all-to-all-start.13 = ((bf16[8,4,32,1024]{3,2,1,0:T(8,128)(2,1)}), bf16[8,4,32,1024]{3,2,1,0:T(8,128)(2,1)}, u32[]{:S(2)}, u32[]{:S(2)}) async-start(bf16[8,4,32,1024]{3,2,1,0:T(8,128)(2,1)} %bitcast.195), calls=%async_computation.13 | async-start | bytes 4194304 | tf_op jit(solution)/shard_map/all_to_all | solution.py:482
  396.6 5.8 copy-start.17
  402.9 8.9 %copy-start.8 = (f32[128,1024]{1,0:T(8,128)S(1)}, f32[128,1024]{1,0:T(8,128)}, u32[]{:S(2)}) copy-start(f32[128,1024]{1,0:T(8,128)} %copy-done.7) | copy-start | bytes 1572868
  407.6 16.8 %all-to-all-start.7 = ((bf16[8,4,96,128]{3,2,1,0:T(8,128)(2,1)}), bf16[8,4,96,128]{3,2,1,0:T(8,128)(2,1)}, u32[]{:S(2)}, u32[]{:S(2)}) async-start(bf16[8,4,96,128]{3,2,1,0:T(8,128)(2,1)} %copy.200), calls=%async_computation.7 | async-start | bytes 1572864 | tf_op jit(solution)/shard_map/all_to_all | solution.py:478
  424.4 31.0 %all-to-all-start.11 = ((bf16[8,4,32,1024]{3,2,1,0:T(8,128)(2,1)}), bf16[8,4,32,1024]{3,2,1,0:T(8,128)(2,1)}, u32[]{:S(2)}, u32[]{:S(2)}) async-start(bf16[8,4,32,1024]{3,2,1,0:T(8,128)(2,1)} %bitcast.196), calls=%async_computation.11 | async-start | bytes 4194304 | tf_op jit(solution)/shard_map/all_to_all | solution.py:486
  434.6 1.5 copy-start.16
  434.6 1.5 copy-start.25
  455.5 15.7 %all-to-all-start.14 = ((bf16[4,32,1024]{2,1,0:T(8,128)(2,1)}), bf16[4,32,1024]{2,1,0:T(8,128)(2,1)}, u32[]{:S(2)}, u32[]{:S(2)}) async-start(bf16[4,32,1024]{2,1,0:T(8,128)(2,1)} %reduce_sum.228), calls=%async_computation.14 | async-start | bytes 524288 | tf_op jit(solution)/shard_map/all_to_all | solution.py:483
  460.3 3.2 copy-start.18
  460.3 3.2 copy-start.19
  471.2 11.9 %all-to-all-start.12 = ((bf16[4,32,1024]{2,1,0:T(8,128)(2,1)}), bf16[4,32,1024]{2,1,0:T(8,128)(2,1)S(1)}, u32[]{:S(2)}, u32[]{:S(2)}) async-start(bf16[4,32,1024]{2,1,0:T(8,128)(2,1)} %reduce_sum.226), calls=%async_computation.12 | async-start | bytes 524288 | tf_op jit(solution)/shard_map/all_to_all | solution.py:487
  483.1 4.3 copy-start.22
  483.1 25.3 %all-to-all-start.9 = ((bf16[8,4,32,768]{3,2,1,0:T(8,128)(2,1)}), bf16[8,4,32,768]{3,2,1,0:T(8,128)(2,1)}, u32[]{:S(2)}, u32[]{:S(2)}) async-start(bf16[8,4,32,768]{3,2,1,0:T(8,128)(2,1)} %bitcast.199), calls=%async_computation.9 | async-start | bytes 3145728 | tf_op jit(solution)/shard_map/all_to_all | solution.py:509
  491.0 22.1 %copy-start.6 = (f32[128,1024]{1,0:T(8,128)S(1)}, f32[128,1024]{1,0:T(8,128)}, u32[]{:S(2)}) copy-start(f32[128,1024]{1,0:T(8,128)} %copy-done.5) | copy-start | bytes 1572868
  491.0 22.2 %copy-start.39 = (f32[128]{0:T(128)S(1)}, f32[128]{0:T(128)}, u32[]{:S(2)}) copy-start(f32[128]{0:T(128)} %copy-done.37) | copy-start | bytes 1540
  491.0 22.2 %copy-start.42 = (f32[128]{0:T(128)S(1)}, f32[128]{0:T(128)}, u32[]{:S(2)}) copy-start(f32[128]{0:T(128)} %copy-done.40) | copy-start | bytes 1540
  508.4 27.3 %all-to-all-start.8 = ((bf16[4,128,1024]{2,1,0:T(8,128)(2,1)}), bf16[4,128,1024]{2,1,0:T(8,128)(2,1)}, u32[]{:S(2)}, u32[]{:S(2)}) async-start(bf16[4,128,1024]{2,1,0:T(8,128)(2,1)} %bitcast.224), calls=%async_computation.8 | async-start | bytes 2097152 | tf_op jit(solution)/shard_map/all_to_all | solution.py:424
  513.4 3.0 copy-start.23
  519.4 63.5 %copy-start.34 = (f32[2,256]{1,0:T(2,128)S(1)}, f32[2,256]{1,0:T(2,128)}, u32[]{:S(2)}) copy-start(f32[2,256]{1,0:T(2,128)} %copy-done.33) | copy-start | bytes 6148
  519.4 64.5 %copy-start.9 = (f32[128,1024]{1,0:T(8,128)S(1)}, f32[128,1024]{1,0:T(8,128)}, u32[]{:S(2)}) copy-start(f32[128,1024]{1,0:T(8,128)} %copy-done.7) | copy-start | bytes 1572868
  535.8 50.1 %all-to-all-start.10 = ((bf16[4,32,768]{2,1,0:T(8,128)(2,1)}), bf16[4,32,768]{2,1,0:T(8,128)(2,1)S(1)}, u32[]{:S(2)}, u32[]{:S(2)}) async-start(bf16[4,32,768]{2,1,0:T(8,128)(2,1)} %reduce_sum.225), calls=%async_computation.10 | async-start | bytes 393216 | tf_op jit(solution)/shard_map/all_to_all | solution.py:510
  586.9 1.7 copy-start.1
  (6 other events, 4.3 us)
Sparse Core Ops, SparseCore 0:
  9.6 38.4 all-gather.17
  50.0 24.7 all-gather.19
  77.7 56.3 all-gather.11
  135.8 29.1 all-gather.21
  167.1 27.2 all-gather.13
  195.8 27.4 all-gather.23
  225.1 27.3 all-gather.15

commit v2 on v1

--- a/solution.py
+++ b/solution.py
@@ -3,6 +3,8 @@
 import jax
 import jax.numpy as jnp
 from jax import lax
+from jax.experimental import pallas as pl
+from jax.experimental.pallas import tpu as pltpu
 from jax.sharding import PartitionSpec as P
 
 HEADS = 16
@@ -412,11 +414,11 @@
     lse = top + jnp.log(row_sum)
     attended = pack_half(jnp.transpose(mixed).astype(BF).reshape(4, 8, 64, 64))
     received = to_all(attended)
-    up = lax.all_to_all(up_parts, "head", 0, 0, tiled=True)
-    up = jnp.swapaxes(lax.all_gather(up, "blk", axis=0), 0, 1).reshape(1024, 1024)
-    down = lax.all_gather(w_down, "blk", axis=0, tiled=True)
-    out = lax.all_gather(w_out, ("head", "blk"), axis=0, tiled=True)
-    cot_all = lax.all_gather(cotangent, "head", axis=0).reshape(512, 1024)
+    up = lax.all_to_all(up_parts, "blk", 0, 0, tiled=True)
+    up = lax.all_gather(up, "head", axis=0)
+    down = lax.all_gather(w_down, "head", axis=0)
+    out = lax.all_gather(w_out, ("head", "blk"), axis=0).reshape(4, 8, 32, 1024)
+    cot_all = lax.all_gather(cotangent, "blk", axis=0).reshape(8, 128, 1024)
     return mixed, lse, received, up, down, out, cot_all
 
 
@@ -427,35 +429,44 @@
     return jnp.sum(parts.astype(F32), axis=0)
 
 
-def phase_three(received, tokens, out, up, down, cot_all, cotangent, scales):
+def scatter_blk(partial):
+    parts = lax.all_to_all(partial, "blk", 0, 0, tiled=True)
+    return jnp.sum(parts.astype(F32), axis=0)
+
+
+def phase_three(received, tokens, out, up, down, cot_all, scales):
+    up = up.reshape(1024, 512)
+    down = down.reshape(512, 1024)
+    out = out.reshape(1024, 1024)
     attended = unpack_half(received).reshape(4, 2, 4, 64, 64)
     attended = jnp.transpose(attended, (1, 3, 0, 2, 4)).reshape(128, 1024)
     middle = tokens.reshape(128, 1024).astype(F32) + jnp.dot(
         attended, out, preferred_element_type=F32
     )
     unit, spread = norm_stats(middle)
-    scale_two = jnp.repeat(1.0 + scales[2:4], 64, axis=0)
+    scale_two = jnp.repeat(scales[2:4], 64, axis=0)
     normed_two = (unit * scale_two).astype(BF)
-    normed_all = lax.all_gather(normed_two, "head", axis=0, tiled=True)
+    normed_all = lax.all_gather(normed_two, "blk", axis=0, tiled=True)
+    cots = cot_all.reshape(1024, 1024)
+    cotangent = cot_all[lax.axis_index("blk")]
     hidden = jnp.dot(normed_all, up, preferred_element_type=F32)
     cdf = 0.5 * (1.0 + lax.erf(hidden * math.sqrt(0.5)))
     active = (hidden * cdf).astype(BF)
     out_partial = jnp.dot(active, down, preferred_element_type=F32).astype(BF)
-    grad_active = contract_cols(cot_all, down)
+    grad_active = contract_cols(cots, down)
     slope = cdf + hidden * jnp.exp(-0.5 * hidden * hidden) * (1.0 / math.sqrt(2 * math.pi))
     grad_hidden = (grad_active * slope).astype(BF)
-    grad_down = contract_rows(active, cot_all).astype(BF)
-    grad_up = contract_rows(normed_all, grad_hidden).astype(BF)
-    grad_normed = scatter_head(contract_cols(grad_hidden, up))
-    grad_middle = cotangent.reshape(128, 1024).astype(F32) + norm_back(
-        unit, spread, grad_normed, scale_two
-    )
+    grad_down = contract_rows(active, cots).astype(BF).reshape(4, 128, 1024)
+    grad_up = contract_rows(normed_all, grad_hidden).astype(BF).reshape(4, 8, 32, 512)
+    grad_normed = scatter_blk(contract_cols(grad_hidden, up).astype(BF).reshape(8, 128, 1024))
+    grad_middle = cotangent.astype(F32) + norm_back(unit, spread, grad_normed, scale_two)
     sums = jnp.sum((grad_normed * unit).reshape(2, 64, 1024), axis=1)
     branch = grad_middle.astype(BF)
-    grad_out = contract_rows(attended, branch).astype(BF)
+    grad_out = contract_rows(attended, branch).astype(BF).reshape(4, 8, 32, 1024)
     grad_att = contract_cols(branch, out).astype(BF).reshape(2, 64, 4, 4, 64)
     grad_att = pack_half(jnp.transpose(grad_att, (2, 0, 3, 1, 4)))
     grad_rx = to_all(grad_att)
+    out_partial = out_partial.reshape(8, 128, 1024)
     return grad_rx, grad_middle, middle, out_partial, grad_down, grad_up, grad_out, sums
 
 
@@ -476,13 +487,11 @@
     packed = pack_half(grad_query.astype(BF).reshape(4, 8, 64, 64))
     back = jnp.swapaxes(jnp.concatenate([kv, packed], axis=-2), 0, 1)
     back = lax.all_to_all(back, "blk", 0, 0, tiled=True)
-    output = (middle + scatter_head(out_partial)).astype(BF).reshape(2, 64, 1024)
-    down = sum_parts(lax.all_to_all(grad_down.reshape(8, 128, 1024), "blk", 0, 0, tiled=True))
-    up = jnp.swapaxes(grad_up.reshape(4, 8, 32, 1024), 0, 1)
-    up = sum_parts(lax.all_to_all(up, "blk", 0, 0, tiled=True))
-    up = lax.all_to_all(up.astype(BF), "head", 0, 0, tiled=True).astype(F32)
-    up = jnp.swapaxes(up, 0, 1).reshape(32, 4096)
-    out = jnp.swapaxes(grad_out.reshape(4, 8, 32, 1024), 0, 1)
+    output = (middle + scatter_blk(out_partial)).astype(BF).reshape(2, 64, 1024)
+    down = sum_parts(lax.all_to_all(grad_down, "head", 0, 0, tiled=True))
+    up = sum_parts(lax.all_to_all(grad_up, "head", 0, 0, tiled=True))
+    up = lax.all_to_all(up.astype(BF), "blk", 0, 0, tiled=True)
+    out = jnp.swapaxes(grad_out, 0, 1)
     out = sum_parts(lax.all_to_all(out, "blk", 0, 0, tiled=True))
     out = sum_parts(lax.all_to_all(out.astype(BF), "head", 0, 0, tiled=True))
     return back, output, down, up, out
@@ -493,15 +502,17 @@
     query = unpack_half(back[:, :, 64:]).reshape(2, 4, 4, 64, 64)
     kv = jnp.transpose(kv, (2, 0, 3, 1, 4)).astype(F32)
     query = jnp.transpose(query, (2, 0, 3, 1, 4)).astype(F32)
-    tab = table_all.reshape(4, 2, 64, 1, 64)
+    tab = jnp.swapaxes(table_all.reshape(4, 64, 2, 64), 1, 2)[:, :, :, None]
     keys = turn(kv[..., :64], tab, -1.0)
     query = turn(query, tab, -1.0)
     kv = jnp.concatenate([keys, kv[..., 64:]], axis=-1).reshape(512, 512)
     grad_proj = jnp.concatenate([kv, query.reshape(512, 256)], axis=-1).astype(BF)
+    normed = normed.reshape(512, 1024)
+    wq = wq.reshape(1024, 768)
     grad_wq = contract_rows(normed, grad_proj).astype(BF)
     grad_normed = scatter_head(contract_cols(grad_proj, wq))
     unit, spread = norm_stats(tokens.reshape(128, 1024).astype(F32))
-    scale_one = jnp.repeat(1.0 + scales[:2], 64, axis=0)
+    scale_one = jnp.repeat(scales[:2], 64, axis=0)
     grad_tokens = grad_middle + norm_back(unit, spread, grad_normed, scale_one)
     first = jnp.sum((grad_normed * unit).reshape(2, 64, 1024), axis=1)
     total = lax.psum(jnp.concatenate([first, sums], axis=0), ("head", "blk"))
@@ -509,6 +520,324 @@
     grad_wq = sum_parts(lax.all_to_all(grad_wq, "blk", 0, 0, tiled=True))
     grad_wq = lax.all_to_all(grad_wq.astype(BF), "head", 0, 0, tiled=True).astype(F32)
     return grad_tokens.reshape(2, 64, 1024), grad_wq, total
+
+
+MESH = pl.DeviceIdType.MESH
+
+
+def flip(value, bits):
+    for bit in (1, 2, 4):
+        if bits & bit:
+            value = value + bit - 2 * bit * lax.rem(lax.div(value, bit), 2)
+    return value
+
+
+def greet(head, blk, heads, blks):
+    barrier = pltpu.get_barrier_semaphore()
+    for k in heads:
+        pl.semaphore_signal(barrier, inc=1, device_id=(flip(head, k), blk), device_id_type=MESH)
+    for k in blks:
+        pl.semaphore_signal(barrier, inc=1, device_id=(head, flip(blk, k)), device_id_type=MESH)
+    pl.semaphore_wait(barrier, len(heads) + len(blks))
+
+
+def send(source, target, send_sem, recv_sem, head, blk):
+    return pltpu.make_async_remote_copy(
+        src_ref=source,
+        dst_ref=target,
+        send_sem=send_sem,
+        recv_sem=recv_sem,
+        device_id=(head, blk),
+        device_id_type=MESH,
+    )
+
+
+class Swap:
+    def __init__(self, head, blk, axis, source, target, sems):
+        self.copies = []
+        count = 4 if axis == "head" else 8
+        me = head if axis == "head" else blk
+        for k in range(1, count):
+            peer = flip(me, k)
+            where = (peer, blk) if axis == "head" else (head, peer)
+            self.copies.append(
+                send(source(peer), target(me), sems.at[0, k], sems.at[1, k], *where)
+            )
+
+    def start(self):
+        for copy in self.copies:
+            copy.start()
+
+    def arrive(self):
+        for copy in self.copies:
+            copy.wait_recv()
+
+    def drain(self):
+        for copy in self.copies:
+            copy.wait_send()
+
+
+class Plane:
+    def __init__(self, head, blk, own, slot, sems):
+        sibling = flip(blk, 1)
+        self.first = [send(own, slot(blk), sems.at[0, 0], sems.at[1, 0], head, sibling)]
+        self.passed = []
+        for i, k in enumerate((2, 4, 6)):
+            peer = flip(blk, k)
+            self.first.append(
+                send(own, slot(blk), sems.at[0, i + 1], sems.at[1, i + 1], head, peer)
+            )
+            self.passed.append(
+                send(slot(peer), slot(peer), sems.at[0, i + 4], sems.at[1, i + 4], head, sibling)
+            )
+
+    def start(self):
+        for i in (3, 1, 2, 0):
+            self.first[i].start()
+
+    def forward(self, i):
+        self.first[i + 1].wait_recv()
+        self.passed[i].start()
+
+    def arrive(self, i):
+        if i < 0:
+            self.first[0].wait_recv()
+        else:
+            self.passed[i].wait_recv()
+
+    def finish(self):
+        for i in range(3):
+            self.forward(i)
+        for i in range(-1, 3):
+            self.arrive(i)
+
+    def drain(self):
+        for copy in self.first + self.passed:
+            copy.wait_send()
+
+
+def line_order(head, step):
+    low = jnp.minimum(head, 3 - head)
+    swap = low * ((step == 0).astype(jnp.int32) - (step == 1).astype(jnp.int32))
+    at = step + swap
+    return jnp.where(head < 2, at, 3 - at)
+
+
+class Line:
+    def __init__(self, head, blk, own, slot, sems):
+        self.head, self.blk, self.own, self.slot, self.sems = head, blk, own, slot, sems
+
+    def copy(self, source, at, up, k):
+        head = self.head
+        target = jnp.where(up, head + 1, head - 1)
+        way = jnp.where(up, 0, 1)
+        return send(
+            source, self.slot(at), self.sems.at[0, way, k], self.sems.at[1, way, k], target, self.blk
+        )
+
+    def start(self):
+        head = self.head
+
+        @pl.when(head < 3)
+        def _():
+            self.copy(self.own, head, True, 0).start()
+
+        @pl.when(head > 0)
+        def _():
+            self.copy(self.own, head, False, 0).start()
+
+    def step(self, at):
+        head = self.head
+        up = at < head
+        k = jnp.where(up, head - 1 - at, at - head - 1)
+        self.copy(self.slot(at), at, up, k).wait_recv()
+
+        @pl.when(jnp.where(up, head < 3, head > 0))
+        def _():
+            self.copy(self.slot(at), at, up, k + 1).start()
+
+    def drain(self):
+        head = self.head
+        for k in range(3):
+
+            @pl.when(jnp.logical_and(head < 3, head >= k))
+            def _():
+                self.copy(self.own, head, True, k).wait_send()
+
+            @pl.when(jnp.logical_and(head > 0, head + k <= 3))
+            def _():
+                self.copy(self.own, head, False, k).wait_send()
+
+
+def half_lane(shape):
+    return lax.broadcasted_iota(jnp.int32, shape, 1) < 64
+
+
+def lane_swap(value):
+    lane = lax.broadcasted_iota(jnp.int32, value.shape, 1)
+    return jnp.where(
+        lax.rem(lane, 64) < 32, pltpu.roll(value, 96, 1), pltpu.roll(value, 32, 1)
+    )
+
+
+def turn_tables(table, sign):
+    lane = lax.broadcasted_iota(jnp.int32, table.shape, 1)
+    cosine = jnp.where(lane < 32, table, 0.0)
+    cosine = cosine + pltpu.roll(cosine, 32, 1)
+    sine = jnp.where(jnp.logical_and(lane >= 32, lane < 64), table, 0.0) * sign
+    sine = sine - pltpu.roll(sine, 96, 1)
+    both = (cosine + pltpu.roll(cosine, 64, 1), sine + pltpu.roll(sine, 64, 1))
+    return both, (jnp.where(lane < 64, cosine, 1.0), sine)
+
+
+def join_halves(top, bottom, right):
+    left = half_lane(top.shape)
+    if right:
+        return jnp.where(left, pltpu.roll(top, 64, 1), bottom)
+    return jnp.where(left, top, pltpu.roll(bottom, 64, 1))
+
+
+def first_kernel(
+    tok, tab, wqp, ttab, tix, sca, scm,
+    tiles, normed, wq, scales, tabg,
+    tokg, wqz, turned, part, sums, parts, out_tiles,
+    zsem, lsem, tsem, wsem, asem, bsem, psem,
+):
+    head, blk = lax.axis_index("head"), lax.axis_index("blk")
+    greet(head, blk, (1, 2, 3), range(1, 8))
+    zswap = Swap(head, blk, "head", lambda i: wqp.at[i], lambda i: wqz.at[i], zsem)
+    zswap.start()
+    line = Line(head, blk, tok, lambda i: tokg.at[i], lsem)
+    tline = Line(head, blk, tab, lambda i: tabg.at[i], tsem)
+    tline.start()
+    line.start()
+    turned[...] = jnp.transpose(ttab[...])
+    rows = turned[pl.ds(pl.multiple_of((head * 8 + blk) * 8, 8), 8), :]
+    step_lane = lax.broadcasted_iota(jnp.int32, rows.shape, 1)
+    terms = []
+    for weight in (sca, scm):
+        for seq in range(2):
+            column = jnp.sum(jnp.where(step_lane == tix[seq], rows, 0.0), axis=1, keepdims=True)
+            terms.append(jnp.sum(column * weight[...].astype(F32), axis=0, keepdims=True))
+    part[...] = jnp.concatenate(terms + [jnp.zeros((4, 1024), F32)], axis=0)
+    one = Swap(head, blk, "blk", lambda i: part, lambda i: sums.at[i], asem)
+    one.start()
+    sums[blk] = part[...]
+    wqz[head] = wqp[head]
+    tokg[head] = tok[...]
+    tabg[head] = tab[...]
+    zswap.arrive()
+    plane = Plane(head, blk, wqz, lambda i: wq.at[:, i], wsem)
+    plane.start()
+    wq[:, pl.ds(blk, 1)] = wqz[...].reshape(4, 1, 32, 768)
+    one.arrive()
+    total = sums[0]
+    for i in range(1, 8):
+        total = total + sums[i]
+    parts[head] = total
+    two = Swap(head, blk, "head", lambda i: parts.at[head], lambda i: parts.at[i], bsem)
+    two.start()
+    two.arrive()
+    total = 1.0 + ((parts[0] + parts[1]) + (parts[2] + parts[3]))
+    scales[...] = total
+
+    def gather(step, carry):
+        at = line_order(head, step)
+
+        @pl.when(step > 0)
+        def _():
+            tline.step(at)
+            line.step(at)
+
+        for seq in range(2):
+            unit, _ = norm_stats(tokg[at, seq].astype(F32))
+            normed[at, pl.ds(64 * seq, 64), :] = (unit * scales[seq : seq + 1, :]).astype(BF)
+        return carry
+
+    lax.fori_loop(0, 4, gather, 0)
+    plane.finish()
+
+    def project(step, carry):
+        at = line_order(head, step)
+        proj = jnp.dot(
+            normed[at], wq[...].reshape(1024, 768), preferred_element_type=F32
+        )
+        for seq in range(2):
+            table = tabg[at]
+            if seq:
+                table = pltpu.roll(table, 64, 1)
+            both, keyed = turn_tables(table, 1.0)
+            mine = proj[64 * seq : 64 * seq + 64]
+            for j in range(4):
+                kv = mine[:, 128 * j : 128 * j + 128]
+                kv = kv * keyed[0] + lane_swap(kv) * keyed[1]
+                out_tiles[4 * seq + j, at, 0:64, :] = kv.astype(BF)
+            for i in range(2):
+                query = mine[:, 512 + 128 * i : 640 + 128 * i]
+                query = query * both[0] + lane_swap(query) * both[1]
+                for right in range(2):
+                    packed = join_halves(query[:32], query[32:], right)
+                    out_tiles[4 * seq + 2 * i + right, at, 64:96, :] = packed.astype(BF)
+        move(at).start()
+        tiles[at, blk] = out_tiles[blk, at]
+        return carry
+
+    def move(at):
+        return Swap(
+            head, blk, "blk", lambda i: out_tiles.at[i, at], lambda i: tiles.at[at, i], psem.at[at]
+        )
+
+    lax.fori_loop(0, 4, project, 0)
+    for at in range(4):
+        move(at).arrive()
+    for at in range(4):
+        move(at).drain()
+    for copies in (zswap, line, tline, plane, one, two):
+        copies.drain()
+
+
+def whole(count):
+    return [pl.BlockSpec(memory_space=pltpu.VMEM)] * count
+
+
+def phase_one_kernel(tokens, table, wq_parts, time_table, time_index, scale_attn, scale_mlp):
+    dma = pltpu.SemaphoreType.DMA
+    return pl.pallas_call(
+        first_kernel,
+        out_shape=(
+            jax.ShapeDtypeStruct((4, 8, 96, 128), BF),
+            jax.ShapeDtypeStruct((4, 128, 1024), BF),
+            jax.ShapeDtypeStruct((4, 8, 32, 768), BF),
+            jax.ShapeDtypeStruct((8, 1024), F32),
+            jax.ShapeDtypeStruct((4, 64, 128), F32),
+        ),
+        in_specs=whole(4) + [pl.BlockSpec(memory_space=pltpu.SMEM)] + whole(2),
+        out_specs=whole(5),
+        scratch_shapes=[
+            pltpu.VMEM((4, 2, 64, 1024), BF),
+            pltpu.VMEM((4, 32, 768), BF),
+            pltpu.VMEM((256, 64), F32),
+            pltpu.VMEM((8, 1024), F32),
+            pltpu.VMEM((8, 8, 1024), F32),
+            pltpu.VMEM((4, 8, 1024), F32),
+            pltpu.VMEM((8, 4, 96, 128), BF),
+            dma((2, 4)),
+            dma((2, 2, 3)),
+            dma((2, 2, 3)),
+            dma((2, 7)),
+            dma((2, 8)),
+            dma((2, 4)),
+            dma((4, 2, 8)),
+        ],
+        compiler_params=pltpu.CompilerParams(
+            collective_id=0, has_side_effects=True, vmem_limit_bytes=48 << 20
+        ),
+        name="first",
+    )(tokens, table, wq_parts, time_table, time_index, scale_attn, scale_mlp)
+def contract_rows_precise(left, right):
+    return lax.dot_general(
+        left, right, (((0,), (0,)), ((), ())), precision=PRECISE, preferred_element_type=F32
+    )
 
 
 def blocked(
@@ -527,26 +856,22 @@
     place = lax.axis_index(("head", "blk"))
     embed = time_table[time_index]
     embed_own = lax.dynamic_slice_in_dim(embed, place * 8, 8, 1)
-    scale_parts = jnp.concatenate(
-        [
-            jnp.dot(embed_own, scale_attn.astype(F32), precision=PRECISE),
-            jnp.dot(embed_own, scale_mlp.astype(F32), precision=PRECISE),
-        ],
-        axis=0,
-    )
     cosine, sine = rotary_tables(positions, HEAD_DIM)
-    table = jnp.concatenate([cosine[:, :, 0], sine[:, :, 0]], axis=-1).reshape(128, 64)
+    cosine, sine = cosine[:, :, 0], sine[:, :, 0]
+    table = jnp.concatenate([cosine[0], sine[0], cosine[1], sine[1]], axis=-1)
     wide = w_qkv.reshape(32, 3, 4, 4, 64)
     kv_cols = jnp.stack([wide[:, 1], wide[:, 2]], axis=3).reshape(32, 4, 512)
     wq_parts = jnp.concatenate([kv_cols, wide[:, 0].reshape(32, 4, 256)], axis=-1)
     wq_parts = jnp.swapaxes(wq_parts, 0, 1)
-    up_parts = jnp.swapaxes(w_up.reshape(32, 4, 1024), 0, 1)
-    tiles, normed, wq, scales, table_all = phase_one(tokens, table, wq_parts, scale_parts)
+    up_parts = jnp.transpose(w_up.reshape(32, 4, 8, 128), (2, 0, 1, 3)).reshape(8, 32, 512)
+    tiles, normed, wq, scales, table_all = phase_one_kernel(
+        tokens, table, wq_parts, time_table, time_index, scale_attn, scale_mlp
+    )
     mixed, lse, received, up, down, out, cot_all = phase_two(
         tiles, up_parts, w_down, w_out, cotangent
     )
     grad_rx, grad_middle, middle, out_partial, grad_down, grad_up, grad_out, sums = phase_three(
-        received, tokens, out, up, down, cot_all, cotangent, scales
+        received, tokens, out, up, down, cot_all, scales
     )
     back, output, down_own, up_own, out_own = phase_four(
         tiles, grad_rx, mixed, lse, out_partial, middle, grad_down, grad_up, grad_out
@@ -560,15 +885,10 @@
         axis=0,
     )
     qkv_own = jnp.transpose(wide, (2, 0, 1, 3, 4)).reshape(32, 3072)
+    up_own = jnp.transpose(up_own.reshape(8, 32, 4, 128), (1, 2, 0, 3)).reshape(32, 4096).astype(F32)
     grad_attn = contract_rows_precise(embed_own, total[:2])
     grad_mlp = contract_rows_precise(embed_own, total[2:])
     return output, grad_tokens, qkv_own, out_own, up_own, down_own, grad_attn, grad_mlp
-
-
-def contract_rows_precise(left, right):
-    return lax.dot_general(
-        left, right, (((0,), (0,)), ((), ())), precision=PRECISE, preferred_element_type=F32
-    )
 
 
 def solution(mesh):

time: 605 us -> 569 us (0.940)
  blocking collectives: 128 us -> 42.2 us
  Pallas kernels: 0 us -> 55.2 us
  waiting for transfers between devices: 205 us -> 212 us
  local copies, waits for them, and re-layouts: 52 us -> 45.2 us
    pallas_call x0 -> x1, Pallas kernels: none -> 55.2 us  [phase_one_kernel(): pl.pallas_call(first_kernel, out_shape=(jax.ShapeDtypeStruct((4, 8, 96, 1...]
    all_to_all x3 -> x1, waiting for transfers between devices: 61.9 us -> 13.8 us  [scatter_head(): lax.all_to_all(partial.astype(BF).reshape(4, 128, 1024), 'head', 0, 0, ti...]
    psum x1 -> x0, blocking collectives: 39.7 us -> none  [phase_one(): scales = lax.psum(scale_parts, ('head', 'blk'))]
    all_to_all x5 -> x6, waiting for transfers between devices: 15.6 us -> 45.8 us  [the longest x2 36.5 us: scatter_blk(): parts = lax.all_to_all(partial, 'blk', 0, 0, tiled=True)]
    all_to_all x2 -> x0, blocking collectives: 27.1 us -> none  [the longest x1 13.8 us: phase_one(): wq = lax.all_to_all(wq_parts, 'head', 0, 0, tiled=True)]
    all_gather x1 -> x0, blocking collectives: 19.7 us -> none  [phase_one(): table_all = lax.all_gather(table, 'head', axis=0)]
    all_gather x7 -> x5, waiting for transfers between devices: 78.6 us -> 96.5 us  [the longest x1 29.9 us: phase_three(): normed_all = lax.all_gather(normed_two, 'blk', axis=0, tiled=True)]
    all_to_all x1 -> x2, waiting for transfers between devices: 0.01 us -> 13.5 us  [to_all(): lax.all_to_all(tiles.reshape(32, 32, 128), ('head', 'blk'), 0, 0, tiled=T...]
  transfers between devices with their start and end apart: 21 -> 19, of which waited for: 12 -> 16; matrix products, arithmetic and copies ran while one was open for 28% -> 28% of each run, Pallas kernels for 0% -> 10%
where the time goes in v2:
time: 569 us; the launch traced here: 558 us
  waiting for transfers between devices  212 us (37%)
  matrix products  75.8 us (13%)
  starting transfers between devices  58.3 us (10%)
  Pallas kernels  55.2 us (10%)
  other arithmetic  54.6 us (10%)
  local copies, waits for them, and re-layouts  45.2 us (8%)
  blocking collectives  42.2 us (7%)
  between operations  14.9 us (3%)
    pallas_call x1, Pallas kernels, phase_one_kernel(): pl.pallas_call(first_kernel, out_shape=(jax.ShapeDtypeStruct((4, 8, 96, 1...  55.2 us
    psum x1, blocking collectives, phase_five(): total = lax.psum(jnp.concatenate([first, sums], axis=0), ('head', 'blk'))  42.2 us
    all_to_all x2, waiting for transfers between devices, scatter_blk(): parts = lax.all_to_all(partial, 'blk', 0, 0, tiled=True)  36.5 us
    all_gather x1, waiting for transfers between devices, phase_three(): normed_all = lax.all_gather(normed_two, 'blk', axis=0, tiled=True)  29.9 us
    all_gather x1, waiting for transfers between devices, phase_two(): cot_all = lax.all_gather(cotangent, 'blk', axis=0).reshape(8, 128, 1024)  29.2 us
    dot_general x6, matrix products, contract_cols(): lax.dot_general(left, right, (((1,), (1,)), ((), ())), preferred_element_...  27.9 us
    all_gather x1, waiting for transfers between devices, phase_two(): down = lax.all_gather(w_down, 'head', axis=0)  24.5 us
    dot_general x6, matrix products, contract_rows(): lax.dot_general(left, right, (((0,), (0,)), ((), ())), preferred_element_...  23 us
  transfers between devices with their start and end apart: 19, of which 16 were waited for; matrix products, arithmetic and copies ran while one was open for 28% of the time, Pallas kernels for 10%

profile of v2, /device:TPU:0, one launch (start us, length us, event | category | flops | bytes accessed | tf_op | source)
XLA Modules:
  0.0 558.3 jit_solution(5615017585743453137)
XLA Ops:
  9.8 5.2 all-to-all-start.1
  16.8 55.2 %first.1 = (bf16[4,8,96,128]{3,2,1,0:T(8,128)(2,1)S(1)}, bf16[4,128,1024]{2,1,0:T(8,128)(2,1)S(1)}, bf16[4,8,32,768]{3,2,1,0:T(8,128)(2,1)S(1)}, f32[8,1024]{1,0:T(8,128)S(1)}, f32[4,64,128]{2,1,0:T(8,128)S(1)}) custom-call(bf16[2,64,1024]{2,1,0:T(8,128)(2,1)S(1)} %copy-done, f32[64,128]{1,0:T(8,128)S(1)} %pad_maximum_fusion.9.tab, ...), custom_call_target="tpu_custom_call" | custom-call | tf_op jit(solution)/shard_map/first/pallas_call | solution.py:805
  72.3 8.1 %multiply_reduce_fusion = (f32[2048]{0:T(1024)S(1)}, f32[2048,2048]{1,0:T(8,128)}) fusion(bf16[2048,64]{1,0:T(8,128)(2,1)S(1)} %bitcast.186, bf16[2048,128]{1,0:T(8,128)(2,1)S(1)} %bitcast.176), kind=kOutput, calls=%fused_computation.7 | convolution fusion | flops 545257472 | bytes 17571840 | tf_op jit(solution)/shard_map/dot_general | solution.py:59
  80.4 8.6 %fusion = f32[2048]{0:T(1024)S(1)} fusion(f32[2048,2048]{1,0:T(8,128)} %get-tuple-element.62, f32[2048]{0:T(1024)S(1)} %get-tuple-element.61), kind=kLoop, calls=%fused_computation.4 | loop fusion | flops 12580864 | bytes 16793600 | tf_op jit(solution)/shard_map/reduce_sum | solution.py:412
  88.9 7.5 %fusion.7 = f32[64,2048]{1,0:T(8,128)S(1)} fusion(f32[2048,2048]{1,0:T(8,128)} %get-tuple-element.62, f32[2048]{0:T(1024)S(1)} %get-tuple-element.61, bf16[2048,128]{1,0:T(8,128)(2,1)S(1)} %bitcast.177, f32[2048]{0:T(1024)S(1)} %fusion), kind=kOutput, calls=%fused_computation.16 | convolution fusion | flops 549584896 | bytes 17842176 | tf_op jit(solution)/shard_map/dot_general | solution.py:53
  100.2 3.6 all-to-all-start
  104.9 9.5 %all-to-all-done = bf16[32,32,128]{2,1,0:T(8,128)(2,1)S(1)} async-done(((bf16[32,32,128]{2,1,0:T(8,128)(2,1)}), bf16[32,32,128]{2,1,0:T(8,128)(2,1)S(1)}, u32[]{:S(2)}, u32[]{:S(2)}) %all-to-all-start) | async-done | bytes 262176 | tf_op jit(solution)/shard_map/all_to_all | solution.py:402
  117.4 2.2 fusion.55
  122.5 13.0 %all-gather.14.cloned.1.call-done = bf16[32,32,512]{2,1,0:T(8,128)(2,1)} async-done(((bf16[8,32,512]{2,1,0:T(8,128)(2,1)}), bf16[32,32,512]{2,1,0:T(8,128)(2,1)}) %all-gather.14.cloned.1.call-update) | async-done | bytes 1048592 | tf_op jit(solution)/shard_map/all_gather | solution.py:418
  135.4 29.9 %all-gather.10.cloned.1.call-done = bf16[1024,1024]{1,0:T(8,128)(2,1)} async-done(((bf16[128,1024]{1,0:T(8,128)(2,1)}), bf16[1024,1024]{1,0:T(8,128)(2,1)}) %all-gather.10.cloned.1.call-update) | async-done | bytes 2097168 | tf_op jit(solution)/shard_map/all_gather | solution.py:449
  165.3 4.9 multiply_convert_fusion.1
  170.2 24.5 %all-gather.16.cloned.1.call-done = bf16[512,1024]{1,0:T(8,128)(2,1)} async-done(((bf16[128,1024]{1,0:T(8,128)(2,1)}), bf16[512,1024]{1,0:T(8,128)(2,1)}) %all-gather.16.cloned.1.call-update) | async-done | bytes 1048592 | tf_op jit(solution)/shard_map/all_gather | solution.py:419
  194.7 29.2 %all-gather.18.cloned.1.call-done = bf16[16,64,1024]{2,1,0:T(8,128)(2,1)} async-done(((bf16[2,64,1024]{2,1,0:T(8,128)(2,1)}), bf16[16,64,1024]{2,1,0:T(8,128)(2,1)}) %all-gather.18.cloned.1.call-update) | async-done | bytes 2097168 | tf_op jit(solution)/shard_map/all_gather | solution.py:421
  223.9 4.4 fusion.15
  228.3 2.6 convolution_convert_fusion
  230.9 4.4 all-to-all-start.3
  235.3 4.1 convolution_convert_fusion.1
  239.4 22.6 %all-to-all-done.3 = bf16[8,128,1024]{2,1,0:T(8,128)(2,1)} async-done(((bf16[8,128,1024]{2,1,0:T(8,128)(2,1)}), bf16[8,128,1024]{2,1,0:T(8,128)(2,1)}, u32[]{:S(2)}, u32[]{:S(2)}) %all-to-all-start.3) | async-done | bytes 2097184 | tf_op jit(solution)/shard_map/all_to_all | solution.py:433
  262.0 4.4 all-to-all-start.2
  266.3 9.9 %fusion.2 = bf16[2048,2048]{1,0:T(8,128)(2,1)} fusion(f32[2048,2048]{1,0:T(8,128)} %get-tuple-element.62, f32[2048]{0:T(1024)S(1)} %log_add_fusion), kind=kLoop, calls=%fused_computation.6 | loop fusion | flops 12582912 | bytes 25174016 | tf_op jit(solution)/shard_map/convert_element_type | solution.py:482
  276.2 2.0 convert_reduce_fusion
  279.1 13.9 %all-to-all-done.2 = bf16[8,128,1024]{2,1,0:T(8,128)(2,1)} async-done(((bf16[8,128,1024]{2,1,0:T(8,128)(2,1)}), bf16[8,128,1024]{2,1,0:T(8,128)(2,1)}, u32[]{:S(2)}, u32[]{:S(2)}) %all-to-all-start.2) | async-done | bytes 2097184 | tf_op jit(solution)/shard_map/all_to_all | solution.py:433
  293.0 2.1 convert_reduce_fusion.1
  295.2 1.8 convert_add_fusion
  301.9 4.2 all-to-all-start.4
  306.1 4.3 convolution_convert_fusion.5
  310.4 2.3 convolution_convert_fusion.6
  312.7 4.0 all-to-all-done.4
  316.7 4.2 all-to-all-start.11
  321.8 2.5 copy.115
  324.3 2.5 copy.116
  326.7 2.3 pad_maximum_fusion.2
  331.7 10.0 %multiply_convert_fusion = bf16[2048,2048]{1,0:T(8,128)(2,1)} fusion(f32[2048,2048]{1,0:T(8,128)} %get-tuple-element.62, bf16[2048,64]{0,1:T(8,128)(2,1)S(1)} %reshape.335, f32[2048]{0:T(1024)S(1)} %fusion.17, f32[2048]{0:T(1024)S(1)} %log_add_fusion, bf16[2048,128]{1,0:T(8,128)(2,1)} %bitcast.178), kind=kOutput, calls=%fused_computation.1 | convolution fusion | flops 557842432 | bytes 25968640 | tf_op jit(solution)/shard_map/dot_general | solution.py:59
  341.7 5.4 all-to-all-done.11
  347.1 4.4 all-to-all-start.13
  351.5 6.1 %fusion.5 = bf16[2048,64]{0,1:T(8,128)(2,1)S(1)} fusion(bf16[2048,2048]{1,0:T(8,128)(2,1)} %multiply_convert_fusion, bf16[2048,64]{1,0:T(8,128)(2,1)} %bitcast.187), kind=kOutput, calls=%fused_computation.14 | convolution fusion | flops 537133056 | bytes 8912896 | tf_op jit(solution)/shard_map/dot_general | solution.py:484
  357.6 2.2 reshape.375
  360.8 5.0 fusion.6
  368.0 5.8 %convolution_convert_fusion.7 = bf16[4,8,64,64]{3,2,1,0:T(8,128)(2,1)S(1)} fusion(bf16[4,8,64,2048]{3,2,1,0:T(8,128)(2,1)} %bitcast.182, bf16[2048,64,1,1]{0,1,2,3:T(8,128)(2,1)} %reshape.375), kind=kOutput, calls=%fused_computation.36 | convolution fusion | flops 537001984 | bytes 8912896 | tf_op jit(solution)/shard_map/dot_general | solution.py:482
  376.8 4.2 all-to-all-start.5
  381.1 1.8 convolution_convert_fusion.2
  384.3 9.4 %all-to-all-done.5 = bf16[8,4,96,128]{3,2,1,0:T(8,128)(2,1)} async-done(((bf16[8,4,96,128]{3,2,1,0:T(8,128)(2,1)}), bf16[8,4,96,128]{3,2,1,0:T(8,128)(2,1)}, u32[]{:S(2)}, u32[]{:S(2)}) %all-to-all-start.5) | async-done | bytes 786464 | tf_op jit(solution)/shard_map/all_to_all | solution.py:489
  393.7 4.6 all-to-all-start.9
  399.5 2.2 reduce_sum.208
  405.9 2.4 subtract_convert_fusion
  409.9 2.2 reshape.339
  413.4 3.2 pad_maximum_fusion.3
  416.6 8.3 %all-to-all-done.9 = bf16[8,4,32,1024]{3,2,1,0:T(8,128)(2,1)} async-done(((bf16[8,4,32,1024]{3,2,1,0:T(8,128)(2,1)}), bf16[8,4,32,1024]{3,2,1,0:T(8,128)(2,1)}, u32[]{:S(2)}, u32[]{:S(2)}) %all-to-all-start.9) | async-done | bytes 2097184 | tf_op jit(solution)/shard_map/all_to_all | solution.py:495
  424.9 3.4 all-to-all-start.12
  428.3 1.9 bitcast_dynamic-update-slice_fusion
  430.2 2.7 reduce_sum.206
  433.0 2.2 all-to-all-done.12
  435.2 4.0 all-to-all-start.10
  440.9 2.1 convolution_convert_fusion.3
  444.4 3.4 all-to-all-done.10
  447.8 4.3 all-to-all-start.7
  452.1 2.0 convolution_convert_fusion.4
  454.1 19.1 %all-to-all-done.7 = bf16[8,4,32,768]{3,2,1,0:T(8,128)(2,1)} async-done(((bf16[8,4,32,768]{3,2,1,0:T(8,128)(2,1)}), bf16[8,4,32,768]{3,2,1,0:T(8,128)(2,1)}, u32[]{:S(2)}, u32[]{:S(2)}) %all-to-all-start.7) | async-done | bytes 1572896 | tf_op jit(solution)/shard_map/all_to_all | solution.py:520
  473.1 3.5 all-to-all-start.6
  477.8 2.3 convert_reduce_fusion.2
  483.5 2.4 reduce_sum.205
  485.9 13.8 %all-to-all-done.6 = bf16[4,128,1024]{2,1,0:T(8,128)(2,1)S(1)} async-done(((bf16[4,128,1024]{2,1,0:T(8,128)(2,1)}), bf16[4,128,1024]{2,1,0:T(8,128)(2,1)S(1)}, u32[]{:S(2)}, u32[]{:S(2)}) %all-to-all-start.6) | async-done | bytes 1048608 | tf_op jit(solution)/shard_map/all_to_all | solution.py:426
  499.7 3.4 all-to-all-start.8
  503.7 42.2 %psum.7 = f32[4,1024]{1,0:T(4,128)S(1)} all-reduce(f32[4,1024]{1,0:T(4,128)S(1)} %pad_maximum_fusion.10), channel_id=1, replica_groups=mesh['head'=4,'blk'=8] {'head','blk'}, use_global_device_ids=true, to_apply=%region_21.0 | all-reduce | flops 4096 | bytes 32768 | tf_op jit(solution)/shard_map/psum | solution.py:518
  (168 shorter events, 54.0 us)
Async XLA Ops:
  7.2 7.9 %copy-start.24 = (s32[2,64]{1,0:T(2,128)S(1)}, s32[2,64]{1,0:T(2,128)}, u32[]{:S(2)}) copy-start(s32[2,64]{1,0:T(2,128)} %param.12) | copy-start | bytes 1540
  7.2 7.9 %copy-start.23 = (bf16[32,3072]{1,0:T(8,128)(2,1)S(1)}, bf16[32,3072]{1,0:T(8,128)(2,1)}, u32[]{:S(2)}) copy-start(bf16[32,3072]{1,0:T(8,128)(2,1)} %param.15) | copy-start | bytes 589828
  7.2 110.2 %all-gather.12.cloned.1.call-start = ((), (), s32[]{:S(2)}) async-start(), calls=%async_computation.15 | async-start | bytes 2162688 | tf_op jit(solution)/shard_map/all_gather | solution.py:420
  9.8 90.4 %all-to-all-start.1 = ((bf16[8,32,512]{2,1,0:T(8,128)(2,1)}), bf16[8,32,512]{2,1,0:T(8,128)(2,1)}, u32[]{:S(2)}, u32[]{:S(2)}) async-start(bf16[8,32,512]{2,1,0:T(8,128)(2,1)} %reshape.325), calls=%async_computation.1 | async-start | bytes 524288 | tf_op jit(solution)/shard_map/all_to_all | solution.py:417
  15.3 1.4 copy-start
  15.3 1.4 copy-start.1
  15.4 1.4 copy-start.2
  15.4 1.4 copy-start.3
  15.4 1.4 copy-start.4
  72.0 16.9 %copy-start.9 = (bf16[4,8,64,128]{3,2,1,0:T(8,128)(2,1)}, bf16[4,8,64,128]{3,2,1,0:T(8,128)(2,1)S(1)}, u32[]{:S(2)}) copy-start(bf16[4,8,64,128]{3,2,1,0:T(8,128)(2,1)S(1)} %slice.149) | copy-start | bytes 1572868
  72.3 8.1 %copy-start.16 = (bf16[4,8,64,64]{3,2,1,0:T(8,128)(2,1)}, bf16[4,8,64,64]{3,2,1,0:T(8,128)(2,1)S(1)}, u32[]{:S(2)}) copy-start(bf16[4,8,64,64]{3,2,1,0:T(8,128)(2,1)S(1)} %pad_maximum_fusion) | copy-start | bytes 786436
  96.4 0.8 copy-start.17
  100.2 14.2 %all-to-all-start = ((bf16[32,32,128]{2,1,0:T(8,128)(2,1)}), bf16[32,32,128]{2,1,0:T(8,128)(2,1)S(1)}, u32[]{:S(2)}, u32[]{:S(2)}) async-start(bf16[32,32,128]{2,1,0:T(8,128)(2,1)} %bitcast.208), calls=%async_computation | async-start | bytes 524288 | tf_op jit(solution)/shard_map/all_to_all | solution.py:402
  103.8 31.6 %all-gather.14.cloned.1.call-start = ((), (), s32[]{:S(2)}) async-start(), calls=%async_computation.16 | async-start | bytes 1310720 | tf_op jit(solution)/shard_map/all_gather | solution.py:418
  104.6 60.8 %all-gather.10.cloned.1.call-start = ((), (), s32[]{:S(2)}) async-start(), calls=%async_computation.14 | async-start | bytes 2359296 | tf_op jit(solution)/shard_map/all_gather | solution.py:449
  117.3 3.9 copy-start.18
  119.6 0.8 copy-start.5
  121.3 73.4 %all-gather.16.cloned.1.call-start = ((), (), s32[]{:S(2)}) async-start(), calls=%async_computation.17 | async-start | bytes 1310720 | tf_op jit(solution)/shard_map/all_gather | solution.py:419
  121.9 102.0 %all-gather.18.cloned.1.call-start = ((), (), s32[]{:S(2)}) async-start(), calls=%async_computation.18 | async-start | bytes 2359296 | tf_op jit(solution)/shard_map/all_gather | solution.py:421
  223.9 4.4 copy-start.26
  228.3 2.6 copy-start.27
  230.9 31.0 %all-to-all-start.3 = ((bf16[8,128,1024]{2,1,0:T(8,128)(2,1)}), bf16[8,128,1024]{2,1,0:T(8,128)(2,1)}, u32[]{:S(2)}, u32[]{:S(2)}) async-start(bf16[8,128,1024]{2,1,0:T(8,128)(2,1)} %bitcast.196), calls=%async_computation.3 | async-start | bytes 4194304 | tf_op jit(solution)/shard_map/all_to_all | solution.py:433
  262.0 31.0 %all-to-all-start.2 = ((bf16[8,128,1024]{2,1,0:T(8,128)(2,1)}), bf16[8,128,1024]{2,1,0:T(8,128)(2,1)}, u32[]{:S(2)}, u32[]{:S(2)}) async-start(bf16[8,128,1024]{2,1,0:T(8,128)(2,1)} %bitcast.197), calls=%async_computation.2 | async-start | bytes 4194304 | tf_op jit(solution)/shard_map/all_to_all | solution.py:433
  276.2 2.1 copy-start.6
  278.3 0.8 copy-start.10
  293.0 2.2 copy-start.7
  293.0 2.2 copy-start.11
  293.0 4.8 copy-start.13
  297.0 0.8 copy-start.14
  301.9 14.8 %all-to-all-start.4 = ((bf16[32,32,128]{2,1,0:T(8,128)(2,1)}), bf16[32,32,128]{2,1,0:T(8,128)(2,1)S(1)}, u32[]{:S(2)}, u32[]{:S(2)}) async-start(bf16[32,32,128]{2,1,0:T(8,128)(2,1)} %bitcast.209), calls=%async_computation.4 | async-start | bytes 524288 | tf_op jit(solution)/shard_map/all_to_all | solution.py:402
  306.1 4.3 copy-start.25
  306.1 4.3 copy-start.28
  316.7 30.4 %all-to-all-start.11 = ((bf16[4,8,32,512]{3,2,1,0:T(8,128)(2,1)}), bf16[4,8,32,512]{3,2,1,0:T(8,128)(2,1)}, u32[]{:S(2)}, u32[]{:S(2)}) async-start(bf16[4,8,32,512]{3,2,1,0:T(8,128)(2,1)} %bitcast.211), calls=%async_computation.11 | async-start | bytes 2097152 | tf_op jit(solution)/shard_map/all_to_all | solution.py:492
  347.1 29.8 %all-to-all-start.13 = ((bf16[4,128,1024]{2,1,0:T(8,128)(2,1)}), bf16[4,128,1024]{2,1,0:T(8,128)(2,1)}, u32[]{:S(2)}, u32[]{:S(2)}) async-start(bf16[4,128,1024]{2,1,0:T(8,128)(2,1)} %bitcast.188), calls=%async_computation.13 | async-start | bytes 2097152 | tf_op jit(solution)/shard_map/all_to_all | solution.py:491
  367.9 5.8 %copy-start.20 = (bf16[2048,64]{1,0:T(8,128)(2,1)S(1)}, bf16[2048,64]{1,0:T(8,128)(2,1)}, u32[]{:S(2)}) copy-start(bf16[2048,64]{1,0:T(8,128)(2,1)} %copy.112) | copy-start | bytes 786436
  374.2 6.9 %copy-start.19 = (bf16[128,1024]{1,0:T(8,128)(2,1)S(1)}, bf16[128,1024]{1,0:T(8,128)(2,1)}, u32[]{:S(2)}) copy-start(bf16[128,1024]{1,0:T(8,128)(2,1)} %copy-done.18) | copy-start | bytes 786436
  376.8 16.8 %all-to-all-start.5 = ((bf16[8,4,96,128]{3,2,1,0:T(8,128)(2,1)}), bf16[8,4,96,128]{3,2,1,0:T(8,128)(2,1)}, u32[]{:S(2)}, u32[]{:S(2)}) async-start(bf16[8,4,96,128]{3,2,1,0:T(8,128)(2,1)} %copy.100), calls=%async_computation.5 | async-start | bytes 1572864 | tf_op jit(solution)/shard_map/all_to_all | solution.py:489
  393.7 31.2 %all-to-all-start.9 = ((bf16[8,4,32,1024]{3,2,1,0:T(8,128)(2,1)}), bf16[8,4,32,1024]{3,2,1,0:T(8,128)(2,1)}, u32[]{:S(2)}, u32[]{:S(2)}) async-start(bf16[8,4,32,1024]{3,2,1,0:T(8,128)(2,1)} %bitcast.183), calls=%async_computation.9 | async-start | bytes 4194304 | tf_op jit(solution)/shard_map/all_to_all | solution.py:495
  403.1 2.9 copy-start.21
  424.9 10.3 %all-to-all-start.12 = ((bf16[8,32,512]{2,1,0:T(8,128)(2,1)}), bf16[8,32,512]{2,1,0:T(8,128)(2,1)S(1)}, u32[]{:S(2)}, u32[]{:S(2)}) async-start(bf16[8,32,512]{2,1,0:T(8,128)(2,1)} %reduce_sum.208), calls=%async_computation.12 | async-start | bytes 524288 | tf_op jit(solution)/shard_map/all_to_all | solution.py:493
  435.2 12.6 %all-to-all-start.10 = ((bf16[4,32,1024]{2,1,0:T(8,128)(2,1)}), bf16[4,32,1024]{2,1,0:T(8,128)(2,1)}, u32[]{:S(2)}, u32[]{:S(2)}) async-start(bf16[4,32,1024]{2,1,0:T(8,128)(2,1)} %reduce_sum.206), calls=%async_computation.10 | async-start | bytes 524288 | tf_op jit(solution)/shard_map/all_to_all | solution.py:496
  444.3 7.7 %copy-start.22 = (bf16[512,768]{1,0:T(8,128)(2,1)S(1)}, bf16[512,768]{1,0:T(8,128)(2,1)}, u32[]{:S(2)}) copy-start(bf16[512,768]{1,0:T(8,128)(2,1)} %constant_dynamic-update-slice_fusion) | copy-start | bytes 2359300
  447.8 25.3 %all-to-all-start.7 = ((bf16[8,4,32,768]{3,2,1,0:T(8,128)(2,1)}), bf16[8,4,32,768]{3,2,1,0:T(8,128)(2,1)}, u32[]{:S(2)}, u32[]{:S(2)}) async-start(bf16[8,4,32,768]{3,2,1,0:T(8,128)(2,1)} %bitcast.185), calls=%async_computation.7 | async-start | bytes 3145728 | tf_op jit(solution)/shard_map/all_to_all | solution.py:520
  473.1 26.5 %all-to-all-start.6 = ((bf16[4,128,1024]{2,1,0:T(8,128)(2,1)}), bf16[4,128,1024]{2,1,0:T(8,128)(2,1)S(1)}, u32[]{:S(2)}, u32[]{:S(2)}) async-start(bf16[4,128,1024]{2,1,0:T(8,128)(2,1)} %bitcast.210), calls=%async_computation.6 | async-start | bytes 2097152 | tf_op jit(solution)/shard_map/all_to_all | solution.py:426
  477.8 3.9 copy-start.8
  477.8 3.9 copy-start.12
  485.9 61.0 %copy-start.15 = (f32[128,1024]{1,0:T(8,128)S(1)}, f32[128,1024]{1,0:T(8,128)}, u32[]{:S(2)}) copy-start(f32[128,1024]{1,0:T(8,128)} %copy-done.14) | copy-start | bytes 1572868
  499.7 49.1 %all-to-all-start.8 = ((bf16[4,32,768]{2,1,0:T(8,128)(2,1)}), bf16[4,32,768]{2,1,0:T(8,128)(2,1)S(1)}, u32[]{:S(2)}, u32[]{:S(2)}) async-start(bf16[4,32,768]{2,1,0:T(8,128)(2,1)} %reduce_sum.205), calls=%async_computation.8 | async-start | bytes 393216 | tf_op jit(solution)/shard_map/all_to_all | solution.py:521
Sparse Core Ops, SparseCore 0:
  10.9 63.6 all-gather.11
  106.2 29.1 all-gather.13
  137.9 27.3 all-gather.9
  166.7 27.9 all-gather.15
  196.4 27.3 all-gather.17

commit v3 on v2

--- a/solution.py
+++ b/solution.py
@@ -341,185 +341,6 @@
         - jnp.mean(scaled, axis=-1, keepdims=True)
         - unit * jnp.mean(scaled * unit, axis=-1, keepdims=True)
     )
-
-
-def pack_half(value):
-    lead, width = value.shape[:-2], value.shape[-1]
-    rows = value.shape[-2]
-    axis = value.ndim - 2
-    return jnp.concatenate(
-        [
-            lax.slice_in_dim(value, 0, rows // 2, axis=axis),
-            lax.slice_in_dim(value, rows // 2, rows, axis=axis),
-        ],
-        axis=-1,
-    )
-
-
-def unpack_half(value):
-    width = value.shape[-1] // 2
-    return jnp.concatenate([value[..., :width], value[..., width:]], axis=-2)
-
-
-def turn(value, table, sign):
-    cosine = table[..., :32]
-    sine = table[..., 32:64] * sign
-    first, second = value[..., :32], value[..., 32:]
-    return jnp.concatenate(
-        [first * cosine - second * sine, second * cosine + first * sine], axis=-1
-    )
-
-
-def phase_one(tokens, table, wq_parts, scale_parts):
-    token_all = lax.all_gather(tokens, "head", axis=0)
-    table_all = lax.all_gather(table, "head", axis=0)
-    scales = lax.psum(scale_parts, ("head", "blk"))
-    wq = lax.all_to_all(wq_parts, "head", 0, 0, tiled=True)
-    wq = jnp.swapaxes(lax.all_gather(wq, "blk", axis=0), 0, 1).reshape(1024, 768)
-    unit, _ = norm_stats(token_all.astype(F32))
-    scale_one = 1.0 + scales[:2]
-    normed = (unit * scale_one[None, :, None, :]).astype(BF).reshape(512, 1024)
-    proj = jnp.dot(normed, wq, preferred_element_type=F32).reshape(4, 2, 64, 768)
-    tab = table_all.reshape(4, 2, 64, 1, 64)
-    pairs = proj[..., :512].reshape(4, 2, 64, 4, 128)
-    keys = turn(pairs[..., :64], tab, 1.0)
-    query = turn(proj[..., 512:].reshape(4, 2, 64, 4, 64), tab, 1.0)
-    kv = jnp.concatenate([keys, pairs[..., 64:]], axis=-1).astype(BF)
-    kv = jnp.transpose(kv, (1, 3, 0, 2, 4))
-    query = pack_half(jnp.transpose(query.astype(BF), (1, 3, 0, 2, 4)))
-    tiles = jnp.concatenate([kv, query], axis=-2).reshape(8, 4, 96, 128)
-    tiles = jnp.swapaxes(lax.all_to_all(tiles, "blk", 0, 0, tiled=True), 0, 1)
-    return tiles, normed, wq, scales, table_all.reshape(512, 64)
-
-
-def split_tiles(tiles):
-    kv = tiles[:, :, :64].reshape(2048, 128)
-    query = unpack_half(tiles[:, :, 64:]).reshape(2048, 64)
-    return query, kv[:, :64], kv[:, 64:]
-
-
-def to_all(tiles):
-    return lax.all_to_all(
-        tiles.reshape(32, 32, 128), ("head", "blk"), 0, 0, tiled=True
-    ).reshape(4, 8, 32, 128)
-
-
-def phase_two(tiles, up_parts, w_down, w_out, cotangent):
-    query, keys, values = split_tiles(tiles)
-    scores = SCORE_SCALE * contract_cols(keys, query)
-    top = jnp.max(scores, axis=0, keepdims=True)
-    weights = jnp.exp(scores - top)
-    row_sum = jnp.sum(weights, axis=0, keepdims=True)
-    mixed = contract_rows(values, weights.astype(BF)) / row_sum
-    lse = top + jnp.log(row_sum)
-    attended = pack_half(jnp.transpose(mixed).astype(BF).reshape(4, 8, 64, 64))
-    received = to_all(attended)
-    up = lax.all_to_all(up_parts, "blk", 0, 0, tiled=True)
-    up = lax.all_gather(up, "head", axis=0)
-    down = lax.all_gather(w_down, "head", axis=0)
-    out = lax.all_gather(w_out, ("head", "blk"), axis=0).reshape(4, 8, 32, 1024)
-    cot_all = lax.all_gather(cotangent, "blk", axis=0).reshape(8, 128, 1024)
-    return mixed, lse, received, up, down, out, cot_all
-
-
-def scatter_head(partial):
-    parts = lax.all_to_all(
-        partial.astype(BF).reshape(4, 128, 1024), "head", 0, 0, tiled=True
-    )
-    return jnp.sum(parts.astype(F32), axis=0)
-
-
-def scatter_blk(partial):
-    parts = lax.all_to_all(partial, "blk", 0, 0, tiled=True)
-    return jnp.sum(parts.astype(F32), axis=0)
-
-
-def phase_three(received, tokens, out, up, down, cot_all, scales):
-    up = up.reshape(1024, 512)
-    down = down.reshape(512, 1024)
-    out = out.reshape(1024, 1024)
-    attended = unpack_half(received).reshape(4, 2, 4, 64, 64)
-    attended = jnp.transpose(attended, (1, 3, 0, 2, 4)).reshape(128, 1024)
-    middle = tokens.reshape(128, 1024).astype(F32) + jnp.dot(
-        attended, out, preferred_element_type=F32
-    )
-    unit, spread = norm_stats(middle)
-    scale_two = jnp.repeat(scales[2:4], 64, axis=0)
-    normed_two = (unit * scale_two).astype(BF)
-    normed_all = lax.all_gather(normed_two, "blk", axis=0, tiled=True)
-    cots = cot_all.reshape(1024, 1024)
-    cotangent = cot_all[lax.axis_index("blk")]
-    hidden = jnp.dot(normed_all, up, preferred_element_type=F32)
-    cdf = 0.5 * (1.0 + lax.erf(hidden * math.sqrt(0.5)))
-    active = (hidden * cdf).astype(BF)
-    out_partial = jnp.dot(active, down, preferred_element_type=F32).astype(BF)
-    grad_active = contract_cols(cots, down)
-    slope = cdf + hidden * jnp.exp(-0.5 * hidden * hidden) * (1.0 / math.sqrt(2 * math.pi))
-    grad_hidden = (grad_active * slope).astype(BF)
-    grad_down = contract_rows(active, cots).astype(BF).reshape(4, 128, 1024)
-    grad_up = contract_rows(normed_all, grad_hidden).astype(BF).reshape(4, 8, 32, 512)
-    grad_normed = scatter_blk(contract_cols(grad_hidden, up).astype(BF).reshape(8, 128, 1024))
-    grad_middle = cotangent.astype(F32) + norm_back(unit, spread, grad_normed, scale_two)
-    sums = jnp.sum((grad_normed * unit).reshape(2, 64, 1024), axis=1)
-    branch = grad_middle.astype(BF)
-    grad_out = contract_rows(attended, branch).astype(BF).reshape(4, 8, 32, 1024)
-    grad_att = contract_cols(branch, out).astype(BF).reshape(2, 64, 4, 4, 64)
-    grad_att = pack_half(jnp.transpose(grad_att, (2, 0, 3, 1, 4)))
-    grad_rx = to_all(grad_att)
-    out_partial = out_partial.reshape(8, 128, 1024)
-    return grad_rx, grad_middle, middle, out_partial, grad_down, grad_up, grad_out, sums
-
-
-def sum_parts(parts):
-    return jnp.sum(parts.astype(F32), axis=0)
-
-
-def phase_four(tiles, grad_rx, mixed, lse, out_partial, middle, grad_down, grad_up, grad_out):
-    query, keys, values = split_tiles(tiles)
-    grad = unpack_half(grad_rx).reshape(2048, 64)
-    delta = jnp.sum(jnp.transpose(grad).astype(F32) * mixed, axis=0, keepdims=True)
-    probs = jnp.exp(SCORE_SCALE * contract_cols(keys, query) - lse)
-    grad_values = jnp.dot(probs.astype(BF), grad, preferred_element_type=F32)
-    grad_scores = (probs * (contract_cols(values, grad) - delta)).astype(BF)
-    grad_keys = SCORE_SCALE * jnp.dot(grad_scores, query, preferred_element_type=F32)
-    grad_query = SCORE_SCALE * contract_rows(grad_scores, keys)
-    kv = jnp.concatenate([grad_keys, grad_values], axis=-1).astype(BF).reshape(4, 8, 64, 128)
-    packed = pack_half(grad_query.astype(BF).reshape(4, 8, 64, 64))
-    back = jnp.swapaxes(jnp.concatenate([kv, packed], axis=-2), 0, 1)
-    back = lax.all_to_all(back, "blk", 0, 0, tiled=True)
-    output = (middle + scatter_blk(out_partial)).astype(BF).reshape(2, 64, 1024)
-    down = sum_parts(lax.all_to_all(grad_down, "head", 0, 0, tiled=True))
-    up = sum_parts(lax.all_to_all(grad_up, "head", 0, 0, tiled=True))
-    up = lax.all_to_all(up.astype(BF), "blk", 0, 0, tiled=True)
-    out = jnp.swapaxes(grad_out, 0, 1)
-    out = sum_parts(lax.all_to_all(out, "blk", 0, 0, tiled=True))
-    out = sum_parts(lax.all_to_all(out.astype(BF), "head", 0, 0, tiled=True))
-    return back, output, down, up, out
-
-
-def phase_five(back, table_all, normed, wq, tokens, scales, grad_middle, sums):
-    kv = back[:, :, :64].reshape(2, 4, 4, 64, 128)
-    query = unpack_half(back[:, :, 64:]).reshape(2, 4, 4, 64, 64)
-    kv = jnp.transpose(kv, (2, 0, 3, 1, 4)).astype(F32)
-    query = jnp.transpose(query, (2, 0, 3, 1, 4)).astype(F32)
-    tab = jnp.swapaxes(table_all.reshape(4, 64, 2, 64), 1, 2)[:, :, :, None]
-    keys = turn(kv[..., :64], tab, -1.0)
-    query = turn(query, tab, -1.0)
-    kv = jnp.concatenate([keys, kv[..., 64:]], axis=-1).reshape(512, 512)
-    grad_proj = jnp.concatenate([kv, query.reshape(512, 256)], axis=-1).astype(BF)
-    normed = normed.reshape(512, 1024)
-    wq = wq.reshape(1024, 768)
-    grad_wq = contract_rows(normed, grad_proj).astype(BF)
-    grad_normed = scatter_head(contract_cols(grad_proj, wq))
-    unit, spread = norm_stats(tokens.reshape(128, 1024).astype(F32))
-    scale_one = jnp.repeat(scales[:2], 64, axis=0)
-    grad_tokens = grad_middle + norm_back(unit, spread, grad_normed, scale_one)
-    first = jnp.sum((grad_normed * unit).reshape(2, 64, 1024), axis=1)
-    total = lax.psum(jnp.concatenate([first, sums], axis=0), ("head", "blk"))
-    grad_wq = jnp.swapaxes(grad_wq.reshape(4, 8, 32, 768), 0, 1)
-    grad_wq = sum_parts(lax.all_to_all(grad_wq, "blk", 0, 0, tiled=True))
-    grad_wq = lax.all_to_all(grad_wq.astype(BF), "head", 0, 0, tiled=True).astype(F32)
-    return grad_tokens.reshape(2, 64, 1024), grad_wq, total
 
 
 MESH = pl.DeviceIdType.MESH
@@ -834,12 +655,699 @@
         ),
         name="first",
     )(tokens, table, wq_parts, time_table, time_index, scale_attn, scale_mlp)
-def contract_rows_precise(left, right):
-    return lax.dot_general(
-        left, right, (((0,), (0,)), ((), ())), precision=PRECISE, preferred_element_type=F32
-    )
-
-
+EXP_SCALE = SCORE_SCALE * math.log2(math.e)
+KEYS = 256
+
+
+class Everyone:
+    def __init__(self, head, blk, source, target, sems):
+        self.head, self.blk, self.source, self.target, self.sems = head, blk, source, target, sems
+
+    def copy(self, kz, k):
+        z, b = flip(self.head, kz), flip(self.blk, k)
+        return send(
+            self.source(z, b),
+            self.target(self.head, self.blk),
+            self.sems.at[0, kz, k],
+            self.sems.at[1, kz, k],
+            z,
+            b,
+        )
+
+    def start(self, kz):
+        for k in range(1 if kz == 0 else 0, 8):
+            self.copy(kz, k).start()
+
+    def arrive(self):
+        for kz in range(4):
+            for k in range(1 if kz == 0 else 0, 8):
+                self.copy(kz, k).wait_recv()
+
+    def drain(self):
+        for kz in range(4):
+            for k in range(1 if kz == 0 else 0, 8):
+                self.copy(kz, k).wait_send()
+
+
+def greet_all(head, blk):
+    barrier = pltpu.get_barrier_semaphore()
+    for kz in range(4):
+        for k in range(8):
+            if kz or k:
+                pl.semaphore_signal(
+                    barrier, inc=1, device_id=(flip(head, kz), flip(blk, k)), device_id_type=MESH
+                )
+    pl.semaphore_wait(barrier, 31)
+
+
+def group_rows(value):
+    return jnp.sum(value.reshape(value.shape[0] // 8, 8, value.shape[1]), axis=0)
+
+
+def second_kernel(
+    tiles, upp, down_own, out_own, cot_own,
+    mixed, lse, received, up, down, out, cots,
+    upz, outz, kvt, scores, att,
+    usem, lsem, dsem, osem, psem, csem, esem,
+):
+    head, blk = lax.axis_index("head"), lax.axis_index("blk")
+    greet_all(head, blk)
+    uswap = Swap(head, blk, "blk", lambda i: upp.at[i], lambda i: upz.at[i], usem)
+    uswap.start()
+    oline = Line(head, blk, out_own, lambda i: outz.at[i], osem)
+    oline.start()
+    dline = Line(head, blk, down_own, lambda i: down.at[i], dsem)
+    dline.start()
+    cplane = Plane(head, blk, cot_own, lambda i: cots.at[i], csem)
+    cplane.start()
+    upz[blk] = upp[blk]
+    outz[head] = out_own[...]
+    down[head] = down_own[...]
+    cots[blk] = cot_own[...]
+    uswap.arrive()
+    up[head] = upz[...]
+    uline = Line(head, blk, upz, lambda i: up.at[i], lsem)
+    uline.start()
+    oplane = Plane(head, blk, outz, lambda i: out.at[:, i], psem)
+    everyone = Everyone(head, blk, lambda z, b: att.at[z, b], lambda z, b: received.at[z, b], esem)
+    kvt[...] = jnp.transpose(tiles[:, :, 0:64, :].reshape(2048, 128))
+
+    def attend(z, carry):
+        packed = tiles[z, :, 64:96, :].reshape(256, 128)
+        left = half_lane((256, 128))
+        flat = packed.astype(F32)
+        results = []
+        for side in range(2):
+            query = flat if side == 0 else pltpu.roll(flat, 64, 1)
+            query = jnp.where(left, query, 0.0).astype(BF)
+            top = None
+            for c in range(2048 // KEYS):
+                keys = tiles[c // 2, 4 * (c % 2) : 4 * (c % 2) + 4, 0:64, :].reshape(KEYS, 128)
+                part = contract_cols(keys, query)
+                scores[side, c] = part
+                peak = jnp.max(part.reshape(KEYS // 8, 8, 256), axis=0)
+                top = peak if top is None else jnp.maximum(top, peak)
+            top = jnp.max(top, axis=0, keepdims=True)
+            total = jnp.zeros((8, 256), F32)
+            mix = jnp.zeros((64, 256), F32)
+            for c in range(2048 // KEYS):
+                weights = jnp.exp2((scores[side, c] - top) * EXP_SCALE)
+                total = total + group_rows(weights)
+                mix = mix + jnp.dot(
+                    kvt[64:128, KEYS * c : KEYS * c + KEYS],
+                    weights.astype(BF),
+                    preferred_element_type=F32,
+                )
+            total = jnp.sum(total, axis=0, keepdims=True)
+            mix = mix / total
+            mixed[z, 64 * side : 64 * side + 64, :] = mix
+            lse[z, side : side + 1, :] = top * SCORE_SCALE + jnp.log(total)
+            results.append(mix)
+        both = jnp.transpose(jnp.concatenate(results, axis=0))
+        att[z] = both.astype(BF).reshape(8, 32, 128)
+
+        @pl.when(z > 0)
+        def _():
+            at = line_order(head, z)
+            oline.step(at)
+            dline.step(at)
+
+        return carry
+
+    lse[...] = jnp.zeros_like(lse)
+    lax.fori_loop(0, 4, attend, 0)
+    for kz in range(4):
+        everyone.start(kz)
+    received[head, blk] = att[head, blk]
+    oplane.start()
+    out[:, pl.ds(blk, 1)] = outz[...].reshape(4, 1, 32, 1024)
+    for step in range(1, 4):
+        uline.step(line_order(head, jnp.int32(step)))
+    cplane.finish()
+    oplane.finish()
+    everyone.arrive()
+    for copies in (uswap, oline, dline, uline, cplane, oplane, everyone):
+        copies.drain()
+
+
+def phase_two_kernel(tiles, up_parts, w_down, w_out, cotangent):
+    dma = pltpu.SemaphoreType.DMA
+    return pl.pallas_call(
+        second_kernel,
+        out_shape=(
+            jax.ShapeDtypeStruct((4, 128, 256), F32),
+            jax.ShapeDtypeStruct((4, 8, 256), F32),
+            jax.ShapeDtypeStruct((4, 8, 32, 128), BF),
+            jax.ShapeDtypeStruct((4, 8, 32, 512), BF),
+            jax.ShapeDtypeStruct((4, 128, 1024), BF),
+            jax.ShapeDtypeStruct((4, 8, 32, 1024), BF),
+            jax.ShapeDtypeStruct((8, 128, 1024), BF),
+        ),
+        in_specs=whole(5),
+        out_specs=whole(7),
+        scratch_shapes=[
+            pltpu.VMEM((8, 32, 512), BF),
+            pltpu.VMEM((4, 32, 1024), BF),
+            pltpu.VMEM((128, 2048), BF),
+            pltpu.VMEM((2, 2048 // KEYS, KEYS, 256), F32),
+            pltpu.VMEM((4, 8, 32, 128), BF),
+            dma((2, 8)),
+            dma((2, 2, 3)),
+            dma((2, 2, 3)),
+            dma((2, 2, 3)),
+            dma((2, 7)),
+            dma((2, 7)),
+            dma((2, 4, 8)),
+        ],
+        compiler_params=pltpu.CompilerParams(
+            collective_id=1, has_side_effects=True, vmem_limit_bytes=56 << 20
+        ),
+        name="second",
+    )(tiles, up_parts, w_down, w_out, cotangent)
+def third_kernel(
+    received, tok, out, up, down, cots, scales,
+    grad_rx, grad_middle, middle, outq, grad_down, grad_up, grad_out, sums,
+    attended, n2g, act, gh, pairs, prx, gsend, gin, tsend, branch,
+    nsem, ssem, gsem, esem,
+):
+    head, blk = lax.axis_index("head"), lax.axis_index("blk")
+    core = lax.rem(blk, 2)
+    greet_all(head, blk)
+    for seq in range(2):
+        for group in range(4):
+            for i in range(2):
+                first = received[group, 4 * seq + 2 * i].astype(F32)
+                second = received[group, 4 * seq + 2 * i + 1].astype(F32)
+                lanes = slice(256 * group + 128 * i, 256 * group + 128 * i + 128)
+                attended[64 * seq : 64 * seq + 32, lanes] = join_halves(first, second, 0).astype(BF)
+                attended[64 * seq + 32 : 64 * seq + 64, lanes] = join_halves(
+                    first, second, 1
+                ).astype(BF)
+    middle[...] = tok[...].astype(F32) + jnp.dot(
+        attended[...], out[...].reshape(1024, 1024), preferred_element_type=F32
+    )
+    for seq in range(2):
+        rows = slice(64 * seq, 64 * seq + 64)
+        unit, _ = norm_stats(middle[rows, :])
+        n2g[blk, rows, :] = (unit * scales[2 + seq : 3 + seq, :]).astype(BF)
+    plane = Plane(head, blk, n2g.at[blk], lambda i: n2g.at[i], nsem)
+    plane.start()
+    sibling = flip(blk, 1)
+
+    def halves(i):
+        return [
+            send(pairs.at[w, i, 1 - core], prx.at[w, i], ssem.at[0, w, i], ssem.at[1, w, i], head, sibling)
+            for w in range(2)
+        ]
+
+    def onward(i):
+        peer = flip(blk, 2 * i)
+        return send(gsend.at[i], gin.at[i], gsem.at[0, i], gsem.at[1, i], head, peer)
+
+    def reduce(i):
+        chip = lax.div(flip(blk, 2 * i), 2)
+        for copy in halves(i):
+            copy.wait_recv()
+        gsend[i] = (pairs[0, i, core].astype(F32) + prx[0, i].astype(F32)).astype(BF)
+        if i:
+            onward(i).start()
+        outq[chip] = (pairs[1, i, core].astype(F32) + prx[1, i].astype(F32)).astype(BF)
+
+    for i in range(4):
+        chip = lax.div(flip(blk, 2 * i), 2)
+        if i == 0:
+            plane.arrive(-1)
+        else:
+            plane.forward(i - 1)
+            if i > 1:
+                reduce(i - 1)
+            plane.arrive(i - 1)
+        at = pl.ds(2 * chip, 2)
+        rows = n2g[at].reshape(256, 1024)
+        hidden = jnp.dot(rows, up[...].reshape(1024, 512), preferred_element_type=F32)
+        grad_active = contract_cols(cots[at].reshape(256, 1024), down[...].reshape(512, 1024))
+        cdf = 0.5 * (1.0 + lax.erf(hidden * math.sqrt(0.5)))
+        active = (hidden * cdf).astype(BF)
+        slope = cdf + hidden * jnp.exp(-0.5 * hidden * hidden) * (1.0 / math.sqrt(2 * math.pi))
+        grad_hidden = (grad_active * slope).astype(BF)
+        act[at] = active.reshape(2, 128, 512)
+        gh[at] = grad_hidden.reshape(2, 128, 512)
+        pairs[0, i] = (
+            contract_cols(grad_hidden, up[...].reshape(1024, 512)).astype(BF).reshape(2, 128, 1024)
+        )
+        pairs[1, i] = (
+            jnp.dot(active, down[...].reshape(512, 1024), preferred_element_type=F32)
+            .astype(BF)
+            .reshape(2, 128, 1024)
+        )
+        for copy in halves(i):
+            copy.start()
+    reduce(3)
+    reduce(0)
+    for group in range(4):
+        lanes = slice(128 * group, 128 * group + 128)
+        grad_down[group] = contract_rows(
+            act[:, :, lanes].reshape(1024, 128), cots[...].reshape(1024, 1024)
+        ).astype(BF)
+    for group in range(4):
+        lanes = slice(256 * group, 256 * group + 256)
+        part = contract_rows(n2g[:, :, lanes].reshape(1024, 256), gh[...].reshape(1024, 512))
+        grad_up[group] = part.astype(BF).reshape(8, 32, 512)
+    for i in range(1, 4):
+        onward(i).wait_recv()
+    sums[...] = jnp.zeros_like(sums)
+    for seq in range(2):
+        rows = slice(64 * seq, 64 * seq + 64)
+        grad = gsend[0, rows, :].astype(F32)
+        for i in range(1, 4):
+            grad = grad + gin[i, rows, :].astype(F32)
+        unit, spread = norm_stats(middle[rows, :])
+        whole_grad = cots[blk, rows, :].astype(F32) + norm_back(
+            unit, spread, grad, scales[2 + seq : 3 + seq, :]
+        )
+        grad_middle[rows, :] = whole_grad
+        branch[rows, :] = whole_grad.astype(BF)
+        sums[seq : seq + 1, :] = jnp.sum(grad * unit, axis=0, keepdims=True)
+    grad_att = contract_cols(branch[...], out[...].reshape(1024, 1024))
+    for seq in range(2):
+        for group in range(4):
+            for i in range(2):
+                lanes = slice(256 * group + 128 * i, 256 * group + 128 * i + 128)
+                top = grad_att[64 * seq : 64 * seq + 32, lanes]
+                bottom = grad_att[64 * seq + 32 : 64 * seq + 64, lanes]
+                for right in range(2):
+                    tsend[group, 4 * seq + 2 * i + right] = join_halves(top, bottom, right).astype(BF)
+    everyone = Everyone(head, blk, lambda z, b: tsend.at[z, b], lambda z, b: grad_rx.at[z, b], esem)
+    for kz in range(4):
+        everyone.start(kz)
+    grad_rx[head, blk] = tsend[head, blk]
+    for group in range(4):
+        lanes = slice(256 * group, 256 * group + 256)
+        part = contract_rows(attended[:, lanes], branch[...])
+        grad_out[group] = part.astype(BF).reshape(8, 32, 1024)
+    everyone.arrive()
+    plane.drain()
+    for i in range(4):
+        for copy in halves(i):
+            copy.wait_send()
+        if i:
+            onward(i).wait_send()
+    everyone.drain()
+
+
+def phase_three_kernel(received, tokens, out, up, down, cots, scales):
+    dma = pltpu.SemaphoreType.DMA
+    return pl.pallas_call(
+        third_kernel,
+        out_shape=(
+            jax.ShapeDtypeStruct((4, 8, 32, 128), BF),
+            jax.ShapeDtypeStruct((128, 1024), F32),
+            jax.ShapeDtypeStruct((128, 1024), F32),
+            jax.ShapeDtypeStruct((4, 128, 1024), BF),
+            jax.ShapeDtypeStruct((4, 128, 1024), BF),
+            jax.ShapeDtypeStruct((4, 8, 32, 512), BF),
+            jax.ShapeDtypeStruct((4, 8, 32, 1024), BF),
+            jax.ShapeDtypeStruct((8, 1024), F32),
+        ),
+        in_specs=whole(7),
+        out_specs=whole(8),
+        scratch_shapes=[
+            pltpu.VMEM((128, 1024), BF),
+            pltpu.VMEM((8, 128, 1024), BF),
+            pltpu.VMEM((8, 128, 512), BF),
+            pltpu.VMEM((8, 128, 512), BF),
+            pltpu.VMEM((2, 4, 2, 128, 1024), BF),
+            pltpu.VMEM((2, 4, 128, 1024), BF),
+            pltpu.VMEM((4, 128, 1024), BF),
+            pltpu.VMEM((4, 128, 1024), BF),
+            pltpu.VMEM((4, 8, 32, 128), BF),
+            pltpu.VMEM((128, 1024), BF),
+            dma((2, 7)),
+            dma((2, 2, 4)),
+            dma((2, 4)),
+            dma((2, 4, 8)),
+        ],
+        compiler_params=pltpu.CompilerParams(
+            collective_id=2, has_side_effects=True, vmem_limit_bytes=58 << 20
+        ),
+        name="third",
+    )(received, tokens, out, up, down, cots, scales)
+class Scatter:
+    def __init__(self, head, blk, terms, near, joined, far, sems):
+        self.head, self.blk, self.core = head, blk, lax.rem(blk, 2)
+        self.terms, self.near, self.joined, self.far, self.sems = terms, near, joined, far, sems
+
+    def halves(self):
+        return send(
+            self.terms.at[:, :, 1 - self.core],
+            self.near,
+            self.sems.at[0, 0],
+            self.sems.at[1, 0],
+            self.head,
+            flip(self.blk, 1),
+        )
+
+    def chips(self, i):
+        peer = flip(self.blk, 2 * i)
+        return send(
+            self.joined.at[lax.div(peer, 2)],
+            self.far.at[i],
+            self.sems.at[0, i],
+            self.sems.at[1, i],
+            self.head,
+            peer,
+        )
+
+    def start(self):
+        self.halves().start()
+
+    def join(self):
+        self.halves().wait_recv()
+        for chip in range(4):
+            mine = self.terms[:, chip, pl.ds(self.core, 1)].astype(F32)
+            mine = mine.reshape(mine.shape[0], *mine.shape[2:])
+            self.joined[chip] = (mine + self.near[:, chip].astype(F32)).astype(BF)
+        for i in (3, 1, 2):
+            self.chips(i).start()
+
+    def total(self):
+        value = self.joined[lax.div(self.blk, 2)].astype(F32)
+        for i in range(1, 4):
+            self.chips(i).wait_recv()
+            value = value + self.far[i].astype(F32)
+        return value
+
+    def drain(self):
+        self.halves().wait_send()
+        for i in range(1, 4):
+            self.chips(i).wait_send()
+
+
+def sum_four(parts):
+    return (parts[0].astype(F32) + parts[1].astype(F32)) + (
+        parts[2].astype(F32) + parts[3].astype(F32)
+    )
+
+
+def fourth_kernel(
+    tiles, grad_rx, mixed, lse, outq, middle, grad_down, grad_up, grad_out,
+    back, output, down_own, up_own, out_own,
+    queries, grads, stats, keyt, dkv, dqt, bsend, oin, din, uin, usum, near, joined, far, osum, zin,
+    qsem, dsem, usem, vsem, osem, xsem, bsem,
+):
+    head, blk = lax.axis_index("head"), lax.axis_index("blk")
+    greet(head, blk, (1, 2, 3), range(1, 8))
+    dswap = Swap(head, blk, "head", lambda i: grad_down.at[i], lambda i: din.at[i], dsem)
+    dswap.start()
+    scatter = Scatter(head, blk, grad_out, near, joined, far, osem)
+    scatter.start()
+    uswap = Swap(head, blk, "head", lambda i: grad_up.at[i], lambda i: uin.at[i], usem)
+    uswap.start()
+    outs = []
+    for i in range(1, 4):
+        peer = flip(blk, 2 * i)
+        outs.append(
+            send(outq.at[lax.div(peer, 2)], oin.at[i], qsem.at[0, i], qsem.at[1, i], head, peer)
+        )
+        outs[-1].start()
+    vswap = Swap(head, blk, "blk", lambda i: usum.at[i], lambda i: up_own.at[i], vsem)
+    xswap = Swap(head, blk, "head", lambda i: osum.at[i], lambda i: zin.at[i], xsem)
+    left = half_lane((256, 128))
+    keyt[...] = jnp.transpose(tiles[:, :, 0:64, :].reshape(2048, 128))[:64]
+
+    def prepare(z, carry):
+        flat = tiles[z, :, 64:96, :].reshape(256, 128).astype(F32)
+        grad = grad_rx[z].reshape(256, 128).astype(F32)
+        product = jnp.transpose(grad) * mixed[z]
+        queries[2 * z] = jnp.where(left, flat, 0.0).astype(BF)
+        queries[2 * z + 1] = jnp.where(left, pltpu.roll(flat, 64, 1), 0.0).astype(BF)
+        grads[2 * z] = jnp.where(left, 0.0, pltpu.roll(grad, 64, 1)).astype(BF)
+        grads[2 * z + 1] = jnp.where(left, 0.0, grad).astype(BF)
+        for side in range(2):
+            delta = jnp.sum(product[64 * side : 64 * side + 64], axis=0, keepdims=True)
+            shift = lse[z, side : side + 1, :] * math.log2(math.e)
+            stats[2 * z + side] = jnp.concatenate([shift, delta, jnp.zeros((6, 256), F32)], axis=0)
+        return carry
+
+    lax.fori_loop(0, 4, prepare, 0)
+    dqt[...] = jnp.zeros_like(dqt)
+
+    def kv_move(z):
+        return Swap(
+            head,
+            blk,
+            "blk",
+            lambda i: bsend.at[i, z, pl.ds(0, 64)],
+            lambda i: back.at[i, z, pl.ds(0, 64)],
+            bsem.at[z],
+        )
+
+    def keys_step(z, carry):
+        dkv[...] = jnp.zeros_like(dkv)
+
+        def query_step(q, inner):
+            query, grad = queries[q], grads[q]
+            shift, delta = stats[q, 0:1, :], stats[q, 1:2, :]
+            dq = dqt[q]
+            for c in range(2):
+                keys = tiles[z, 4 * c : 4 * c + 4, 0:64, :].reshape(256, 128)
+                probs = jnp.exp2(contract_cols(keys, query) * EXP_SCALE - shift)
+                slopes = (probs * (contract_cols(keys, grad) - delta)).astype(BF)
+                dkv[c] += jnp.dot(slopes, query, preferred_element_type=F32) + jnp.dot(
+                    probs.astype(BF), grad, preferred_element_type=F32
+                )
+                at = pl.ds(pl.multiple_of(512 * z + 256 * c, 256), 256)
+                dq = dq + jnp.dot(keyt[:, at], slopes, preferred_element_type=F32)
+            dqt[q] = dq
+            return inner
+
+        lax.fori_loop(0, 8, query_step, 0)
+        scale = jnp.where(left, SCORE_SCALE, 1.0)
+        for c in range(2):
+            bsend[4 * c : 4 * c + 4, pl.ds(z, 1), 0:64, :] = (
+                (dkv[c] * scale).astype(BF).reshape(4, 1, 64, 128)
+            )
+        kv_move(z).start()
+
+        @pl.when(z == 0)
+        def _():
+            scatter.join()
+
+        @pl.when(z == 2)
+        def _():
+            total = middle[...] + outq[lax.div(blk, 2)].astype(F32)
+            for i in range(1, 4):
+                outs[i - 1].wait_recv()
+                total = total + oin[i].astype(F32)
+            output[...] = total.astype(BF)
+            osum[...] = scatter.total().astype(BF)
+            xswap.start()
+            zin[head] = osum[head]
+
+        return carry
+
+    lax.fori_loop(0, 4, keys_step, 0)
+    for z in range(4):
+        both = jnp.concatenate([dqt[2 * z], dqt[2 * z + 1]], axis=0)
+        both = (jnp.transpose(both) * SCORE_SCALE).astype(BF)
+        bsend[:, z, 64:96, :] = both.reshape(8, 32, 128)
+    qmove = Swap(
+        head,
+        blk,
+        "blk",
+        lambda i: bsend.at[i, :, pl.ds(64, 32)],
+        lambda i: back.at[i, :, pl.ds(64, 32)],
+        bsem.at[4],
+    )
+    qmove.start()
+    back[blk] = bsend[blk]
+    uswap.arrive()
+    uin[head] = grad_up[head]
+    usum[...] = sum_four(uin).astype(BF)
+    vswap.start()
+    up_own[blk] = usum[blk]
+    dswap.arrive()
+    din[head] = grad_down[head]
+    down_own[...] = sum_four(din)
+    xswap.arrive()
+    out_own[...] = sum_four(zin)
+    vswap.arrive()
+    for z in range(4):
+        kv_move(z).arrive()
+    qmove.arrive()
+    for z in range(4):
+        kv_move(z).drain()
+    for copy in outs:
+        copy.wait_send()
+    for copies in (dswap, scatter, uswap, vswap, xswap, qmove):
+        copies.drain()
+
+
+def phase_four_kernel(tiles, grad_rx, mixed, lse, outq, middle, grad_down, grad_up, grad_out):
+    dma = pltpu.SemaphoreType.DMA
+    return pl.pallas_call(
+        fourth_kernel,
+        out_shape=(
+            jax.ShapeDtypeStruct((8, 4, 96, 128), BF),
+            jax.ShapeDtypeStruct((128, 1024), BF),
+            jax.ShapeDtypeStruct((128, 1024), F32),
+            jax.ShapeDtypeStruct((8, 32, 512), BF),
+            jax.ShapeDtypeStruct((32, 1024), F32),
+        ),
+        in_specs=whole(9),
+        out_specs=whole(5),
+        scratch_shapes=[
+            pltpu.VMEM((8, 256, 128), BF),
+            pltpu.VMEM((8, 256, 128), BF),
+            pltpu.VMEM((8, 8, 256), F32),
+            pltpu.VMEM((64, 2048), BF),
+            pltpu.VMEM((2, 256, 128), F32),
+            pltpu.VMEM((8, 64, 256), F32),
+            pltpu.VMEM((8, 4, 96, 128), BF),
+            pltpu.VMEM((4, 128, 1024), BF),
+            pltpu.VMEM((4, 128, 1024), BF),
+            pltpu.VMEM((4, 8, 32, 512), BF),
+            pltpu.VMEM((8, 32, 512), BF),
+            pltpu.VMEM((4, 4, 32, 1024), BF),
+            pltpu.VMEM((4, 4, 32, 1024), BF),
+            pltpu.VMEM((4, 4, 32, 1024), BF),
+            pltpu.VMEM((4, 32, 1024), BF),
+            pltpu.VMEM((4, 32, 1024), BF),
+            dma((2, 4)),
+            dma((2, 4)),
+            dma((2, 4)),
+            dma((2, 8)),
+            dma((2, 4)),
+            dma((2, 4)),
+            dma((5, 2, 8)),
+        ],
+        compiler_params=pltpu.CompilerParams(
+            collective_id=3, has_side_effects=True, vmem_limit_bytes=56 << 20
+        ),
+        name="fourth",
+    )(tiles, grad_rx, mixed, lse, outq, middle, grad_down, grad_up, grad_out)
+def fifth_kernel(
+    back, tabg, normed, wq, tok, scales, grad_middle, sums, ttab, tix,
+    grad_tokens, gq, grad_attn, grad_mlp,
+    gp, gnp, gin, terms, near, joined, far, osum, turned, part, sums_in, parts,
+    gsem, osem, xsem, asem, bsem,
+):
+    head, blk = lax.axis_index("head"), lax.axis_index("blk")
+    greet(head, blk, (1, 2, 3), range(1, 8))
+    gswap = Swap(head, blk, "head", lambda i: gnp.at[i], lambda i: gin.at[i], gsem)
+
+    def unturn(step, carry):
+        at = flip(head, step)
+        for seq in range(2):
+            table = tabg[at]
+            if seq:
+                table = pltpu.roll(table, 64, 1)
+            both, keyed = turn_tables(table, -1.0)
+            rows = slice(64 * seq, 64 * seq + 64)
+            for j in range(4):
+                kv = back[4 * seq + j, at, 0:64, :].astype(F32)
+                kv = kv * keyed[0] + lane_swap(kv) * keyed[1]
+                gp[at, rows, 128 * j : 128 * j + 128] = kv.astype(BF)
+            for i in range(2):
+                first = back[4 * seq + 2 * i, at, 64:96, :].astype(F32)
+                second = back[4 * seq + 2 * i + 1, at, 64:96, :].astype(F32)
+                query = jnp.concatenate(
+                    [join_halves(first, second, 0), join_halves(first, second, 1)], axis=0
+                )
+                query = query * both[0] + lane_swap(query) * both[1]
+                gp[at, rows, 512 + 128 * i : 640 + 128 * i] = query.astype(BF)
+        gnp[at] = contract_cols(gp[at], wq[...].reshape(1024, 768)).astype(BF)
+        return carry
+
+    for step in (3, 2, 1, 0):
+        unturn(step, 0)
+        if step:
+            gswap.copies[step - 1].start()
+    for group in range(4):
+        lanes = slice(256 * group, 256 * group + 256)
+        value = contract_rows(normed[:, :, lanes].reshape(512, 256), gp[...].reshape(512, 768))
+        terms[group] = value.astype(BF).reshape(4, 2, 32, 768)
+    scatter = Scatter(head, blk, terms, near, joined, far, osem)
+    scatter.start()
+    turned[...] = jnp.transpose(ttab[...])
+    picked = turned[pl.ds(pl.multiple_of((head * 8 + blk) * 8, 8), 8), :]
+    step_lane = lax.broadcasted_iota(jnp.int32, picked.shape, 1)
+    columns = [
+        jnp.sum(jnp.where(step_lane == tix[seq], picked, 0.0), axis=1, keepdims=True)
+        for seq in range(2)
+    ]
+    scatter.join()
+    osum[...] = scatter.total().astype(BF)
+    xswap = Swap(head, blk, "head", lambda i: osum.at[i], lambda i: gq.at[i], xsem)
+    xswap.start()
+    gq[head] = osum[head]
+    gswap.arrive()
+    gin[head] = gnp[head]
+    firsts = []
+    for seq in range(2):
+        rows = slice(64 * seq, 64 * seq + 64)
+        grad = sum_four([gin[i, rows, :] for i in range(4)])
+        unit, spread = norm_stats(tok[rows, :].astype(F32))
+        grad_tokens[rows, :] = grad_middle[rows, :] + norm_back(
+            unit, spread, grad, scales[seq : seq + 1, :]
+        )
+        firsts.append(jnp.sum(grad * unit, axis=0, keepdims=True))
+    part[...] = jnp.concatenate(firsts + [sums[0:2, :], jnp.zeros((4, 1024), F32)], axis=0)
+    one = Swap(head, blk, "blk", lambda i: part, lambda i: sums_in.at[i], asem)
+    one.start()
+    sums_in[blk] = part[...]
+    one.arrive()
+    total = sums_in[0]
+    for i in range(1, 8):
+        total = total + sums_in[i]
+    parts[head] = total
+    two = Swap(head, blk, "head", lambda i: parts.at[head], lambda i: parts.at[i], bsem)
+    two.start()
+    two.arrive()
+    total = (parts[0] + parts[1]) + (parts[2] + parts[3])
+    grad_attn[...] = columns[0] * total[0:1] + columns[1] * total[1:2]
+    grad_mlp[...] = columns[0] * total[2:3] + columns[1] * total[3:4]
+    xswap.arrive()
+    for copies in (gswap, scatter, xswap, one, two):
+        copies.drain()
+
+
+def phase_five_kernel(back, tabg, normed, wq, tok, scales, grad_middle, sums, ttab, tix):
+    dma = pltpu.SemaphoreType.DMA
+    return pl.pallas_call(
+        fifth_kernel,
+        out_shape=(
+            jax.ShapeDtypeStruct((128, 1024), F32),
+            jax.ShapeDtypeStruct((4, 32, 768), BF),
+            jax.ShapeDtypeStruct((8, 1024), F32),
+            jax.ShapeDtypeStruct((8, 1024), F32),
+        ),
+        in_specs=whole(9) + [pl.BlockSpec(memory_space=pltpu.SMEM)],
+        out_specs=whole(4),
+        scratch_shapes=[
+            pltpu.VMEM((4, 128, 768), BF),
+            pltpu.VMEM((4, 128, 1024), BF),
+            pltpu.VMEM((4, 128, 1024), BF),
+            pltpu.VMEM((4, 4, 2, 32, 768), BF),
+            pltpu.VMEM((4, 4, 32, 768), BF),
+            pltpu.VMEM((4, 4, 32, 768), BF),
+            pltpu.VMEM((4, 4, 32, 768), BF),
+            pltpu.VMEM((4, 32, 768), BF),
+            pltpu.VMEM((256, 64), F32),
+            pltpu.VMEM((8, 1024), F32),
+            pltpu.VMEM((8, 8, 1024), F32),
+            pltpu.VMEM((4, 8, 1024), F32),
+            dma((2, 4)),
+            dma((2, 4)),
+            dma((2, 4)),
+            dma((2, 8)),
+            dma((2, 4)),
+        ],
+        compiler_params=pltpu.CompilerParams(
+            collective_id=4, has_side_effects=True, vmem_limit_bytes=48 << 20
+        ),
+        name="fifth",
+    )(back, tabg, normed, wq, tok, scales, grad_middle, sums, ttab, tix)
 def blocked(
     tokens,
     positions,
@@ -853,9 +1361,6 @@
     scale_mlp,
     cotangent,
 ):
-    place = lax.axis_index(("head", "blk"))
-    embed = time_table[time_index]
-    embed_own = lax.dynamic_slice_in_dim(embed, place * 8, 8, 1)
     cosine, sine = rotary_tables(positions, HEAD_DIM)
     cosine, sine = cosine[:, :, 0], sine[:, :, 0]
     table = jnp.concatenate([cosine[0], sine[0], cosine[1], sine[1]], axis=-1)
@@ -864,31 +1369,56 @@
     wq_parts = jnp.concatenate([kv_cols, wide[:, 0].reshape(32, 4, 256)], axis=-1)
     wq_parts = jnp.swapaxes(wq_parts, 0, 1)
     up_parts = jnp.transpose(w_up.reshape(32, 4, 8, 128), (2, 0, 1, 3)).reshape(8, 32, 512)
+    flat_tokens = tokens.reshape(128, 1024)
     tiles, normed, wq, scales, table_all = phase_one_kernel(
         tokens, table, wq_parts, time_table, time_index, scale_attn, scale_mlp
     )
-    mixed, lse, received, up, down, out, cot_all = phase_two(
-        tiles, up_parts, w_down, w_out, cotangent
-    )
-    grad_rx, grad_middle, middle, out_partial, grad_down, grad_up, grad_out, sums = phase_three(
-        received, tokens, out, up, down, cot_all, scales
-    )
-    back, output, down_own, up_own, out_own = phase_four(
-        tiles, grad_rx, mixed, lse, out_partial, middle, grad_down, grad_up, grad_out
-    )
-    grad_tokens, grad_wq, total = phase_five(
-        back, table_all, normed, wq, tokens, scales, grad_middle, sums
+    mixed, lse, received, up, down, out, cot_all = phase_two_kernel(
+        tiles, up_parts, w_down, w_out, cotangent.reshape(128, 1024)
+    )
+    grad_rx, grad_middle, middle, outq, grad_down, grad_up, grad_out, sums = phase_three_kernel(
+        received, flat_tokens, out, up, down, cot_all, scales
+    )
+    back, output, down_own, up_own, out_own = phase_four_kernel(
+        tiles,
+        grad_rx,
+        mixed,
+        lse,
+        outq,
+        middle,
+        grad_down,
+        grad_up,
+        grad_out.reshape(4, 4, 2, 32, 1024),
+    )
+    grad_tokens, grad_wq, grad_attn, grad_mlp = phase_five_kernel(
+        back,
+        table_all,
+        normed,
+        wq,
+        flat_tokens,
+        scales,
+        grad_middle,
+        sums,
+        time_table,
+        time_index,
     )
     kv_cols = grad_wq[:, :, :512].reshape(4, 32, 4, 2, 64)
     wide = jnp.stack(
         [grad_wq[:, :, 512:].reshape(4, 32, 4, 64), kv_cols[:, :, :, 0], kv_cols[:, :, :, 1]],
         axis=0,
     )
-    qkv_own = jnp.transpose(wide, (2, 0, 1, 3, 4)).reshape(32, 3072)
-    up_own = jnp.transpose(up_own.reshape(8, 32, 4, 128), (1, 2, 0, 3)).reshape(32, 4096).astype(F32)
-    grad_attn = contract_rows_precise(embed_own, total[:2])
-    grad_mlp = contract_rows_precise(embed_own, total[2:])
-    return output, grad_tokens, qkv_own, out_own, up_own, down_own, grad_attn, grad_mlp
+    qkv_own = jnp.transpose(wide, (2, 0, 1, 3, 4)).reshape(32, 3072).astype(F32)
+    up_own = jnp.transpose(up_own.reshape(8, 32, 4, 128), (1, 2, 0, 3)).reshape(32, 4096)
+    return (
+        output.reshape(2, 64, 1024),
+        grad_tokens.reshape(2, 64, 1024),
+        qkv_own,
+        out_own,
+        up_own.astype(F32),
+        down_own,
+        grad_attn,
+        grad_mlp,
+    )
 
 
 def solution(mesh):

time: 569 us -> 278 us (0.49); the launches traced: 558 us -> 278 us
  waiting for transfers between devices: 212 us -> 0 us
  Pallas kernels: 55.2 us -> 262 us
  matrix products: 75.8 us -> 0 us
  starting transfers between devices: 58.3 us -> 0 us
  other arithmetic: 54.6 us -> 1.33 us
  blocking collectives: 42.2 us -> 0 us
  local copies, waits for them, and re-layouts: 45.2 us -> 13.4 us
  between operations: 14.9 us -> 1.04 us
    pallas_call x0 -> x4, Pallas kernels: none -> 213 us  [the longest x1 59.9 us: phase_four_kernel(): pl.pallas_call(fourth_kernel, out_shape=(jax.ShapeDtypeStruct((8, 4, 96,...]
    all_to_all x14 -> x0, waiting for transfers between devices: 113 us -> none  [the longest x2 36.5 us: scatter_blk(): parts = lax.all_to_all(partial, 'blk', 0, 0, tiled=True)]
    all_gather x5 -> x0, waiting for transfers between devices: 96.5 us -> none  [the longest x1 29.9 us: phase_three(): normed_all = lax.all_gather(normed_two, 'blk', axis=0, tiled=True)]
    dot_general x19 -> x0, matrix products: 75.8 us -> none  [the longest x6 27.9 us: contract_cols(): lax.dot_general(left, right, (((1,), (1,)), ((), ())), preferred_element_...]
    all_to_all x14 -> x0, starting transfers between devices: 57.8 us -> none  [the longest x2 8.72 us: scatter_blk(): parts = lax.all_to_all(partial, 'blk', 0, 0, tiled=True)]
    psum x1 -> x0, blocking collectives: 42.2 us -> none  [phase_five(): total = lax.psum(jnp.concatenate([first, sums], axis=0), ('head', 'blk'))]
    reduce_sum x17 -> x0, other arithmetic: 26.6 us -> none  [the longest x5 11.2 us: sum_parts(): return jnp.sum(parts.astype(F32), axis=0)]
    reshape x12 -> x0, local copies, waits for them, and re-layouts: 15.9 us -> none  [the longest x2 3.7 us: phase_four(): grad = unpack_half(grad_rx).reshape(2048, 64)]
  transfers between devices with their start and end apart: 19 -> 0, of which waited for: 16 -> 0; matrix products, arithmetic and copies ran while one was open for 28% -> 0% of each run, Pallas kernels for 10% -> 0%
where the time goes in v3:
time: 278 us
  Pallas kernels  262 us (94%)
  local copies, waits for them, and re-layouts  13.4 us (5%)
    pallas_call x1, Pallas kernels, phase_four_kernel(): pl.pallas_call(fourth_kernel, out_shape=(jax.ShapeDtypeStruct((8, 4, 96,...  59.9 us
    pallas_call x1, Pallas kernels, phase_two_kernel(): pl.pallas_call(second_kernel, out_shape=(jax.ShapeDtypeStruct((4, 128, 25...  57.2 us
    pallas_call x1, Pallas kernels, phase_three_kernel(): pl.pallas_call(third_kernel, out_shape=(jax.ShapeDtypeStruct((4, 8, 32, 1...  53.4 us
    pallas_call x1, Pallas kernels, phase_one_kernel(): pl.pallas_call(first_kernel, out_shape=(jax.ShapeDtypeStruct((4, 8, 96, 1...  48.4 us
    pallas_call x1, Pallas kernels, phase_five_kernel(): pl.pallas_call(fifth_kernel, out_shape=(jax.ShapeDtypeStruct((128, 1024),...  42.9 us
    unnamed x44, local copies, waits for them, and re-layouts  8.41 us

profile of v3, /device:TPU:0, one launch (start us, length us, event | category | flops | bytes accessed | tf_op | source)
XLA Modules:
  0.0 277.5 jit_solution(7720828337643665800)
XLA Ops:
  0.6 0.0 copy-start.15
  0.7 0.7 convert_element_type.24
  1.4 0.3 multiply_cosine_fusion
  1.7 0.1 pad_maximum_fusion.1.tab
  1.8 1.0 copy.46
  2.8 0.1 copy.55
  2.9 0.8 reshape.89.upp
  3.7 0.0 copy-done.15
  3.7 0.0 copy-start.1
  3.7 0.0 copy-start.5
  3.7 0.0 copy-start.10
  3.7 0.0 copy-start.11
  3.8 0.3 reshape.86
  4.0 0.1 fusion
  4.2 0.1 copy_bitcast_fusion.4
  4.3 0.1 pad_maximum_fusion
  4.3 0.2 copy.35
  4.5 0.2 reshape.87
  4.7 0.2 reshape.99
  4.9 0.0 copy-done.1
  5.0 0.0 copy-done.5
  5.0 0.0 copy-done.9
  5.0 0.0 copy-done.10
  5.0 0.0 copy-done.11
  5.0 48.4 %first.1 = (bf16[4,8,96,128]{3,2,1,0:T(8,128)(2,1)S(1)}, bf16[4,128,1024]{2,1,0:T(8,128)(2,1)S(1)}, bf16[4,8,32,768]{3,2,1,0:T(8,128)(2,1)S(1)}, f32[8,1024]{1,0:T(8,128)S(1)}, f32[4,64,128]{2,1,0:T(8,128)S(1)}) custom-call(bf16[2,64,1024]{2,1,0:T(8,128)(2,1)S(1)} %copy-done.1, f32[64,128]{1,0:T(8,128)S(1)} %pad_maximum_fusion.1.tab, ...), custom_call_target="tpu_custom_call" | custom-call | tf_op jit(solution)/shard_map/first/pallas_call | solution.py:626
  53.4 0.0 copy-start
  53.4 0.9 copy-done
  54.3 57.2 %second.1 = (f32[4,128,256]{2,1,0:T(8,128)}, f32[4,8,256]{2,1,0:T(8,128)}, bf16[4,8,32,128]{3,2,1,0:T(8,128)(2,1)}, bf16[4,8,32,512]{3,2,1,0:T(8,128)(2,1)}, bf1...) custom-call(bf16[4,8,96,128]{3,2,1,0:T(8,128)(2,1)} %copy-done, ...), custom_call_target="tpu_custom_call" | custom-call | tf_op jit(solution)/shard_map/second/pallas_call | solution.py:795
  111.5 0.0 copy-done.6
  111.5 53.4 %third.1 = (bf16[4,8,32,128]{3,2,1,0:T(8,128)(2,1)}, f32[128,1024]{1,0:T(8,128)}, f32[128,1024]{1,0:T(8,128)}, bf16[4,128,1024]{2,1,0:T(8,128)(2,1)}, bf16[4,128...) custom-call(bf16[4,8,32,128]{3,2,1,0:T(8,128)(2,1)} %get-tuple-eleme, ...), custom_call_target="tpu_custom_call" | custom-call | tf_op jit(solution)/shard_map/third/pallas_call | solution.py:960
  164.9 0.0 copy-start.2
  164.9 0.0 copy-start.4
  164.9 0.0 copy-start.7
  164.9 0.0 copy-start.8
  164.9 59.9 %fourth.1 = (bf16[8,4,96,128]{3,2,1,0:T(8,128)(2,1)}, bf16[128,1024]{1,0:T(8,128)(2,1)}, f32[128,1024]{1,0:T(8,128)}, bf16[8,32,512]{2,1,0:T(8,128)(2,1)}, f32[32,1024]{1,0:T(8,128)}) custom-call(bf16[4,8,96,128]{3,2,1,0:T(8,128)(2,1)} %copy-done, bf16[4,8,32,128]{3,2,1,0:T(8,128)(2,1)} %get-tuple-element.44.grad_rx, ...), custom_call_target="tpu_custom_call" | custom-call | tf_op jit(solution)/shard_map/fourth/pallas_call | solution.py:1188
  224.8 0.0 copy-done.2
  224.8 0.0 copy-done.4
  224.8 0.0 copy-done.7
  224.8 0.0 copy-done.8
  224.8 0.0 copy-start.3
  224.8 1.1 copy-done.3
  226.0 42.9 %fifth.1 = (f32[128,1024]{1,0:T(8,128)S(1)}, bf16[4,32,768]{2,1,0:T(8,128)(2,1)S(1)}, f32[8,1024]{1,0:T(8,128)S(1)}, f32[8,1024]{1,0:T(8,128)S(1)}) custom-call(bf16[8,4,96,128]{3,2,1,0:T(8,128)(2,1)S(1)} %copy-done.3, f32[4,64,128]{2,1,0:T(8,128)S(1)} %get-tuple-element.54.tabg, bf16[4,128,1024]{2,1,0:T(8,128)(2,1)S(1)} %get-tuple-element.55.normed, ...), custom_call_target="tpu_custom_call" | custom-call | tf_op jit(solution)/shard_map/fifth/pallas_call | solution.py:1317
  268.9 0.1 stack_reshape.3
  269.1 0.2 reshape.95
  269.3 0.4 fusion.1
  269.7 0.0 copy-start.13
  269.7 0.1 convert_bitcast_fusion
  269.9 0.5 copy.41
  270.4 0.0 copy-start.14
  270.4 1.3 reshape.96
  271.7 0.0 copy-done.13
  271.7 0.2 reshape.98
  271.9 0.0 copy-start.12
  271.9 0.3 copy.42
  272.2 1.1 copy.54
  273.3 0.0 copy-done.14
  273.3 0.7 copy.64
  274.0 0.8 copy.65
  274.8 0.0 copy-done.16
  274.8 0.7 copy.66
  275.5 0.0 copy-done.12
  275.5 0.8 copy.67
  276.3 0.6 copy.68
  276.9 0.6 copy.69
  (12 shorter events, 0.1 us)
Async XLA Ops:
  0.6 3.1 %copy-start.15 = (bf16[32,3072]{1,0:T(8,128)(2,1)S(1)}, bf16[32,3072]{1,0:T(8,128)(2,1)}, u32[]{:S(2)}) copy-start(bf16[32,3072]{1,0:T(8,128)(2,1)} %param.15) | copy-start | bytes 589828
  3.7 1.2 copy-start.1
  3.7 1.2 copy-start.5
  3.7 1.2 copy-start.9
  3.7 1.2 copy-start.10
  3.7 1.2 copy-start.11
  53.4 0.9 copy-start
  54.3 57.2 %copy-start.6 = (f32[8,1024]{1,0:T(8,128)}, f32[8,1024]{1,0:T(8,128)S(1)}, u32[]{:S(2)}) copy-start(f32[8,1024]{1,0:T(8,128)S(1)} %get-tuple-element.43.scales) | copy-start | bytes 98308
  164.9 59.9 %copy-start.2 = (bf16[2,64,1024]{2,1,0:T(8,128)(2,1)S(1)}, bf16[2,64,1024]{2,1,0:T(8,128)(2,1)}, u32[]{:S(2)}) copy-start(bf16[2,64,1024]{2,1,0:T(8,128)(2,1)} %tok.1) | copy-start | bytes 786436
  164.9 59.9 %copy-start.4 = (f32[128,1024]{1,0:T(8,128)S(1)}, f32[128,1024]{1,0:T(8,128)}, u32[]{:S(2)}) copy-start(f32[128,1024]{1,0:T(8,128)} %get-tuple-element.57.grad_middle) | copy-start | bytes 1572868
  164.9 59.9 %copy-start.7 = (f32[8,1024]{1,0:T(8,128)S(1)}, f32[8,1024]{1,0:T(8,128)}, u32[]{:S(2)}) copy-start(f32[8,1024]{1,0:T(8,128)} %copy-done.6) | copy-start | bytes 98308
  164.9 59.9 %copy-start.8 = (f32[8,1024]{1,0:T(8,128)S(1)}, f32[8,1024]{1,0:T(8,128)}, u32[]{:S(2)}) copy-start(f32[8,1024]{1,0:T(8,128)} %get-tuple-element.58.sums) | copy-start | bytes 98308
  224.8 1.1 copy-start.3
  269.7 2.0 copy-start.13
  270.4 2.9 %copy-start.14 = (bf16[128,1024]{1,0:T(8,128)(2,1)S(1)}, bf16[128,1024]{1,0:T(8,128)(2,1)}, u32[]{:S(2)}) copy-start(bf16[128,1024]{1,0:T(8,128)(2,1)} %get-tuple-element.52) | copy-start | bytes 786436
  271.7 3.1 %copy-start.16 = (f32[32,1024]{1,0:T(8,128)S(1)}, f32[32,1024]{1,0:T(8,128)}, u32[]{:S(2)}) copy-start(f32[32,1024]{1,0:T(8,128)} %get-tuple-element.92) | copy-start | bytes 393220
  271.9 3.6 %copy-start.12 = (f32[128,1024]{1,0:T(8,128)S(1)}, f32[128,1024]{1,0:T(8,128)}, u32[]{:S(2)}) copy-start(f32[128,1024]{1,0:T(8,128)} %get-tuple-element.94) | copy-start | bytes 1572868

commit v4 on v3

--- a/solution.py
+++ b/solution.py
@@ -490,6 +490,148 @@
                 self.copy(self.own, head, False, k).wait_send()
 
 
+class Reach:
+    def __init__(self, head, blk, own, slot, sems):
+        self.head, self.blk, self.own, self.slot, self.sems = head, blk, own, slot, sems
+        self.middle = jnp.logical_and(head > 0, head < 3)
+
+    def copy(self, k):
+        peer = flip(self.head, k)
+        return send(
+            self.own, self.slot(self.head), self.sems.at[0, k], self.sems.at[1, k], peer, self.blk
+        )
+
+    def passed(self):
+        at = self.slot(flip(self.head, 2))
+        return send(at, at, self.sems.at[0, 0], self.sems.at[1, 3], flip(self.head, 1), self.blk)
+
+    def start(self):
+        self.copy(2).start()
+        self.copy(1).start()
+
+        @pl.when(self.middle)
+        def _():
+            self.copy(3).start()
+
+    def forward(self):
+        self.copy(2).wait_recv()
+
+        @pl.when(self.middle)
+        def _():
+            self.passed().start()
+
+    def arrive(self):
+        self.copy(1).wait_recv()
+        self.copy(3).wait_recv()
+
+    def drain(self):
+        self.copy(1).wait_send()
+        self.copy(2).wait_send()
+
+        @pl.when(self.middle)
+        def _():
+            self.copy(3).wait_send()
+            self.passed().wait_send()
+
+
+class Fold:
+    def __init__(self, head, blk, terms, via, joined, into, sems):
+        self.head, self.blk, self.sems = head, blk, sems
+        self.terms, self.via, self.joined, self.into = terms, via, joined, into
+        self.middle = jnp.logical_and(head > 0, head < 3)
+
+    def copy(self, k):
+        peer = flip(self.head, k)
+        return send(
+            self.terms.at[peer],
+            self.into.at[k],
+            self.sems.at[0, k],
+            self.sems.at[1, k],
+            peer,
+            self.blk,
+        )
+
+    def handed(self):
+        return send(
+            self.terms.at[flip(self.head, 3)],
+            self.via,
+            self.sems.at[0, 0],
+            self.sems.at[1, 0],
+            flip(self.head, 1),
+            self.blk,
+        )
+
+    def relayed(self):
+        return send(
+            self.joined,
+            self.into.at[2],
+            self.sems.at[0, 2],
+            self.sems.at[1, 2],
+            flip(self.head, 2),
+            self.blk,
+        )
+
+    def start_far(self):
+        @pl.when(jnp.logical_not(self.middle))
+        def _():
+            self.handed().start()
+
+    def start_one(self, k):
+        if k == 1:
+            self.copy(1).start()
+        elif k == 2:
+
+            @pl.when(jnp.logical_not(self.middle))
+            def _():
+                self.copy(2).start()
+
+        else:
+
+            @pl.when(self.middle)
+            def _():
+                self.copy(3).start()
+
+    def start(self):
+        self.start_far()
+        for k in (2, 3, 1):
+            self.start_one(k)
+
+    def relay(self):
+        @pl.when(self.middle)
+        def _():
+            self.handed().wait_recv()
+            mine = self.terms[flip(self.head, 2)].astype(F32)
+            self.joined[...] = (mine + self.via[...].astype(F32)).astype(BF)
+            self.relayed().start()
+
+    def arrive(self):
+        self.copy(1).wait_recv()
+        self.copy(2).wait_recv()
+
+        @pl.when(self.middle)
+        def _():
+            self.copy(3).wait_recv()
+
+        @pl.when(jnp.logical_not(self.middle))
+        def _():
+            self.into[3] = jnp.zeros_like(self.into[3])
+
+        self.into[0] = self.terms[self.head]
+
+    def drain(self):
+        self.copy(1).wait_send()
+
+        @pl.when(self.middle)
+        def _():
+            self.copy(3).wait_send()
+            self.relayed().wait_send()
+
+        @pl.when(jnp.logical_not(self.middle))
+        def _():
+            self.copy(2).wait_send()
+            self.handed().wait_send()
+
+
 def half_lane(shape):
     return lax.broadcasted_iota(jnp.int32, shape, 1) < 64
 
@@ -519,10 +661,10 @@
 
 
 def first_kernel(
-    tok, tab, wqp, ttab, tix, sca, scm,
-    tiles, normed, wq, scales, tabg,
-    tokg, wqz, turned, part, sums, parts, out_tiles,
-    zsem, lsem, tsem, wsem, asem, bsem, psem,
+    tok, tab, wqp, ttab, sca, scm, upp, out_own, tix,
+    tiles, normed, wq, scales, tabg, upz, outz, tokg,
+    wqz, turned, part, sums, parts, out_tiles,
+    zsem, lsem, tsem, wsem, asem, bsem, psem, usem, osem,
 ):
     head, blk = lax.axis_index("head"), lax.axis_index("blk")
     greet(head, blk, (1, 2, 3), range(1, 8))
@@ -532,6 +674,8 @@
     tline = Line(head, blk, tab, lambda i: tabg.at[i], tsem)
     tline.start()
     line.start()
+    uswap = Swap(head, blk, "blk", lambda i: upp.at[i], lambda i: upz.at[i], usem)
+    oline = Reach(head, blk, out_own, lambda i: outz.at[i], osem)
     turned[...] = jnp.transpose(ttab[...])
     rows = turned[pl.ds(pl.multiple_of((head * 8 + blk) * 8, 8), 8), :]
     step_lane = lax.broadcasted_iota(jnp.int32, rows.shape, 1)
@@ -543,14 +687,13 @@
     part[...] = jnp.concatenate(terms + [jnp.zeros((4, 1024), F32)], axis=0)
     one = Swap(head, blk, "blk", lambda i: part, lambda i: sums.at[i], asem)
     one.start()
+    uswap.start()
     sums[blk] = part[...]
     wqz[head] = wqp[head]
     tokg[head] = tok[...]
     tabg[head] = tab[...]
-    zswap.arrive()
-    plane = Plane(head, blk, wqz, lambda i: wq.at[:, i], wsem)
-    plane.start()
-    wq[:, pl.ds(blk, 1)] = wqz[...].reshape(4, 1, 32, 768)
+    upz[blk] = upp[blk]
+    outz[head] = out_own[...]
     one.arrive()
     total = sums[0]
     for i in range(1, 8):
@@ -558,6 +701,10 @@
     parts[head] = total
     two = Swap(head, blk, "head", lambda i: parts.at[head], lambda i: parts.at[i], bsem)
     two.start()
+    zswap.arrive()
+    plane = Plane(head, blk, wqz, lambda i: wq.at[:, i], wsem)
+    plane.start()
+    wq[:, pl.ds(blk, 1)] = wqz[...].reshape(4, 1, 32, 768)
     two.arrive()
     total = 1.0 + ((parts[0] + parts[1]) + (parts[2] + parts[3]))
     scales[...] = total
@@ -574,9 +721,6 @@
             unit, _ = norm_stats(tokg[at, seq].astype(F32))
             normed[at, pl.ds(64 * seq, 64), :] = (unit * scales[seq : seq + 1, :]).astype(BF)
         return carry
-
-    lax.fori_loop(0, 4, gather, 0)
-    plane.finish()
 
     def project(step, carry):
         at = line_order(head, step)
@@ -608,12 +752,24 @@
             head, blk, "blk", lambda i: out_tiles.at[i, at], lambda i: tiles.at[at, i], psem.at[at]
         )
 
-    lax.fori_loop(0, 4, project, 0)
+    lax.fori_loop(0, 3, gather, 0)
+    oline.start()
+    plane.finish()
+    lax.fori_loop(0, 3, project, 0)
+
+    def last(step, carry):
+        gather(step, carry)
+        return project(step, carry)
+
+    lax.fori_loop(3, 4, last, 0)
+    oline.forward()
+    uswap.arrive()
+    oline.arrive()
     for at in range(4):
         move(at).arrive()
     for at in range(4):
         move(at).drain()
-    for copies in (zswap, line, tline, plane, one, two):
+    for copies in (zswap, line, tline, plane, one, two, uswap, oline):
         copies.drain()
 
 
@@ -621,7 +777,9 @@
     return [pl.BlockSpec(memory_space=pltpu.VMEM)] * count
 
 
-def phase_one_kernel(tokens, table, wq_parts, time_table, time_index, scale_attn, scale_mlp):
+def phase_one_kernel(
+    tokens, table, wq_parts, time_table, time_index, scale_attn, scale_mlp, up_parts, w_out
+):
     dma = pltpu.SemaphoreType.DMA
     return pl.pallas_call(
         first_kernel,
@@ -631,11 +789,13 @@
             jax.ShapeDtypeStruct((4, 8, 32, 768), BF),
             jax.ShapeDtypeStruct((8, 1024), F32),
             jax.ShapeDtypeStruct((4, 64, 128), F32),
+            jax.ShapeDtypeStruct((8, 32, 512), BF),
+            jax.ShapeDtypeStruct((4, 32, 1024), BF),
+            jax.ShapeDtypeStruct((4, 2, 64, 1024), BF),
         ),
-        in_specs=whole(4) + [pl.BlockSpec(memory_space=pltpu.SMEM)] + whole(2),
-        out_specs=whole(5),
+        in_specs=whole(8) + [pl.BlockSpec(memory_space=pltpu.SMEM)],
+        out_specs=whole(8),
         scratch_shapes=[
-            pltpu.VMEM((4, 2, 64, 1024), BF),
             pltpu.VMEM((4, 32, 768), BF),
             pltpu.VMEM((256, 64), F32),
             pltpu.VMEM((8, 1024), F32),
@@ -649,12 +809,16 @@
             dma((2, 8)),
             dma((2, 4)),
             dma((4, 2, 8)),
+            dma((2, 8)),
+            dma((2, 4)),
         ],
         compiler_params=pltpu.CompilerParams(
             collective_id=0, has_side_effects=True, vmem_limit_bytes=48 << 20
         ),
         name="first",
-    )(tokens, table, wq_parts, time_table, time_index, scale_attn, scale_mlp)
+    )(tokens, table, wq_parts, time_table, scale_attn, scale_mlp, up_parts, w_out, time_index)
+
+
 EXP_SCALE = SCORE_SCALE * math.log2(math.e)
 KEYS = 256
 
@@ -705,30 +869,25 @@
 
 
 def second_kernel(
-    tiles, upp, down_own, out_own, cot_own,
+    tiles, upz, down_own, outz, cot_own,
     mixed, lse, received, up, down, out, cots,
-    upz, outz, kvt, scores, att,
-    usem, lsem, dsem, osem, psem, csem, esem,
+    kvt, scores, att,
+    lsem, dsem, psem, csem, esem,
 ):
     head, blk = lax.axis_index("head"), lax.axis_index("blk")
     greet_all(head, blk)
-    uswap = Swap(head, blk, "blk", lambda i: upp.at[i], lambda i: upz.at[i], usem)
-    uswap.start()
-    oline = Line(head, blk, out_own, lambda i: outz.at[i], osem)
-    oline.start()
-    dline = Line(head, blk, down_own, lambda i: down.at[i], dsem)
+    uline = Reach(head, blk, upz, lambda i: up.at[i], lsem)
+    uline.start()
+    dline = Reach(head, blk, down_own, lambda i: down.at[i], dsem)
     dline.start()
+    oplane = Plane(head, blk, outz, lambda i: out.at[:, i], psem)
+    oplane.start()
     cplane = Plane(head, blk, cot_own, lambda i: cots.at[i], csem)
     cplane.start()
-    upz[blk] = upp[blk]
-    outz[head] = out_own[...]
+    up[head] = upz[...]
     down[head] = down_own[...]
     cots[blk] = cot_own[...]
-    uswap.arrive()
-    up[head] = upz[...]
-    uline = Line(head, blk, upz, lambda i: up.at[i], lsem)
-    uline.start()
-    oplane = Plane(head, blk, outz, lambda i: out.at[:, i], psem)
+    out[:, pl.ds(blk, 1)] = outz[...].reshape(4, 1, 32, 1024)
     everyone = Everyone(head, blk, lambda z, b: att.at[z, b], lambda z, b: received.at[z, b], esem)
     kvt[...] = jnp.transpose(tiles[:, :, 0:64, :].reshape(2048, 128))
 
@@ -766,12 +925,6 @@
         both = jnp.transpose(jnp.concatenate(results, axis=0))
         att[z] = both.astype(BF).reshape(8, 32, 128)
 
-        @pl.when(z > 0)
-        def _():
-            at = line_order(head, z)
-            oline.step(at)
-            dline.step(at)
-
         return carry
 
     lse[...] = jnp.zeros_like(lse)
@@ -779,18 +932,23 @@
     for kz in range(4):
         everyone.start(kz)
     received[head, blk] = att[head, blk]
-    oplane.start()
-    out[:, pl.ds(blk, 1)] = outz[...].reshape(4, 1, 32, 1024)
-    for step in range(1, 4):
-        uline.step(line_order(head, jnp.int32(step)))
-    cplane.finish()
-    oplane.finish()
+    for i in range(3):
+        oplane.forward(i)
+    for i in range(3):
+        cplane.forward(i)
+    uline.forward()
+    dline.forward()
+    for i in range(-1, 3):
+        oplane.arrive(i)
+        cplane.arrive(i)
     everyone.arrive()
-    for copies in (uswap, oline, dline, uline, cplane, oplane, everyone):
+    uline.arrive()
+    dline.arrive()
+    for copies in (dline, uline, cplane, oplane, everyone):
         copies.drain()
 
 
-def phase_two_kernel(tiles, up_parts, w_down, w_out, cotangent):
+def phase_two_kernel(tiles, upz, w_down, outz, cotangent):
     dma = pltpu.SemaphoreType.DMA
     return pl.pallas_call(
         second_kernel,
@@ -806,15 +964,11 @@
         in_specs=whole(5),
         out_specs=whole(7),
         scratch_shapes=[
-            pltpu.VMEM((8, 32, 512), BF),
-            pltpu.VMEM((4, 32, 1024), BF),
             pltpu.VMEM((128, 2048), BF),
             pltpu.VMEM((2, 2048 // KEYS, KEYS, 256), F32),
             pltpu.VMEM((4, 8, 32, 128), BF),
-            dma((2, 8)),
-            dma((2, 2, 3)),
-            dma((2, 2, 3)),
-            dma((2, 2, 3)),
+            dma((2, 4)),
+            dma((2, 4)),
             dma((2, 7)),
             dma((2, 7)),
             dma((2, 4, 8)),
@@ -823,12 +977,12 @@
             collective_id=1, has_side_effects=True, vmem_limit_bytes=56 << 20
         ),
         name="second",
-    )(tiles, up_parts, w_down, w_out, cotangent)
+    )(tiles, upz, w_down, outz, cotangent)
 def third_kernel(
     received, tok, out, up, down, cots, scales,
-    grad_rx, grad_middle, middle, outq, grad_down, grad_up, grad_out, sums,
-    attended, n2g, act, gh, pairs, prx, gsend, gin, tsend, branch,
-    nsem, ssem, gsem, esem,
+    grad_rx, grad_middle, middle, outq, down_own, grad_up, grad_out, sums,
+    grad_down, dvia, djoin, din, attended, n2g, act, gh, pairs, prx, gsend, gin, tsend, branch,
+    nsem, ssem, gsem, esem, dsem,
 ):
     head, blk = lax.axis_index("head"), lax.axis_index("blk")
     core = lax.rem(blk, 2)
@@ -851,7 +1005,9 @@
         unit, _ = norm_stats(middle[rows, :])
         n2g[blk, rows, :] = (unit * scales[2 + seq : 3 + seq, :]).astype(BF)
     plane = Plane(head, blk, n2g.at[blk], lambda i: n2g.at[i], nsem)
-    plane.start()
+    for i in (1, 2, 0):
+        plane.first[i].start()
+    dfold = Fold(head, blk, grad_down, dvia, djoin, din, dsem)
     sibling = flip(blk, 1)
 
     def halves(i):
@@ -902,6 +1058,8 @@
         )
         for copy in halves(i):
             copy.start()
+        if i == 0:
+            plane.first[3].start()
     reduce(3)
     reduce(0)
     for group in range(4):
@@ -909,10 +1067,12 @@
         grad_down[group] = contract_rows(
             act[:, :, lanes].reshape(1024, 128), cots[...].reshape(1024, 1024)
         ).astype(BF)
+    dfold.start()
     for group in range(4):
         lanes = slice(256 * group, 256 * group + 256)
         part = contract_rows(n2g[:, :, lanes].reshape(1024, 256), gh[...].reshape(1024, 512))
         grad_up[group] = part.astype(BF).reshape(8, 32, 512)
+    dfold.relay()
     for i in range(1, 4):
         onward(i).wait_recv()
     sums[...] = jnp.zeros_like(sums)
@@ -945,8 +1105,11 @@
         lanes = slice(256 * group, 256 * group + 256)
         part = contract_rows(attended[:, lanes], branch[...])
         grad_out[group] = part.astype(BF).reshape(8, 32, 1024)
+    dfold.arrive()
+    down_own[...] = sum_four(din)
     everyone.arrive()
     plane.drain()
+    dfold.drain()
     for i in range(4):
         for copy in halves(i):
             copy.wait_send()
@@ -964,7 +1127,7 @@
             jax.ShapeDtypeStruct((128, 1024), F32),
             jax.ShapeDtypeStruct((128, 1024), F32),
             jax.ShapeDtypeStruct((4, 128, 1024), BF),
-            jax.ShapeDtypeStruct((4, 128, 1024), BF),
+            jax.ShapeDtypeStruct((128, 1024), F32),
             jax.ShapeDtypeStruct((4, 8, 32, 512), BF),
             jax.ShapeDtypeStruct((4, 8, 32, 1024), BF),
             jax.ShapeDtypeStruct((8, 1024), F32),
@@ -972,6 +1135,10 @@
         in_specs=whole(7),
         out_specs=whole(8),
         scratch_shapes=[
+            pltpu.VMEM((4, 128, 1024), BF),
+            pltpu.VMEM((128, 1024), BF),
+            pltpu.VMEM((128, 1024), BF),
+            pltpu.VMEM((4, 128, 1024), BF),
             pltpu.VMEM((128, 1024), BF),
             pltpu.VMEM((8, 128, 1024), BF),
             pltpu.VMEM((8, 128, 512), BF),
@@ -986,6 +1153,7 @@
             dma((2, 2, 4)),
             dma((2, 4)),
             dma((2, 4, 8)),
+            dma((2, 4)),
         ],
         compiler_params=pltpu.CompilerParams(
             collective_id=2, has_side_effects=True, vmem_limit_bytes=58 << 20
@@ -1050,18 +1218,17 @@
 
 
 def fourth_kernel(
-    tiles, grad_rx, mixed, lse, outq, middle, grad_down, grad_up, grad_out,
-    back, output, down_own, up_own, out_own,
-    queries, grads, stats, keyt, dkv, dqt, bsend, oin, din, uin, usum, near, joined, far, osum, zin,
-    qsem, dsem, usem, vsem, osem, xsem, bsem,
+    tiles, grad_rx, mixed, lse, outq, middle, grad_up, grad_out,
+    back, output, up_own, out_own,
+    queries, grads, stats, keyt, dkv, dqt, bsend, oin, uin, usum, near, joined, far, osum, zin,
+    uvia, ujoin,
+    qsem, usem, vsem, osem, xsem, bsem,
 ):
     head, blk = lax.axis_index("head"), lax.axis_index("blk")
     greet(head, blk, (1, 2, 3), range(1, 8))
-    dswap = Swap(head, blk, "head", lambda i: grad_down.at[i], lambda i: din.at[i], dsem)
-    dswap.start()
     scatter = Scatter(head, blk, grad_out, near, joined, far, osem)
     scatter.start()
-    uswap = Swap(head, blk, "head", lambda i: grad_up.at[i], lambda i: uin.at[i], usem)
+    uswap = Fold(head, blk, grad_up, uvia, ujoin, uin, usem)
     uswap.start()
     outs = []
     for i in range(1, 4):
@@ -1133,6 +1300,10 @@
         def _():
             scatter.join()
 
+        @pl.when(z == 1)
+        def _():
+            uswap.relay()
+
         @pl.when(z == 2)
         def _():
             total = middle[...] + outq[lax.div(blk, 2)].astype(F32)
@@ -1162,13 +1333,9 @@
     qmove.start()
     back[blk] = bsend[blk]
     uswap.arrive()
-    uin[head] = grad_up[head]
     usum[...] = sum_four(uin).astype(BF)
     vswap.start()
     up_own[blk] = usum[blk]
-    dswap.arrive()
-    din[head] = grad_down[head]
-    down_own[...] = sum_four(din)
     xswap.arrive()
     out_own[...] = sum_four(zin)
     vswap.arrive()
@@ -1179,23 +1346,22 @@
         kv_move(z).drain()
     for copy in outs:
         copy.wait_send()
-    for copies in (dswap, scatter, uswap, vswap, xswap, qmove):
+    for copies in (scatter, uswap, vswap, xswap, qmove):
         copies.drain()
 
 
-def phase_four_kernel(tiles, grad_rx, mixed, lse, outq, middle, grad_down, grad_up, grad_out):
+def phase_four_kernel(tiles, grad_rx, mixed, lse, outq, middle, grad_up, grad_out):
     dma = pltpu.SemaphoreType.DMA
     return pl.pallas_call(
         fourth_kernel,
         out_shape=(
             jax.ShapeDtypeStruct((8, 4, 96, 128), BF),
             jax.ShapeDtypeStruct((128, 1024), BF),
-            jax.ShapeDtypeStruct((128, 1024), F32),
             jax.ShapeDtypeStruct((8, 32, 512), BF),
             jax.ShapeDtypeStruct((32, 1024), F32),
         ),
-        in_specs=whole(9),
-        out_specs=whole(5),
+        in_specs=whole(8),
+        out_specs=whole(4),
         scratch_shapes=[
             pltpu.VMEM((8, 256, 128), BF),
             pltpu.VMEM((8, 256, 128), BF),
@@ -1205,7 +1371,6 @@
             pltpu.VMEM((8, 64, 256), F32),
             pltpu.VMEM((8, 4, 96, 128), BF),
             pltpu.VMEM((4, 128, 1024), BF),
-            pltpu.VMEM((4, 128, 1024), BF),
             pltpu.VMEM((4, 8, 32, 512), BF),
             pltpu.VMEM((8, 32, 512), BF),
             pltpu.VMEM((4, 4, 32, 1024), BF),
@@ -1213,7 +1378,8 @@
             pltpu.VMEM((4, 4, 32, 1024), BF),
             pltpu.VMEM((4, 32, 1024), BF),
             pltpu.VMEM((4, 32, 1024), BF),
-            dma((2, 4)),
+            pltpu.VMEM((8, 32, 512), BF),
+            pltpu.VMEM((8, 32, 512), BF),
             dma((2, 4)),
             dma((2, 4)),
             dma((2, 8)),
@@ -1225,16 +1391,16 @@
             collective_id=3, has_side_effects=True, vmem_limit_bytes=56 << 20
         ),
         name="fourth",
-    )(tiles, grad_rx, mixed, lse, outq, middle, grad_down, grad_up, grad_out)
+    )(tiles, grad_rx, mixed, lse, outq, middle, grad_up, grad_out)
 def fifth_kernel(
-    back, tabg, normed, wq, tok, scales, grad_middle, sums, ttab, tix,
+    back, tabg, normed, wq, tokg, scales, grad_middle, sums, ttab, tix,
     grad_tokens, gq, grad_attn, grad_mlp,
-    gp, gnp, gin, terms, near, joined, far, osum, turned, part, sums_in, parts,
+    gp, gnf, gnp, gvia, gjoin, gin, terms, near, joined, far, osum, turned, part, sums_in, parts,
     gsem, osem, xsem, asem, bsem,
 ):
     head, blk = lax.axis_index("head"), lax.axis_index("blk")
     greet(head, blk, (1, 2, 3), range(1, 8))
-    gswap = Swap(head, blk, "head", lambda i: gnp.at[i], lambda i: gin.at[i], gsem)
+    gswap = Fold(head, blk, gnp, gvia, gjoin, gin, gsem)
 
     def unturn(step, carry):
         at = flip(head, step)
@@ -1256,13 +1422,16 @@
                 )
                 query = query * both[0] + lane_swap(query) * both[1]
                 gp[at, rows, 512 + 128 * i : 640 + 128 * i] = query.astype(BF)
-        gnp[at] = contract_cols(gp[at], wq[...].reshape(1024, 768)).astype(BF)
+        gnf[at] = contract_cols(gp[at], wq[...].reshape(1024, 768))
+        gnp[at] = gnf[at].astype(BF)
         return carry
 
     for step in (3, 2, 1, 0):
         unturn(step, 0)
+        if step == 3:
+            gswap.start_far()
         if step:
-            gswap.copies[step - 1].start()
+            gswap.start_one(step)
     for group in range(4):
         lanes = slice(256 * group, 256 * group + 256)
         value = contract_rows(normed[:, :, lanes].reshape(512, 256), gp[...].reshape(512, 768))
@@ -1276,26 +1445,24 @@
         jnp.sum(jnp.where(step_lane == tix[seq], picked, 0.0), axis=1, keepdims=True)
         for seq in range(2)
     ]
-    scatter.join()
-    osum[...] = scatter.total().astype(BF)
-    xswap = Swap(head, blk, "head", lambda i: osum.at[i], lambda i: gq.at[i], xsem)
-    xswap.start()
-    gq[head] = osum[head]
-    gswap.arrive()
-    gin[head] = gnp[head]
-    firsts = []
-    for seq in range(2):
-        rows = slice(64 * seq, 64 * seq + 64)
-        grad = sum_four([gin[i, rows, :] for i in range(4)])
-        unit, spread = norm_stats(tok[rows, :].astype(F32))
-        grad_tokens[rows, :] = grad_middle[rows, :] + norm_back(
-            unit, spread, grad, scales[seq : seq + 1, :]
-        )
-        firsts.append(jnp.sum(grad * unit, axis=0, keepdims=True))
-    part[...] = jnp.concatenate(firsts + [sums[0:2, :], jnp.zeros((4, 1024), F32)], axis=0)
+    gswap.relay()
+    part[...] = jnp.concatenate(
+        [jnp.zeros((2, 1024), F32), sums[0:2, :], jnp.zeros((4, 1024), F32)], axis=0
+    )
+
+    def gather(at, carry):
+        for seq in range(2):
+            unit, _ = norm_stats(tokg[at, seq].astype(F32))
+            part[seq : seq + 1, :] += jnp.sum(
+                gnf[at, pl.ds(64 * seq, 64), :] * unit, axis=0, keepdims=True
+            )
+        return carry
+
+    lax.fori_loop(0, 4, gather, 0)
     one = Swap(head, blk, "blk", lambda i: part, lambda i: sums_in.at[i], asem)
     one.start()
     sums_in[blk] = part[...]
+    scatter.join()
     one.arrive()
     total = sums_in[0]
     for i in range(1, 8):
@@ -1303,16 +1470,28 @@
     parts[head] = total
     two = Swap(head, blk, "head", lambda i: parts.at[head], lambda i: parts.at[i], bsem)
     two.start()
+    osum[...] = scatter.total().astype(BF)
+    xswap = Swap(head, blk, "head", lambda i: osum.at[i], lambda i: gq.at[i], xsem)
+    xswap.start()
+    gq[head] = osum[head]
     two.arrive()
     total = (parts[0] + parts[1]) + (parts[2] + parts[3])
     grad_attn[...] = columns[0] * total[0:1] + columns[1] * total[1:2]
     grad_mlp[...] = columns[0] * total[2:3] + columns[1] * total[3:4]
+    gswap.arrive()
+    for seq in range(2):
+        rows = slice(64 * seq, 64 * seq + 64)
+        grad = sum_four([gin[i, rows, :] for i in range(4)])
+        unit, spread = norm_stats(tokg[head, seq].astype(F32))
+        grad_tokens[rows, :] = grad_middle[rows, :] + norm_back(
+            unit, spread, grad, scales[seq : seq + 1, :]
+        )
     xswap.arrive()
     for copies in (gswap, scatter, xswap, one, two):
         copies.drain()
 
 
-def phase_five_kernel(back, tabg, normed, wq, tok, scales, grad_middle, sums, ttab, tix):
+def phase_five_kernel(back, tabg, normed, wq, tokg, scales, grad_middle, sums, ttab, tix):
     dma = pltpu.SemaphoreType.DMA
     return pl.pallas_call(
         fifth_kernel,
@@ -1326,7 +1505,10 @@
         out_specs=whole(4),
         scratch_shapes=[
             pltpu.VMEM((4, 128, 768), BF),
+            pltpu.VMEM((4, 128, 1024), F32),
             pltpu.VMEM((4, 128, 1024), BF),
+            pltpu.VMEM((128, 1024), BF),
+            pltpu.VMEM((128, 1024), BF),
             pltpu.VMEM((4, 128, 1024), BF),
             pltpu.VMEM((4, 4, 2, 32, 768), BF),
             pltpu.VMEM((4, 4, 32, 768), BF),
@@ -1347,7 +1529,7 @@
             collective_id=4, has_side_effects=True, vmem_limit_bytes=48 << 20
         ),
         name="fifth",
-    )(back, tabg, normed, wq, tok, scales, grad_middle, sums, ttab, tix)
+    )(back, tabg, normed, wq, tokg, scales, grad_middle, sums, ttab, tix)
 def blocked(
     tokens,
     positions,
@@ -1370,23 +1552,22 @@
     wq_parts = jnp.swapaxes(wq_parts, 0, 1)
     up_parts = jnp.transpose(w_up.reshape(32, 4, 8, 128), (2, 0, 1, 3)).reshape(8, 32, 512)
     flat_tokens = tokens.reshape(128, 1024)
-    tiles, normed, wq, scales, table_all = phase_one_kernel(
-        tokens, table, wq_parts, time_table, time_index, scale_attn, scale_mlp
+    tiles, normed, wq, scales, table_all, upz, outz, tokens_all = phase_one_kernel(
+        tokens, table, wq_parts, time_table, time_index, scale_attn, scale_mlp, up_parts, w_out
     )
     mixed, lse, received, up, down, out, cot_all = phase_two_kernel(
-        tiles, up_parts, w_down, w_out, cotangent.reshape(128, 1024)
-    )
-    grad_rx, grad_middle, middle, outq, grad_down, grad_up, grad_out, sums = phase_three_kernel(
+        tiles, upz, w_down, outz, cotangent.reshape(128, 1024)
+    )
+    grad_rx, grad_middle, middle, outq, down_own, grad_up, grad_out, sums = phase_three_kernel(
         received, flat_tokens, out, up, down, cot_all, scales
     )
-    back, output, down_own, up_own, out_own = phase_four_kernel(
+    back, output, up_own, out_own = phase_four_kernel(
         tiles,
         grad_rx,
         mixed,
         lse,
         outq,
         middle,
-        grad_down,
         grad_up,
         grad_out.reshape(4, 4, 2, 32, 1024),
     )
@@ -1395,7 +1576,7 @@
         table_all,
         normed,
         wq,
-        flat_tokens,
+        tokens_all,
         scales,
         grad_middle,
         sums,

time: 278 us -> 246 us (0.88)
  Pallas kernels: 262 us -> 230 us
    pallas_call x1, Pallas kernels: 42.9 us -> 29.6 us  [phase_five_kernel(): pl.pallas_call(fifth_kernel, out_shape=(jax.ShapeDtypeStruct((128, 1024),...]
    pallas_call x1, Pallas kernels: 59.9 us -> 47.2 us  [phase_four_kernel(): pl.pallas_call(fourth_kernel, out_shape=(jax.ShapeDtypeStruct((8, 4, 96,...]
    pallas_call x1, Pallas kernels: 48.4 us -> 44 us  [phase_one_kernel(): pl.pallas_call(first_kernel, out_shape=(jax.ShapeDtypeStruct((4, 8, 96, 1...]
    pallas_call x1, Pallas kernels: 57.2 us -> 53.9 us  [phase_two_kernel(): pl.pallas_call(second_kernel, out_shape=(jax.ShapeDtypeStruct((4, 128, 25...]
    unnamed x44 -> x48, local copies, waits for them, and re-layouts: 8.41 us -> 9.81 us
where the time goes in v4:
time: 246 us
  Pallas kernels  230 us (93%)
  local copies, waits for them, and re-layouts  14.1 us (6%)
    pallas_call x1, Pallas kernels, phase_three_kernel(): pl.pallas_call(third_kernel, out_shape=(jax.ShapeDtypeStruct((4, 8, 32, 1...  54.8 us
    pallas_call x1, Pallas kernels, phase_two_kernel(): pl.pallas_call(second_kernel, out_shape=(jax.ShapeDtypeStruct((4, 128, 25...  53.9 us
    pallas_call x1, Pallas kernels, phase_four_kernel(): pl.pallas_call(fourth_kernel, out_shape=(jax.ShapeDtypeStruct((8, 4, 96,...  47.2 us
    pallas_call x1, Pallas kernels, phase_one_kernel(): pl.pallas_call(first_kernel, out_shape=(jax.ShapeDtypeStruct((4, 8, 96, 1...  44 us
    pallas_call x1, Pallas kernels, phase_five_kernel(): pl.pallas_call(fifth_kernel, out_shape=(jax.ShapeDtypeStruct((128, 1024),...  29.6 us
    unnamed x48, local copies, waits for them, and re-layouts  9.81 us

profile of v4, /device:TPU:0, one launch (start us, length us, event | category | flops | bytes accessed | tf_op | source)
XLA Modules:
  0.0 246.0 jit_solution(14976518383594401293)
XLA Ops:
  0.6 0.0 copy-start.17
  0.7 0.7 convert_element_type.24
  1.4 0.3 multiply_cosine_fusion
  1.7 0.1 pad_maximum_fusion.1.tab
  1.8 1.0 copy.46
  2.8 0.1 copy.55
  2.9 0.1 reshape.89.upp
  3.0 0.0 copy-done.17
  3.0 0.0 copy-start.1
  3.0 0.0 copy-start.4
  3.1 0.0 copy-start.9
  3.1 0.0 copy-start.11
  3.1 0.0 copy-start.12
  3.1 0.0 copy-start.13
  3.1 0.3 reshape.86
  3.4 0.1 fusion
  3.5 0.1 copy_bitcast_fusion.4
  3.6 0.1 pad_maximum_fusion
  3.7 0.2 copy.35
  3.9 0.2 reshape.87
  4.1 0.2 reshape.99
  4.3 0.0 copy-done.1
  4.3 0.0 copy-done.4
  4.3 0.0 copy-done.9
  4.3 0.0 copy-done.11
  4.3 0.0 copy-done.12
  4.3 0.0 copy-done.13
  4.4 44.0 %first.1 = (bf16[4,8,96,128]{3,2,1,0:T(8,128)(2,1)S(1)}, bf16[4,128,1024]{2,1,0:T(8,128)(2,1)S(1)}, bf16[4,8,32,768]{3,2,1,0:T(8,128)(2,1)S(1)}, f32[8,1024]{1,0...) custom-call(bf16[2,64,1024]{2,1,0:T(8,128)(2,1)S(1)} %copy-done.1, ...), custom_call_target="tpu_custom_call" | custom-call | tf_op jit(solution)/shard_map/first/pallas_call | solution.py:784
  48.3 0.0 copy-start
  48.3 0.9 copy-done
  49.2 0.7 copy-done.5
  49.9 0.7 copy-done.6
  50.6 53.9 %second.1 = (f32[4,128,256]{2,1,0:T(8,128)}, f32[4,8,256]{2,1,0:T(8,128)}, bf16[4,8,32,128]{3,2,1,0:T(8,128)(2,1)}, bf16[4,8,32,512]{3,2,1,0:T(8,128)(2,1)}, bf1...) custom-call(bf16[4,8,96,128]{3,2,1,0:T(8,128)(2,1)} %copy-done, ...), custom_call_target="tpu_custom_call" | custom-call | tf_op jit(solution)/shard_map/second/pallas_call | solution.py:953
  104.6 0.0 copy-done.7
  104.6 54.8 %third.1 = (bf16[4,8,32,128]{3,2,1,0:T(8,128)(2,1)}, f32[128,1024]{1,0:T(8,128)}, f32[128,1024]{1,0:T(8,128)}, bf16[4,128,1024]{2,1,0:T(8,128)(2,1)}, f32[128,10...) custom-call(bf16[4,8,32,128]{3,2,1,0:T(8,128)(2,1)} %get-tuple-element.42.rec, ...), custom_call_target="tpu_custom_call" | custom-call | tf_op jit(solution)/shard_map/third/pallas_call | solution.py:1123
  159.4 0.0 copy-start.3
  159.4 0.0 copy-start.8
  159.4 0.0 copy-start.10
  159.4 47.2 %fourth.1 = (bf16[8,4,96,128]{3,2,1,0:T(8,128)(2,1)}, bf16[128,1024]{1,0:T(8,128)(2,1)}, bf16[8,32,512]{2,1,0:T(8,128)(2,1)}, f32[32,1024]{1,0:T(8,128)}) custom-call(bf16[4,8,96,128]{3,2,1,0:T(8,128)(2,1)} %copy-done, bf16[4,8,32,128]{3,2,1,0:T(8,128)(2,1)} %get-tuple-element.48.grad_rx, f32[4,128,256]{2,1,0:T(8,128)} %get-tuple-element.49.mixed, ...), custom_call_target="tpu_custom_call" | custom-call | tf_op jit(solution)/shard_map/fourth/pallas_call | solution.py:1355
  206.6 0.0 copy-done.3
  206.6 0.0 copy-done.8
  206.6 0.0 copy-done.10
  206.6 0.0 copy-start.2
  206.6 1.1 copy-done.2
  207.8 29.6 %fifth.1 = (f32[128,1024]{1,0:T(8,128)S(1)}, bf16[4,32,768]{2,1,0:T(8,128)(2,1)S(1)}, f32[8,1024]{1,0:T(8,128)S(1)}, f32[8,1024]{1,0:T(8,128)S(1)}) custom-call(bf16[8,4,96,128]{3,2,1,0:T(8,128)(2,1)S(1)} %copy-done.2, f32[4,64,128]{2,1,0:T(8,128)S(1)} %get-tuple-element.57.tabg, bf16[4,128,1024]{2,1,0:T(8,128)(2,1)S(1)} %get-tuple-element.58.normed, ...), custom_call_target="tpu_custom_call" | custom-call | tf_op jit(solution)/shard_map/fifth/pallas_call | solution.py:1496
  237.4 0.1 stack_reshape.3
  237.6 0.2 reshape.95
  237.8 0.4 fusion.1
  238.2 0.0 copy-start.15
  238.2 0.1 convert_bitcast_fusion
  238.4 0.5 copy.41
  238.9 0.0 copy-start.16
  238.9 1.3 reshape.96
  240.2 0.0 copy-done.15
  240.2 0.2 reshape.98
  240.4 0.0 copy-start.14
  240.4 0.3 copy.42
  240.7 1.1 copy.54
  241.8 0.7 copy.64
  242.5 0.8 copy.65
  243.3 0.7 copy.66
  244.0 0.8 copy.67
  244.8 0.6 copy.68
  245.4 0.6 copy.69
  (16 shorter events, 0.1 us)
Async XLA Ops:
  0.6 2.4 copy-start.17
  3.0 1.3 copy-start.1
  3.0 1.3 copy-start.4
  3.1 1.3 copy-start.9
  3.1 1.3 copy-start.11
  3.1 1.3 copy-start.12
  3.1 1.2 copy-start.13
  48.3 0.9 copy-start
  49.2 0.7 copy-start.5
  49.9 0.7 copy-start.6
  50.6 53.9 %copy-start.7 = (f32[8,1024]{1,0:T(8,128)}, f32[8,1024]{1,0:T(8,128)S(1)}, u32[]{:S(2)}) copy-start(f32[8,1024]{1,0:T(8,128)S(1)} %get-tuple-element.47.scales) | copy-start | bytes 98308
  159.4 47.2 %copy-start.3 = (f32[128,1024]{1,0:T(8,128)S(1)}, f32[128,1024]{1,0:T(8,128)}, u32[]{:S(2)}) copy-start(f32[128,1024]{1,0:T(8,128)} %get-tuple-element.61.grad_middle) | copy-start | bytes 1572868
  159.4 47.2 %copy-start.8 = (f32[8,1024]{1,0:T(8,128)S(1)}, f32[8,1024]{1,0:T(8,128)}, u32[]{:S(2)}) copy-start(f32[8,1024]{1,0:T(8,128)} %copy-done.7) | copy-start | bytes 98308
  159.4 47.2 %copy-start.10 = (f32[8,1024]{1,0:T(8,128)S(1)}, f32[8,1024]{1,0:T(8,128)}, u32[]{:S(2)}) copy-start(f32[8,1024]{1,0:T(8,128)} %get-tuple-element.62.sums) | copy-start | bytes 98308
  206.6 1.1 copy-start.2
  238.2 2.0 copy-start.15
  238.9 2.9 %copy-start.16 = (bf16[128,1024]{1,0:T(8,128)(2,1)S(1)}, bf16[128,1024]{1,0:T(8,128)(2,1)}, u32[]{:S(2)}) copy-start(bf16[128,1024]{1,0:T(8,128)(2,1)} %get-tuple-element.55) | copy-start | bytes 786436
  240.2 3.1 %copy-start.18 = (f32[32,1024]{1,0:T(8,128)S(1)}, f32[32,1024]{1,0:T(8,128)}, u32[]{:S(2)}) copy-start(f32[32,1024]{1,0:T(8,128)} %get-tuple-element.96) | copy-start | bytes 393220
  240.4 3.6 %copy-start.14 = (f32[128,1024]{1,0:T(8,128)S(1)}, f32[128,1024]{1,0:T(8,128)}, u32[]{:S(2)}) copy-start(f32[128,1024]{1,0:T(8,128)} %get-tuple-element.98) | copy-start | bytes 1572868

commit v5 on v4

--- a/solution.py
+++ b/solution.py
@@ -660,14 +660,82 @@
     return jnp.where(left, top, pltpu.roll(bottom, 64, 1))
 
 
-def first_kernel(
-    tok, tab, wqp, ttab, sca, scm, upp, out_own, tix,
-    tiles, normed, wq, scales, tabg, upz, outz, tokg,
-    wqz, turned, part, sums, parts, out_tiles,
+EXP_SCALE = SCORE_SCALE * math.log2(math.e)
+KEYS = 256
+
+
+def flip_by(head, k):
+    low, high = lax.rem(k, 2), lax.div(k, 2)
+    value = head + low - 2 * low * lax.rem(head, 2)
+    return value + 2 * high - 4 * high * lax.div(head, 2)
+
+
+class Everyone:
+    def __init__(self, head, blk, source, target, sems):
+        self.head, self.blk, self.source, self.target, self.sems = head, blk, source, target, sems
+
+    def copy(self, kz, k):
+        z, b = flip_by(self.head, jnp.int32(kz)), flip(self.blk, k)
+        return send(
+            self.source(z, b),
+            self.target(self.head, self.blk),
+            self.sems.at[0, kz, k],
+            self.sems.at[1, kz, k],
+            z,
+            b,
+        )
+
+    def start(self, kz):
+        if isinstance(kz, int):
+            first = kz > 0
+        else:
+
+            @pl.when(kz > 0)
+            def _():
+                self.copy(kz, 0).start()
+
+            first = False
+        for k in range(0 if first else 1, 8):
+            self.copy(kz, k).start()
+
+    def arrive(self):
+        for kz in range(4):
+            for k in range(1 if kz == 0 else 0, 8):
+                self.copy(kz, k).wait_recv()
+
+    def drain(self):
+        for kz in range(4):
+            for k in range(1 if kz == 0 else 0, 8):
+                self.copy(kz, k).wait_send()
+
+
+def greet_all(head, blk):
+    barrier = pltpu.get_barrier_semaphore()
+    for kz in range(4):
+        for k in range(8):
+            if kz or k:
+                pl.semaphore_signal(
+                    barrier, inc=1, device_id=(flip(head, kz), flip(blk, k)), device_id_type=MESH
+                )
+    pl.semaphore_wait(barrier, 31)
+
+
+def group_rows(value):
+    return jnp.sum(value.reshape(value.shape[0] // 8, 8, value.shape[1]), axis=0)
+
+
+def front_kernel(
+    tok, tab, wqp, ttab, sca, scm, upp, out_own, down_own, cot_own, tix,
+    tiles, normed, wq, scales, tabg, tokg, mixed, lse,
+    grad_rx, grad_middle, middle, outq, grad_down, grad_up, grad_out, sums,
+    wqz, turned, part, sums_in, parts, out_tiles, upz, outz, up, down, out, cots,
+    kvt, scores, att, received, attended, n2g, act, gh, pairs, prx, gsend, gin, tsend, branch,
     zsem, lsem, tsem, wsem, asem, bsem, psem, usem, osem,
+    usem2, dsem, qsem, csem, esem, nsem, ssem, gsem, fsem,
 ):
     head, blk = lax.axis_index("head"), lax.axis_index("blk")
-    greet(head, blk, (1, 2, 3), range(1, 8))
+    core = lax.rem(blk, 2)
+    greet_all(head, blk)
     zswap = Swap(head, blk, "head", lambda i: wqp.at[i], lambda i: wqz.at[i], zsem)
     zswap.start()
     line = Line(head, blk, tok, lambda i: tokg.at[i], lsem)
@@ -676,6 +744,12 @@
     line.start()
     uswap = Swap(head, blk, "blk", lambda i: upp.at[i], lambda i: upz.at[i], usem)
     oline = Reach(head, blk, out_own, lambda i: outz.at[i], osem)
+    uline = Line(head, blk, upz, lambda i: up.at[i], usem2)
+    dline = Line(head, blk, down_own, lambda i: down.at[i], dsem)
+    oplane = Plane(head, blk, outz, lambda i: out.at[:, i], qsem)
+    cplane = Plane(head, blk, cot_own, lambda i: cots.at[i], csem)
+    everyone = Everyone(head, blk, lambda z, b: att.at[z, b], lambda z, b: received.at[z, b], esem)
+    backward = Everyone(head, blk, lambda z, b: tsend.at[z, b], lambda z, b: grad_rx.at[z, b], fsem)
     turned[...] = jnp.transpose(ttab[...])
     rows = turned[pl.ds(pl.multiple_of((head * 8 + blk) * 8, 8), 8), :]
     step_lane = lax.broadcasted_iota(jnp.int32, rows.shape, 1)
@@ -685,19 +759,21 @@
             column = jnp.sum(jnp.where(step_lane == tix[seq], rows, 0.0), axis=1, keepdims=True)
             terms.append(jnp.sum(column * weight[...].astype(F32), axis=0, keepdims=True))
     part[...] = jnp.concatenate(terms + [jnp.zeros((4, 1024), F32)], axis=0)
-    one = Swap(head, blk, "blk", lambda i: part, lambda i: sums.at[i], asem)
+    one = Swap(head, blk, "blk", lambda i: part, lambda i: sums_in.at[i], asem)
     one.start()
     uswap.start()
-    sums[blk] = part[...]
+    sums_in[blk] = part[...]
     wqz[head] = wqp[head]
     tokg[head] = tok[...]
     tabg[head] = tab[...]
     upz[blk] = upp[blk]
     outz[head] = out_own[...]
+    down[head] = down_own[...]
+    cots[blk] = cot_own[...]
     one.arrive()
-    total = sums[0]
+    total = sums_in[0]
     for i in range(1, 8):
-        total = total + sums[i]
+        total = total + sums_in[i]
     parts[head] = total
     two = Swap(head, blk, "head", lambda i: parts.at[head], lambda i: parts.at[i], bsem)
     two.start()
@@ -762,147 +838,28 @@
         return project(step, carry)
 
     lax.fori_loop(3, 4, last, 0)
+    uswap.arrive()
+    up[head] = upz[...]
+    uline.start()
     oline.forward()
-    uswap.arrive()
     oline.arrive()
+    out[:, pl.ds(blk, 1)] = outz[...].reshape(4, 1, 32, 1024)
     for at in range(4):
         move(at).arrive()
-    for at in range(4):
-        move(at).drain()
-    for copies in (zswap, line, tline, plane, one, two, uswap, oline):
-        copies.drain()
-
-
-def whole(count):
-    return [pl.BlockSpec(memory_space=pltpu.VMEM)] * count
-
-
-def phase_one_kernel(
-    tokens, table, wq_parts, time_table, time_index, scale_attn, scale_mlp, up_parts, w_out
-):
-    dma = pltpu.SemaphoreType.DMA
-    return pl.pallas_call(
-        first_kernel,
-        out_shape=(
-            jax.ShapeDtypeStruct((4, 8, 96, 128), BF),
-            jax.ShapeDtypeStruct((4, 128, 1024), BF),
-            jax.ShapeDtypeStruct((4, 8, 32, 768), BF),
-            jax.ShapeDtypeStruct((8, 1024), F32),
-            jax.ShapeDtypeStruct((4, 64, 128), F32),
-            jax.ShapeDtypeStruct((8, 32, 512), BF),
-            jax.ShapeDtypeStruct((4, 32, 1024), BF),
-            jax.ShapeDtypeStruct((4, 2, 64, 1024), BF),
-        ),
-        in_specs=whole(8) + [pl.BlockSpec(memory_space=pltpu.SMEM)],
-        out_specs=whole(8),
-        scratch_shapes=[
-            pltpu.VMEM((4, 32, 768), BF),
-            pltpu.VMEM((256, 64), F32),
-            pltpu.VMEM((8, 1024), F32),
-            pltpu.VMEM((8, 8, 1024), F32),
-            pltpu.VMEM((4, 8, 1024), F32),
-            pltpu.VMEM((8, 4, 96, 128), BF),
-            dma((2, 4)),
-            dma((2, 2, 3)),
-            dma((2, 2, 3)),
-            dma((2, 7)),
-            dma((2, 8)),
-            dma((2, 4)),
-            dma((4, 2, 8)),
-            dma((2, 8)),
-            dma((2, 4)),
-        ],
-        compiler_params=pltpu.CompilerParams(
-            collective_id=0, has_side_effects=True, vmem_limit_bytes=48 << 20
-        ),
-        name="first",
-    )(tokens, table, wq_parts, time_table, scale_attn, scale_mlp, up_parts, w_out, time_index)
-
-
-EXP_SCALE = SCORE_SCALE * math.log2(math.e)
-KEYS = 256
-
-
-class Everyone:
-    def __init__(self, head, blk, source, target, sems):
-        self.head, self.blk, self.source, self.target, self.sems = head, blk, source, target, sems
-
-    def copy(self, kz, k):
-        z, b = flip(self.head, kz), flip(self.blk, k)
-        return send(
-            self.source(z, b),
-            self.target(self.head, self.blk),
-            self.sems.at[0, kz, k],
-            self.sems.at[1, kz, k],
-            z,
-            b,
-        )
-
-    def start(self, kz):
-        for k in range(1 if kz == 0 else 0, 8):
-            self.copy(kz, k).start()
-
-    def arrive(self):
-        for kz in range(4):
-            for k in range(1 if kz == 0 else 0, 8):
-                self.copy(kz, k).wait_recv()
-
-    def drain(self):
-        for kz in range(4):
-            for k in range(1 if kz == 0 else 0, 8):
-                self.copy(kz, k).wait_send()
-
-
-def greet_all(head, blk):
-    barrier = pltpu.get_barrier_semaphore()
-    for kz in range(4):
-        for k in range(8):
-            if kz or k:
-                pl.semaphore_signal(
-                    barrier, inc=1, device_id=(flip(head, kz), flip(blk, k)), device_id_type=MESH
-                )
-    pl.semaphore_wait(barrier, 31)
-
-
-def group_rows(value):
-    return jnp.sum(value.reshape(value.shape[0] // 8, 8, value.shape[1]), axis=0)
-
-
-def second_kernel(
-    tiles, upz, down_own, outz, cot_own,
-    mixed, lse, received, up, down, out, cots,
-    kvt, scores, att,
-    lsem, dsem, psem, csem, esem,
-):
-    head, blk = lax.axis_index("head"), lax.axis_index("blk")
-    greet_all(head, blk)
-    uline = Reach(head, blk, upz, lambda i: up.at[i], lsem)
-    uline.start()
-    dline = Reach(head, blk, down_own, lambda i: down.at[i], dsem)
-    dline.start()
-    oplane = Plane(head, blk, outz, lambda i: out.at[:, i], psem)
     oplane.start()
-    cplane = Plane(head, blk, cot_own, lambda i: cots.at[i], csem)
-    cplane.start()
-    up[head] = upz[...]
-    down[head] = down_own[...]
-    cots[blk] = cot_own[...]
-    out[:, pl.ds(blk, 1)] = outz[...].reshape(4, 1, 32, 1024)
-    everyone = Everyone(head, blk, lambda z, b: att.at[z, b], lambda z, b: received.at[z, b], esem)
     kvt[...] = jnp.transpose(tiles[:, :, 0:64, :].reshape(2048, 128))
 
-    def attend(z, carry):
-        packed = tiles[z, :, 64:96, :].reshape(256, 128)
-        left = half_lane((256, 128))
-        flat = packed.astype(F32)
+    def attend(step, carry):
+        z = flip_by(head, 3 - step)
+        flat = jnp.transpose(tiles[z, :, 64:96, :].reshape(256, 128).astype(F32))
+        blank = jnp.zeros((64, 256), F32)
         results = []
         for side in range(2):
-            query = flat if side == 0 else pltpu.roll(flat, 64, 1)
-            query = jnp.where(left, query, 0.0).astype(BF)
+            query = jnp.concatenate([flat[64 * side : 64 * side + 64], blank], axis=0).astype(BF)
             top = None
             for c in range(2048 // KEYS):
                 keys = tiles[c // 2, 4 * (c % 2) : 4 * (c % 2) + 4, 0:64, :].reshape(KEYS, 128)
-                part = contract_cols(keys, query)
+                part = jnp.dot(keys, query, preferred_element_type=F32)
                 scores[side, c] = part
                 peak = jnp.max(part.reshape(KEYS // 8, 8, 256), axis=0)
                 top = peak if top is None else jnp.maximum(top, peak)
@@ -924,69 +881,33 @@
             results.append(mix)
         both = jnp.transpose(jnp.concatenate(results, axis=0))
         att[z] = both.astype(BF).reshape(8, 32, 128)
+        everyone.start(3 - step)
+
+        @pl.when(step == 0)
+        def _():
+            uline.step(line_order(head, jnp.int32(1)))
+
+        @pl.when(step == 1)
+        def _():
+            uline.step(line_order(head, jnp.int32(2)))
+
+        @pl.when(step == 2)
+        def _():
+            uline.step(line_order(head, jnp.int32(3)))
+            dline.start()
+            for i in range(3):
+                oplane.forward(i)
+            cplane.start()
 
         return carry
 
     lse[...] = jnp.zeros_like(lse)
     lax.fori_loop(0, 4, attend, 0)
-    for kz in range(4):
-        everyone.start(kz)
     received[head, blk] = att[head, blk]
-    for i in range(3):
-        oplane.forward(i)
-    for i in range(3):
-        cplane.forward(i)
-    uline.forward()
-    dline.forward()
+    dline.step(line_order(head, jnp.int32(1)))
     for i in range(-1, 3):
         oplane.arrive(i)
-        cplane.arrive(i)
     everyone.arrive()
-    uline.arrive()
-    dline.arrive()
-    for copies in (dline, uline, cplane, oplane, everyone):
-        copies.drain()
-
-
-def phase_two_kernel(tiles, upz, w_down, outz, cotangent):
-    dma = pltpu.SemaphoreType.DMA
-    return pl.pallas_call(
-        second_kernel,
-        out_shape=(
-            jax.ShapeDtypeStruct((4, 128, 256), F32),
-            jax.ShapeDtypeStruct((4, 8, 256), F32),
-            jax.ShapeDtypeStruct((4, 8, 32, 128), BF),
-            jax.ShapeDtypeStruct((4, 8, 32, 512), BF),
-            jax.ShapeDtypeStruct((4, 128, 1024), BF),
-            jax.ShapeDtypeStruct((4, 8, 32, 1024), BF),
-            jax.ShapeDtypeStruct((8, 128, 1024), BF),
-        ),
-        in_specs=whole(5),
-        out_specs=whole(7),
-        scratch_shapes=[
-            pltpu.VMEM((128, 2048), BF),
-            pltpu.VMEM((2, 2048 // KEYS, KEYS, 256), F32),
-            pltpu.VMEM((4, 8, 32, 128), BF),
-            dma((2, 4)),
-            dma((2, 4)),
-            dma((2, 7)),
-            dma((2, 7)),
-            dma((2, 4, 8)),
-        ],
-        compiler_params=pltpu.CompilerParams(
-            collective_id=1, has_side_effects=True, vmem_limit_bytes=56 << 20
-        ),
-        name="second",
-    )(tiles, upz, w_down, outz, cotangent)
-def third_kernel(
-    received, tok, out, up, down, cots, scales,
-    grad_rx, grad_middle, middle, outq, down_own, grad_up, grad_out, sums,
-    grad_down, dvia, djoin, din, attended, n2g, act, gh, pairs, prx, gsend, gin, tsend, branch,
-    nsem, ssem, gsem, esem, dsem,
-):
-    head, blk = lax.axis_index("head"), lax.axis_index("blk")
-    core = lax.rem(blk, 2)
-    greet_all(head, blk)
     for seq in range(2):
         for group in range(4):
             for i in range(2):
@@ -997,17 +918,20 @@
                 attended[64 * seq + 32 : 64 * seq + 64, lanes] = join_halves(
                     first, second, 1
                 ).astype(BF)
-    middle[...] = tok[...].astype(F32) + jnp.dot(
+    middle[...] = tok[...].astype(F32).reshape(128, 1024) + jnp.dot(
         attended[...], out[...].reshape(1024, 1024), preferred_element_type=F32
     )
     for seq in range(2):
         rows = slice(64 * seq, 64 * seq + 64)
         unit, _ = norm_stats(middle[rows, :])
         n2g[blk, rows, :] = (unit * scales[2 + seq : 3 + seq, :]).astype(BF)
-    plane = Plane(head, blk, n2g.at[blk], lambda i: n2g.at[i], nsem)
+    nplane = Plane(head, blk, n2g.at[blk], lambda i: n2g.at[i], nsem)
     for i in (1, 2, 0):
-        plane.first[i].start()
-    dfold = Fold(head, blk, grad_down, dvia, djoin, din, dsem)
+        nplane.first[i].start()
+    dline.step(line_order(head, jnp.int32(2)))
+    nplane.first[3].start()
+    cplane.finish()
+    dline.step(line_order(head, jnp.int32(3)))
     sibling = flip(blk, 1)
 
     def halves(i):
@@ -1032,12 +956,12 @@
     for i in range(4):
         chip = lax.div(flip(blk, 2 * i), 2)
         if i == 0:
-            plane.arrive(-1)
+            nplane.arrive(-1)
         else:
-            plane.forward(i - 1)
+            nplane.forward(i - 1)
             if i > 1:
                 reduce(i - 1)
-            plane.arrive(i - 1)
+            nplane.arrive(i - 1)
         at = pl.ds(2 * chip, 2)
         rows = n2g[at].reshape(256, 1024)
         hidden = jnp.dot(rows, up[...].reshape(1024, 512), preferred_element_type=F32)
@@ -1058,8 +982,6 @@
         )
         for copy in halves(i):
             copy.start()
-        if i == 0:
-            plane.first[3].start()
     reduce(3)
     reduce(0)
     for group in range(4):
@@ -1067,12 +989,10 @@
         grad_down[group] = contract_rows(
             act[:, :, lanes].reshape(1024, 128), cots[...].reshape(1024, 1024)
         ).astype(BF)
-    dfold.start()
     for group in range(4):
         lanes = slice(256 * group, 256 * group + 256)
         part = contract_rows(n2g[:, :, lanes].reshape(1024, 256), gh[...].reshape(1024, 512))
         grad_up[group] = part.astype(BF).reshape(8, 32, 512)
-    dfold.relay()
     for i in range(1, 4):
         onward(i).wait_recv()
     sums[...] = jnp.zeros_like(sums)
@@ -1088,57 +1008,87 @@
         grad_middle[rows, :] = whole_grad
         branch[rows, :] = whole_grad.astype(BF)
         sums[seq : seq + 1, :] = jnp.sum(grad * unit, axis=0, keepdims=True)
-    grad_att = contract_cols(branch[...], out[...].reshape(1024, 1024))
-    for seq in range(2):
-        for group in range(4):
+
+    def give(step, carry):
+        group = flip_by(head, 3 - step)
+        part = contract_cols(branch[...], out[group].reshape(256, 1024))
+        for seq in range(2):
             for i in range(2):
-                lanes = slice(256 * group + 128 * i, 256 * group + 128 * i + 128)
-                top = grad_att[64 * seq : 64 * seq + 32, lanes]
-                bottom = grad_att[64 * seq + 32 : 64 * seq + 64, lanes]
+                lanes = slice(128 * i, 128 * i + 128)
+                top = part[64 * seq : 64 * seq + 32, lanes]
+                bottom = part[64 * seq + 32 : 64 * seq + 64, lanes]
                 for right in range(2):
                     tsend[group, 4 * seq + 2 * i + right] = join_halves(top, bottom, right).astype(BF)
-    everyone = Everyone(head, blk, lambda z, b: tsend.at[z, b], lambda z, b: grad_rx.at[z, b], esem)
-    for kz in range(4):
-        everyone.start(kz)
+        backward.start(3 - step)
+        return carry
+
+    lax.fori_loop(0, 4, give, 0)
     grad_rx[head, blk] = tsend[head, blk]
     for group in range(4):
         lanes = slice(256 * group, 256 * group + 256)
         part = contract_rows(attended[:, lanes], branch[...])
         grad_out[group] = part.astype(BF).reshape(8, 32, 1024)
-    dfold.arrive()
-    down_own[...] = sum_four(din)
-    everyone.arrive()
-    plane.drain()
-    dfold.drain()
+    backward.arrive()
+    for at in range(4):
+        move(at).drain()
     for i in range(4):
         for copy in halves(i):
             copy.wait_send()
         if i:
             onward(i).wait_send()
-    everyone.drain()
-
-
-def phase_three_kernel(received, tokens, out, up, down, cots, scales):
+    for copies in (
+        zswap, line, tline, plane, one, two, uswap, oline,
+        uline, dline, oplane, cplane, everyone, nplane, backward,
+    ):
+        copies.drain()
+
+
+def whole(count):
+    return [pl.BlockSpec(memory_space=pltpu.VMEM)] * count
+
+
+def front(tokens, table, wq_parts, time_table, scales_in, up_parts, w_out, w_down, cot, time_index):
     dma = pltpu.SemaphoreType.DMA
+    shape = jax.ShapeDtypeStruct
     return pl.pallas_call(
-        third_kernel,
+        front_kernel,
         out_shape=(
-            jax.ShapeDtypeStruct((4, 8, 32, 128), BF),
-            jax.ShapeDtypeStruct((128, 1024), F32),
-            jax.ShapeDtypeStruct((128, 1024), F32),
-            jax.ShapeDtypeStruct((4, 128, 1024), BF),
-            jax.ShapeDtypeStruct((128, 1024), F32),
-            jax.ShapeDtypeStruct((4, 8, 32, 512), BF),
-            jax.ShapeDtypeStruct((4, 8, 32, 1024), BF),
-            jax.ShapeDtypeStruct((8, 1024), F32),
+            shape((4, 8, 96, 128), BF),
+            shape((4, 128, 1024), BF),
+            shape((4, 8, 32, 768), BF),
+            shape((8, 1024), F32),
+            shape((4, 64, 128), F32),
+            shape((4, 2, 64, 1024), BF),
+            shape((4, 128, 256), F32),
+            shape((4, 8, 256), F32),
+            shape((4, 8, 32, 128), BF),
+            shape((128, 1024), F32),
+            shape((128, 1024), F32),
+            shape((4, 128, 1024), BF),
+            shape((4, 128, 1024), BF),
+            shape((4, 8, 32, 512), BF),
+            shape((4, 8, 32, 1024), BF),
+            shape((8, 1024), F32),
         ),
-        in_specs=whole(7),
-        out_specs=whole(8),
+        in_specs=whole(10) + [pl.BlockSpec(memory_space=pltpu.SMEM)],
+        out_specs=whole(16),
         scratch_shapes=[
+            pltpu.VMEM((4, 32, 768), BF),
+            pltpu.VMEM((256, 64), F32),
+            pltpu.VMEM((8, 1024), F32),
+            pltpu.VMEM((8, 8, 1024), F32),
+            pltpu.VMEM((4, 8, 1024), F32),
+            pltpu.VMEM((8, 4, 96, 128), BF),
+            pltpu.VMEM((8, 32, 512), BF),
+            pltpu.VMEM((4, 32, 1024), BF),
+            pltpu.VMEM((4, 8, 32, 512), BF),
             pltpu.VMEM((4, 128, 1024), BF),
-            pltpu.VMEM((128, 1024), BF),
-            pltpu.VMEM((128, 1024), BF),
-            pltpu.VMEM((4, 128, 1024), BF),
+            pltpu.VMEM((4, 8, 32, 1024), BF),
+            pltpu.VMEM((8, 128, 1024), BF),
+            pltpu.VMEM((128, 2048), BF),
+            pltpu.VMEM((2, 2048 // KEYS, KEYS, 256), F32),
+            pltpu.VMEM((4, 8, 32, 128), BF),
+            pltpu.VMEM((4, 8, 32, 128), BF),
             pltpu.VMEM((128, 1024), BF),
             pltpu.VMEM((8, 128, 1024), BF),
             pltpu.VMEM((8, 128, 512), BF),
@@ -1149,17 +1099,32 @@
             pltpu.VMEM((4, 128, 1024), BF),
             pltpu.VMEM((4, 8, 32, 128), BF),
             pltpu.VMEM((128, 1024), BF),
+            dma((2, 4)),
+            dma((2, 2, 3)),
+            dma((2, 2, 3)),
+            dma((2, 7)),
+            dma((2, 8)),
+            dma((2, 4)),
+            dma((4, 2, 8)),
+            dma((2, 8)),
+            dma((2, 4)),
+            dma((2, 2, 3)),
+            dma((2, 2, 3)),
+            dma((2, 7)),
+            dma((2, 7)),
+            dma((2, 4, 8)),
             dma((2, 7)),
             dma((2, 2, 4)),
             dma((2, 4)),
             dma((2, 4, 8)),
-            dma((2, 4)),
         ],
         compiler_params=pltpu.CompilerParams(
-            collective_id=2, has_side_effects=True, vmem_limit_bytes=58 << 20
+            collective_id=0, has_side_effects=True, vmem_limit_bytes=56 << 20
         ),
-        name="third",
-    )(received, tokens, out, up, down, cots, scales)
+        name="front",
+    )(tokens, table, wq_parts, time_table, *scales_in, up_parts, w_out, w_down, cot, time_index)
+
+
 class Scatter:
     def __init__(self, head, blk, terms, near, joined, far, sems):
         self.head, self.blk, self.core = head, blk, lax.rem(blk, 2)
@@ -1218,18 +1183,20 @@
 
 
 def fourth_kernel(
-    tiles, grad_rx, mixed, lse, outq, middle, grad_up, grad_out,
-    back, output, up_own, out_own,
-    queries, grads, stats, keyt, dkv, dqt, bsend, oin, uin, usum, near, joined, far, osum, zin,
-    uvia, ujoin,
-    qsem, usem, vsem, osem, xsem, bsem,
+    tiles, grad_rx, mixed, lse, outq, middle, grad_down, grad_up, grad_out,
+    back, output, down_own, up_own, out_own,
+    queries, grads, queries_t, grads_t, stats, keyt, dkv, dqt, bsend, oin, din, uin, usum, near, joined, far, osum, zin,
+    dvia, djoin, uvia, ujoin,
+    qsem, dsem, usem, vsem, osem, xsem, bsem,
 ):
     head, blk = lax.axis_index("head"), lax.axis_index("blk")
     greet(head, blk, (1, 2, 3), range(1, 8))
     scatter = Scatter(head, blk, grad_out, near, joined, far, osem)
     scatter.start()
+    dswap = Fold(head, blk, grad_down, dvia, djoin, din, dsem)
     uswap = Fold(head, blk, grad_up, uvia, ujoin, uin, usem)
     uswap.start()
+    dswap.start()
     outs = []
     for i in range(1, 4):
         peer = flip(blk, 2 * i)
@@ -1248,6 +1215,13 @@
         product = jnp.transpose(grad) * mixed[z]
         queries[2 * z] = jnp.where(left, flat, 0.0).astype(BF)
         queries[2 * z + 1] = jnp.where(left, pltpu.roll(flat, 64, 1), 0.0).astype(BF)
+        turned = jnp.transpose(flat)
+        slopes = jnp.transpose(grad)
+        blank = jnp.zeros((64, 256), F32)
+        for side in range(2):
+            rows = slice(64 * side, 64 * side + 64)
+            queries_t[2 * z + side] = jnp.concatenate([turned[rows], blank], axis=0).astype(BF)
+            grads_t[2 * z + side] = jnp.concatenate([blank, slopes[rows]], axis=0).astype(BF)
         grads[2 * z] = jnp.where(left, 0.0, pltpu.roll(grad, 64, 1)).astype(BF)
         grads[2 * z + 1] = jnp.where(left, 0.0, grad).astype(BF)
         for side in range(2):
@@ -1274,12 +1248,15 @@
 
         def query_step(q, inner):
             query, grad = queries[q], grads[q]
+            query_t, grad_t = queries_t[q], grads_t[q]
             shift, delta = stats[q, 0:1, :], stats[q, 1:2, :]
             dq = dqt[q]
             for c in range(2):
                 keys = tiles[z, 4 * c : 4 * c + 4, 0:64, :].reshape(256, 128)
-                probs = jnp.exp2(contract_cols(keys, query) * EXP_SCALE - shift)
-                slopes = (probs * (contract_cols(keys, grad) - delta)).astype(BF)
+                probs = jnp.dot(keys, query_t, preferred_element_type=F32)
+                probs = jnp.exp2(probs * EXP_SCALE - shift)
+                slopes = jnp.dot(keys, grad_t, preferred_element_type=F32)
+                slopes = (probs * (slopes - delta)).astype(BF)
                 dkv[c] += jnp.dot(slopes, query, preferred_element_type=F32) + jnp.dot(
                     probs.astype(BF), grad, preferred_element_type=F32
                 )
@@ -1303,6 +1280,7 @@
         @pl.when(z == 1)
         def _():
             uswap.relay()
+            dswap.relay()
 
         @pl.when(z == 2)
         def _():
@@ -1336,6 +1314,8 @@
     usum[...] = sum_four(uin).astype(BF)
     vswap.start()
     up_own[blk] = usum[blk]
+    dswap.arrive()
+    down_own[...] = sum_four(din)
     xswap.arrive()
     out_own[...] = sum_four(zin)
     vswap.arrive()
@@ -1346,30 +1326,34 @@
         kv_move(z).drain()
     for copy in outs:
         copy.wait_send()
-    for copies in (scatter, uswap, vswap, xswap, qmove):
+    for copies in (dswap, scatter, uswap, vswap, xswap, qmove):
         copies.drain()
 
 
-def phase_four_kernel(tiles, grad_rx, mixed, lse, outq, middle, grad_up, grad_out):
+def phase_four_kernel(tiles, grad_rx, mixed, lse, outq, middle, grad_down, grad_up, grad_out):
     dma = pltpu.SemaphoreType.DMA
     return pl.pallas_call(
         fourth_kernel,
         out_shape=(
             jax.ShapeDtypeStruct((8, 4, 96, 128), BF),
             jax.ShapeDtypeStruct((128, 1024), BF),
+            jax.ShapeDtypeStruct((128, 1024), F32),
             jax.ShapeDtypeStruct((8, 32, 512), BF),
             jax.ShapeDtypeStruct((32, 1024), F32),
         ),
-        in_specs=whole(8),
-        out_specs=whole(4),
+        in_specs=whole(9),
+        out_specs=whole(5),
         scratch_shapes=[
             pltpu.VMEM((8, 256, 128), BF),
             pltpu.VMEM((8, 256, 128), BF),
+            pltpu.VMEM((8, 128, 256), BF),
+            pltpu.VMEM((8, 128, 256), BF),
             pltpu.VMEM((8, 8, 256), F32),
             pltpu.VMEM((64, 2048), BF),
             pltpu.VMEM((2, 256, 128), F32),
             pltpu.VMEM((8, 64, 256), F32),
             pltpu.VMEM((8, 4, 96, 128), BF),
+            pltpu.VMEM((4, 128, 1024), BF),
             pltpu.VMEM((4, 128, 1024), BF),
             pltpu.VMEM((4, 8, 32, 512), BF),
             pltpu.VMEM((8, 32, 512), BF),
@@ -1378,8 +1362,11 @@
             pltpu.VMEM((4, 4, 32, 1024), BF),
             pltpu.VMEM((4, 32, 1024), BF),
             pltpu.VMEM((4, 32, 1024), BF),
+            pltpu.VMEM((128, 1024), BF),
+            pltpu.VMEM((128, 1024), BF),
             pltpu.VMEM((8, 32, 512), BF),
             pltpu.VMEM((8, 32, 512), BF),
+            dma((2, 4)),
             dma((2, 4)),
             dma((2, 4)),
             dma((2, 8)),
@@ -1391,7 +1378,7 @@
             collective_id=3, has_side_effects=True, vmem_limit_bytes=56 << 20
         ),
         name="fourth",
-    )(tiles, grad_rx, mixed, lse, outq, middle, grad_up, grad_out)
+    )(tiles, grad_rx, mixed, lse, outq, middle, grad_down, grad_up, grad_out)
 def fifth_kernel(
     back, tabg, normed, wq, tokg, scales, grad_middle, sums, ttab, tix,
     grad_tokens, gq, grad_attn, grad_mlp,
@@ -1551,23 +1538,21 @@
     wq_parts = jnp.concatenate([kv_cols, wide[:, 0].reshape(32, 4, 256)], axis=-1)
     wq_parts = jnp.swapaxes(wq_parts, 0, 1)
     up_parts = jnp.transpose(w_up.reshape(32, 4, 8, 128), (2, 0, 1, 3)).reshape(8, 32, 512)
-    flat_tokens = tokens.reshape(128, 1024)
-    tiles, normed, wq, scales, table_all, upz, outz, tokens_all = phase_one_kernel(
-        tokens, table, wq_parts, time_table, time_index, scale_attn, scale_mlp, up_parts, w_out
-    )
-    mixed, lse, received, up, down, out, cot_all = phase_two_kernel(
-        tiles, upz, w_down, outz, cotangent.reshape(128, 1024)
-    )
-    grad_rx, grad_middle, middle, outq, down_own, grad_up, grad_out, sums = phase_three_kernel(
-        received, flat_tokens, out, up, down, cot_all, scales
-    )
-    back, output, up_own, out_own = phase_four_kernel(
+    (
+        tiles, normed, wq, scales, table_all, tokens_all, mixed, lse,
+        grad_rx, grad_middle, middle, outq, grad_down, grad_up, grad_out, sums,
+    ) = front(
+        tokens, table, wq_parts, time_table, (scale_attn, scale_mlp), up_parts, w_out,
+        w_down, cotangent.reshape(128, 1024), time_index,
+    )
+    back, output, down_own, up_own, out_own = phase_four_kernel(
         tiles,
         grad_rx,
         mixed,
         lse,
         outq,
         middle,
+        grad_down,
         grad_up,
         grad_out.reshape(4, 4, 2, 32, 1024),
     )

time: 246 us -> 220 us (0.89)
  Pallas kernels: 230 us -> 204 us
    pallas_call x3 -> x1, Pallas kernels: 153 us -> 121 us  [front(): pl.pallas_call(front_kernel, out_shape=(shape((4, 8, 96, 128), BF), shape...]
    pallas_call x1, Pallas kernels: 47.2 us -> 51.1 us  [phase_four_kernel(): pl.pallas_call(fourth_kernel, out_shape=(jax.ShapeDtypeStruct((8, 4, 96,...]
    unnamed x48 -> x40, local copies, waits for them, and re-layouts: 9.81 us -> 7.5 us
where the time goes in v5:
time: 220 us
  Pallas kernels  204 us (93%)
  local copies, waits for them, and re-layouts  12.5 us (6%)
  other arithmetic  2.63 us (1%)
    pallas_call x1, Pallas kernels, front(): pl.pallas_call(front_kernel, out_shape=(shape((4, 8, 96, 128), BF), shape...  121 us
    pallas_call x1, Pallas kernels, phase_four_kernel(): pl.pallas_call(fourth_kernel, out_shape=(jax.ShapeDtypeStruct((8, 4, 96,...  51.1 us
    pallas_call x1, Pallas kernels, phase_five_kernel(): pl.pallas_call(fifth_kernel, out_shape=(jax.ShapeDtypeStruct((128, 1024),...  31.2 us
    unnamed x40, local copies, waits for them, and re-layouts  7.5 us

profile of v5, /device:TPU:0, one launch (start us, length us, event | category | flops | bytes accessed | tf_op | source)
XLA Modules:
  0.0 219.9 jit_solution(15396640324783387742)
XLA Ops:
  0.6 0.0 copy-start.13
  0.7 0.7 convert_element_type.24
  1.4 0.3 multiply_cosine_fusion
  1.7 0.7 pad_maximum_fusion.1.tab
  2.4 1.0 copy.46
  3.4 0.1 copy.55
  3.5 0.8 reshape.86.upp
  4.3 0.0 copy-done.13
  4.3 0.3 reshape.83
  4.6 0.1 fusion
  4.8 0.1 copy_bitcast_fusion.4
  4.8 0.1 pad_maximum_fusion
  4.9 0.2 copy.35
  5.1 0.2 reshape.84
  5.3 0.2 reshape.95
  5.5 0.7 maximum_bitcast_fusion.wqp
  6.2 121.4 %front.1 = (bf16[4,8,96,128]{3,2,1,0:T(8,128)(2,1)}, bf16[4,128,1024]{2,1,0:T(8,128)(2,1)}, bf16[4,8,32,768]{3,2,1,0:T(8,128)(2,1)}, f32[8,1024]{1,0:T(8,128)}, ...) custom-call(bf16[2,64,1024]{2,1,0:T(8,128)(2,1)} %tok.1, ...), custom_call_target="tpu_custom_call" | custom-call | tf_op jit(solution)/shard_map/front/pallas_call | solution.py:1053
  127.6 0.0 copy-start
  127.6 0.0 copy-start.1
  127.6 0.0 copy-start.2
  127.6 0.0 copy-start.4
  127.6 0.0 copy-start.5
  127.7 0.0 copy-start.6
  127.7 0.0 copy-start.7
  127.7 0.0 copy-start.8
  127.7 0.0 copy-start.9
  127.7 51.1 %fourth.1 = (bf16[8,4,96,128]{3,2,1,0:T(8,128)(2,1)}, bf16[128,1024]{1,0:T(8,128)(2,1)}, f32[128,1024]{1,0:T(8,128)}, bf16[8,32,512]{2,1,0:T(8,128)(2,1)}, f32[32,1024]{1,0:T(8,128)}) custom-call(bf16[4,8,96,128]{3,2,1,0:T(8,128)(2,1)} %get-tuple-element.33.tiles, bf16[4,8,32,128]{3,2,1,0:T(8,128)(2,1)} %get-tuple-element.34.grad_rx, ...), custom_call_target="tpu_custom_call" | custom-call | tf_op jit(solution)/shard_map/fourth/pallas_call | solution.py:1335
  178.8 0.0 copy-done
  178.9 0.0 copy-done.1
  178.9 0.0 copy-done.2
  178.9 0.0 copy-done.4
  178.9 0.0 copy-done.5
  178.9 0.0 copy-done.6
  178.9 0.0 copy-done.7
  178.9 0.0 copy-done.8
  178.9 0.0 copy-done.9
  178.9 0.0 copy-start.3
  178.9 1.1 copy-done.3
  180.1 31.2 %fifth.1 = (f32[128,1024]{1,0:T(8,128)S(1)}, bf16[4,32,768]{2,1,0:T(8,128)(2,1)S(1)}, f32[8,1024]{1,0:T(8,128)S(1)}, f32[8,1024]{1,0:T(8,128)S(1)}) custom-call(bf16[8,4,96,128]{3,2,1,0:T(8,128)(2,1)S(1)} %copy-done.3, f32[4,64,128]{2,1,0:T(8,128)S(1)} %copy-done.6, bf16[4,128,1024]{2,1,0:T(8,128)(2,1)S(1)} %copy-done.1, ...), custom_call_target="tpu_custom_call" | custom-call | tf_op jit(solution)/shard_map/fifth/pallas_call | solution.py:1483
  211.3 0.1 stack_reshape.3
  211.5 0.2 reshape.91
  211.7 0.4 fusion.1
  212.1 0.0 copy-start.11
  212.1 0.1 convert_bitcast_fusion
  212.2 0.5 copy.41
  212.8 0.0 copy-start.12
  212.8 1.3 reshape.92
  214.1 0.0 copy-done.11
  214.1 0.0 copy-start.14
  214.1 0.2 reshape.94
  214.3 0.0 copy-start.10
  214.3 0.3 copy.42
  214.6 1.1 copy.54
  215.7 0.0 copy-done.12
  215.7 0.7 copy.64
  216.4 0.8 copy.65
  217.2 0.0 copy-done.14
  217.2 0.7 copy.66
  217.9 0.0 copy-done.10
  217.9 0.8 copy.67
  218.7 0.6 copy.68
  219.3 0.6 copy.69
  (8 shorter events, 0.1 us)
Async XLA Ops:
  0.6 3.7 %copy-start.13 = (bf16[32,3072]{1,0:T(8,128)(2,1)S(1)}, bf16[32,3072]{1,0:T(8,128)(2,1)}, u32[]{:S(2)}) copy-start(bf16[32,3072]{1,0:T(8,128)(2,1)} %param.15) | copy-start | bytes 589828
  127.6 51.2 %copy-start = (bf16[4,8,32,768]{3,2,1,0:T(8,128)(2,1)S(1)}, bf16[4,8,32,768]{3,2,1,0:T(8,128)(2,1)}, u32[]{:S(2)}) copy-start(bf16[4,8,32,768]{3,2,1,0:T(8,128)(2,1)} %get-tuple-element.46.wq) | copy-start | bytes 4718596
  127.6 51.2 %copy-start.1 = (bf16[4,128,1024]{2,1,0:T(8,128)(2,1)S(1)}, bf16[4,128,1024]{2,1,0:T(8,128)(2,1)}, u32[]{:S(2)}) copy-start(bf16[4,128,1024]{2,1,0:T(8,128)(2,1)} %get-tuple-element.45.normed) | copy-start | bytes 3145732
  127.6 51.2 %copy-start.2 = (bf16[4,2,64,1024]{3,2,1,0:T(8,128)(2,1)S(1)}, bf16[4,2,64,1024]{3,2,1,0:T(8,128)(2,1)}, u32[]{:S(2)}) copy-start(bf16[4,2,64,1024]{3,2,1,0:T(8,128)(2,1)} %get-tuple-element.47.tokg) | copy-start | bytes 3145732
  127.6 51.2 %copy-start.4 = (f32[128,1024]{1,0:T(8,128)S(1)}, f32[128,1024]{1,0:T(8,128)}, u32[]{:S(2)}) copy-start(f32[128,1024]{1,0:T(8,128)} %get-tuple-element.49.grad_middle) | copy-start | bytes 1572868
  127.6 51.2 %copy-start.5 = (f32[64,256]{1,0:T(8,128)S(1)}, f32[64,256]{1,0:T(8,128)}, u32[]{:S(2)}) copy-start(f32[64,256]{1,0:T(8,128)} %ttab.3) | copy-start | bytes 196612
  127.7 51.2 %copy-start.6 = (f32[4,64,128]{2,1,0:T(8,128)S(1)}, f32[4,64,128]{2,1,0:T(8,128)}, u32[]{:S(2)}) copy-start(f32[4,64,128]{2,1,0:T(8,128)} %get-tuple-element.44.tabg) | copy-start | bytes 393220
  127.7 51.2 %copy-start.7 = (f32[8,1024]{1,0:T(8,128)S(1)}, f32[8,1024]{1,0:T(8,128)}, u32[]{:S(2)}) copy-start(f32[8,1024]{1,0:T(8,128)} %get-tuple-element.48.scales) | copy-start | bytes 98308
  127.7 51.2 %copy-start.8 = (f32[8,1024]{1,0:T(8,128)S(1)}, f32[8,1024]{1,0:T(8,128)}, u32[]{:S(2)}) copy-start(f32[8,1024]{1,0:T(8,128)} %get-tuple-element.50.sums) | copy-start | bytes 98308
  127.7 51.2 %copy-start.9 = (s32[2]{0:T(128)S(1)}, s32[2]{0:T(128)}, u32[]{:S(2)}) copy-start(s32[2]{0:T(128)} %tix.3) | copy-start | bytes 28
  178.9 1.1 copy-start.3
  212.1 2.0 copy-start.11
  212.8 2.9 %copy-start.12 = (bf16[128,1024]{1,0:T(8,128)(2,1)S(1)}, bf16[128,1024]{1,0:T(8,128)(2,1)}, u32[]{:S(2)}) copy-start(bf16[128,1024]{1,0:T(8,128)(2,1)} %get-tuple-element.42) | copy-start | bytes 786436
  214.1 3.1 %copy-start.14 = (f32[32,1024]{1,0:T(8,128)S(1)}, f32[32,1024]{1,0:T(8,128)}, u32[]{:S(2)}) copy-start(f32[32,1024]{1,0:T(8,128)} %get-tuple-element.84) | copy-start | bytes 393220
  214.3 3.6 %copy-start.10 = (f32[128,1024]{1,0:T(8,128)S(1)}, f32[128,1024]{1,0:T(8,128)}, u32[]{:S(2)}) copy-start(f32[128,1024]{1,0:T(8,128)} %get-tuple-element.86) | copy-start | bytes 1572868

commit v6 on v5

--- a/solution.py
+++ b/solution.py
@@ -673,9 +673,14 @@
 class Everyone:
     def __init__(self, head, blk, source, target, sems):
         self.head, self.blk, self.source, self.target, self.sems = head, blk, source, target, sems
+        self.peers = [flip(blk, k) for k in range(8)]
 
     def copy(self, kz, k):
-        z, b = flip_by(self.head, jnp.int32(kz)), flip(self.blk, k)
+        z = flip_by(self.head, jnp.int32(kz))
+        return self.copy_to(z, kz, k)
+
+    def copy_to(self, z, kz, k):
+        b = self.peers[k]
         return send(
             self.source(z, b),
             self.target(self.head, self.blk),
@@ -686,22 +691,24 @@
         )
 
     def start(self, kz):
-        if isinstance(kz, int):
-            first = kz > 0
-        else:
-
-            @pl.when(kz > 0)
-            def _():
-                self.copy(kz, 0).start()
-
-            first = False
-        for k in range(0 if first else 1, 8):
-            self.copy(kz, k).start()
-
-    def arrive(self):
-        for kz in range(4):
-            for k in range(1 if kz == 0 else 0, 8):
-                self.copy(kz, k).wait_recv()
+        z = flip_by(self.head, jnp.int32(kz))
+
+        @pl.when(kz > 0)
+        def _():
+            self.copy_to(z, kz, 0).start()
+
+        for k in range(1, 8):
+            self.copy_to(z, kz, k).start()
+
+    def arrive(self, kz):
+        z = flip_by(self.head, jnp.int32(kz))
+
+        @pl.when(kz > 0)
+        def _():
+            self.copy_to(z, kz, 0).wait_recv()
+
+        for k in range(1, 8):
+            self.copy_to(z, kz, k).wait_recv()
 
     def drain(self):
         for kz in range(4):
@@ -724,14 +731,77 @@
     return jnp.sum(value.reshape(value.shape[0] // 8, 8, value.shape[1]), axis=0)
 
 
-def front_kernel(
+VMEM_LIMIT = 61 << 20
+
+
+class Scatter:
+    def __init__(self, head, blk, terms, near, joined, far, sems):
+        self.head, self.blk, self.core = head, blk, lax.rem(blk, 2)
+        self.terms, self.near, self.joined, self.far, self.sems = terms, near, joined, far, sems
+
+    def halves(self):
+        return send(
+            self.terms.at[:, :, 1 - self.core],
+            self.near,
+            self.sems.at[0, 0],
+            self.sems.at[1, 0],
+            self.head,
+            flip(self.blk, 1),
+        )
+
+    def chips(self, i):
+        peer = flip(self.blk, 2 * i)
+        return send(
+            self.joined.at[lax.div(peer, 2)],
+            self.far.at[i],
+            self.sems.at[0, i],
+            self.sems.at[1, i],
+            self.head,
+            peer,
+        )
+
+    def start(self):
+        self.halves().start()
+
+    def join(self):
+        self.halves().wait_recv()
+        for chip in range(4):
+            mine = self.terms[:, chip, pl.ds(self.core, 1)].astype(F32)
+            mine = mine.reshape(mine.shape[0], *mine.shape[2:])
+            self.joined[chip] = (mine + self.near[:, chip].astype(F32)).astype(BF)
+        for i in (3, 1, 2):
+            self.chips(i).start()
+
+    def total(self):
+        value = self.joined[lax.div(self.blk, 2)].astype(F32)
+        for i in range(1, 4):
+            self.chips(i).wait_recv()
+            value = value + self.far[i].astype(F32)
+        return value
+
+    def drain(self):
+        self.halves().wait_send()
+        for i in range(1, 4):
+            self.chips(i).wait_send()
+
+
+def sum_four(parts):
+    return (parts[0].astype(F32) + parts[1].astype(F32)) + (
+        parts[2].astype(F32) + parts[3].astype(F32)
+    )
+
+
+def layer_kernel(
     tok, tab, wqp, ttab, sca, scm, upp, out_own, down_own, cot_own, tix,
-    tiles, normed, wq, scales, tabg, tokg, mixed, lse,
-    grad_rx, grad_middle, middle, outq, grad_down, grad_up, grad_out, sums,
-    wqz, turned, part, sums_in, parts, out_tiles, upz, outz, up, down, out, cots,
-    kvt, scores, att, received, attended, n2g, act, gh, pairs, prx, gsend, gin, tsend, branch,
-    zsem, lsem, tsem, wsem, asem, bsem, psem, usem, osem,
-    usem2, dsem, qsem, csem, esem, nsem, ssem, gsem, fsem,
+    output, g_down, g_up, g_out, grad_tokens, gq, grad_attn, grad_mlp,
+    tiles, normed, wq, scales, tabg, tokg, mixed, lse, grad_rx, grad_middle, middle, outq, grad_down,
+    grad_up, grad_out, sums, wqz, turned, part, sums_in, parts, out_tiles, upz, outz, up, down, out, cots,
+    kvt, scores, att, received, attended, n2g, act, gh, pairs, prx, gsend, gin, tsend, branch, queries,
+    grads, queries_t, grads_t, stats, keyt, dkv, dqt, bsend, back, oin, din, dvia, djoin, uin, uvia, ujoin,
+    usum, near, joined, far, osum, zin, gp, gnp, gvia, gjoin, gin_r, terms, near_q, joined_q, far_q, osum_q,
+    part_r, sums_in_r, parts_r, zsem, lsem, tsem, wsem, asem, bsem, psem, usem, osem, usem2, dsem, qsem,
+    csem, esem, nsem, ssem, gsem, fsem, qsem_r, dsem_r, usem_r, vsem, osem_r, xsem, bsem_r, gsem_r, osem_q,
+    xsem_q, asem_r, csem_r,
 ):
     head, blk = lax.axis_index("head"), lax.axis_index("blk")
     core = lax.rem(blk, 2)
@@ -753,12 +823,12 @@
     turned[...] = jnp.transpose(ttab[...])
     rows = turned[pl.ds(pl.multiple_of((head * 8 + blk) * 8, 8), 8), :]
     step_lane = lax.broadcasted_iota(jnp.int32, rows.shape, 1)
-    terms = []
+    pieces = []
     for weight in (sca, scm):
         for seq in range(2):
             column = jnp.sum(jnp.where(step_lane == tix[seq], rows, 0.0), axis=1, keepdims=True)
-            terms.append(jnp.sum(column * weight[...].astype(F32), axis=0, keepdims=True))
-    part[...] = jnp.concatenate(terms + [jnp.zeros((4, 1024), F32)], axis=0)
+            pieces.append(jnp.sum(column * weight[...].astype(F32), axis=0, keepdims=True))
+    part[...] = jnp.concatenate(pieces + [jnp.zeros((4, 1024), F32)], axis=0)
     one = Swap(head, blk, "blk", lambda i: part, lambda i: sums_in.at[i], asem)
     one.start()
     uswap.start()
@@ -907,20 +977,21 @@
     dline.step(line_order(head, jnp.int32(1)))
     for i in range(-1, 3):
         oplane.arrive(i)
-    everyone.arrive()
-    for seq in range(2):
-        for group in range(4):
+    middle[...] = tok[...].astype(F32).reshape(128, 1024)
+    for kz in range(4):
+        group = flip(head, kz)
+        everyone.arrive(kz)
+        for seq in range(2):
             for i in range(2):
                 first = received[group, 4 * seq + 2 * i].astype(F32)
                 second = received[group, 4 * seq + 2 * i + 1].astype(F32)
-                lanes = slice(256 * group + 128 * i, 256 * group + 128 * i + 128)
-                attended[64 * seq : 64 * seq + 32, lanes] = join_halves(first, second, 0).astype(BF)
-                attended[64 * seq + 32 : 64 * seq + 64, lanes] = join_halves(
-                    first, second, 1
-                ).astype(BF)
-    middle[...] = tok[...].astype(F32).reshape(128, 1024) + jnp.dot(
-        attended[...], out[...].reshape(1024, 1024), preferred_element_type=F32
-    )
+                lanes = slice(128 * i, 128 * i + 128)
+                for right in range(2):
+                    at = slice(64 * seq + 32 * right, 64 * seq + 32 * right + 32)
+                    attended[group, at, lanes] = join_halves(first, second, right).astype(BF)
+        middle[...] += jnp.dot(
+            attended[group], out[group].reshape(256, 1024), preferred_element_type=F32
+        )
     for seq in range(2):
         rows = slice(64 * seq, 64 * seq + 64)
         unit, _ = norm_stats(middle[rows, :])
@@ -991,8 +1062,19 @@
         ).astype(BF)
     for group in range(4):
         lanes = slice(256 * group, 256 * group + 256)
-        part = contract_rows(n2g[:, :, lanes].reshape(1024, 256), gh[...].reshape(1024, 512))
-        grad_up[group] = part.astype(BF).reshape(8, 32, 512)
+        value = contract_rows(n2g[:, :, lanes].reshape(1024, 256), gh[...].reshape(1024, 512))
+        grad_up[group] = value.astype(BF).reshape(8, 32, 512)
+    uswap_r = Fold(head, blk, grad_up, uvia, ujoin, uin, usem_r)
+    dfold = Fold(head, blk, grad_down, dvia, djoin, din, dsem_r)
+    folds = (uswap_r, dfold)
+    for fold in folds:
+        fold.start_far()
+        fold.start_one(3)
+
+        @pl.when(fold.middle)
+        def _():
+            fold.copy(1).start()
+
     for i in range(1, 4):
         onward(i).wait_recv()
     sums[...] = jnp.zeros_like(sums)
@@ -1011,12 +1093,12 @@
 
     def give(step, carry):
         group = flip_by(head, 3 - step)
-        part = contract_cols(branch[...], out[group].reshape(256, 1024))
+        value = contract_cols(branch[...], out[group].reshape(256, 1024))
         for seq in range(2):
             for i in range(2):
                 lanes = slice(128 * i, 128 * i + 128)
-                top = part[64 * seq : 64 * seq + 32, lanes]
-                bottom = part[64 * seq + 32 : 64 * seq + 64, lanes]
+                top = value[64 * seq : 64 * seq + 32, lanes]
+                bottom = value[64 * seq + 32 : 64 * seq + 64, lanes]
                 for right in range(2):
                     tsend[group, 4 * seq + 2 * i + right] = join_halves(top, bottom, right).astype(BF)
         backward.start(3 - step)
@@ -1025,186 +1107,17 @@
     lax.fori_loop(0, 4, give, 0)
     grad_rx[head, blk] = tsend[head, blk]
     for group in range(4):
-        lanes = slice(256 * group, 256 * group + 256)
-        part = contract_rows(attended[:, lanes], branch[...])
-        grad_out[group] = part.astype(BF).reshape(8, 32, 1024)
-    backward.arrive()
-    for at in range(4):
-        move(at).drain()
-    for i in range(4):
-        for copy in halves(i):
-            copy.wait_send()
-        if i:
-            onward(i).wait_send()
-    for copies in (
-        zswap, line, tline, plane, one, two, uswap, oline,
-        uline, dline, oplane, cplane, everyone, nplane, backward,
-    ):
-        copies.drain()
-
-
-def whole(count):
-    return [pl.BlockSpec(memory_space=pltpu.VMEM)] * count
-
-
-def front(tokens, table, wq_parts, time_table, scales_in, up_parts, w_out, w_down, cot, time_index):
-    dma = pltpu.SemaphoreType.DMA
-    shape = jax.ShapeDtypeStruct
-    return pl.pallas_call(
-        front_kernel,
-        out_shape=(
-            shape((4, 8, 96, 128), BF),
-            shape((4, 128, 1024), BF),
-            shape((4, 8, 32, 768), BF),
-            shape((8, 1024), F32),
-            shape((4, 64, 128), F32),
-            shape((4, 2, 64, 1024), BF),
-            shape((4, 128, 256), F32),
-            shape((4, 8, 256), F32),
-            shape((4, 8, 32, 128), BF),
-            shape((128, 1024), F32),
-            shape((128, 1024), F32),
-            shape((4, 128, 1024), BF),
-            shape((4, 128, 1024), BF),
-            shape((4, 8, 32, 512), BF),
-            shape((4, 8, 32, 1024), BF),
-            shape((8, 1024), F32),
-        ),
-        in_specs=whole(10) + [pl.BlockSpec(memory_space=pltpu.SMEM)],
-        out_specs=whole(16),
-        scratch_shapes=[
-            pltpu.VMEM((4, 32, 768), BF),
-            pltpu.VMEM((256, 64), F32),
-            pltpu.VMEM((8, 1024), F32),
-            pltpu.VMEM((8, 8, 1024), F32),
-            pltpu.VMEM((4, 8, 1024), F32),
-            pltpu.VMEM((8, 4, 96, 128), BF),
-            pltpu.VMEM((8, 32, 512), BF),
-            pltpu.VMEM((4, 32, 1024), BF),
-            pltpu.VMEM((4, 8, 32, 512), BF),
-            pltpu.VMEM((4, 128, 1024), BF),
-            pltpu.VMEM((4, 8, 32, 1024), BF),
-            pltpu.VMEM((8, 128, 1024), BF),
-            pltpu.VMEM((128, 2048), BF),
-            pltpu.VMEM((2, 2048 // KEYS, KEYS, 256), F32),
-            pltpu.VMEM((4, 8, 32, 128), BF),
-            pltpu.VMEM((4, 8, 32, 128), BF),
-            pltpu.VMEM((128, 1024), BF),
-            pltpu.VMEM((8, 128, 1024), BF),
-            pltpu.VMEM((8, 128, 512), BF),
-            pltpu.VMEM((8, 128, 512), BF),
-            pltpu.VMEM((2, 4, 2, 128, 1024), BF),
-            pltpu.VMEM((2, 4, 128, 1024), BF),
-            pltpu.VMEM((4, 128, 1024), BF),
-            pltpu.VMEM((4, 128, 1024), BF),
-            pltpu.VMEM((4, 8, 32, 128), BF),
-            pltpu.VMEM((128, 1024), BF),
-            dma((2, 4)),
-            dma((2, 2, 3)),
-            dma((2, 2, 3)),
-            dma((2, 7)),
-            dma((2, 8)),
-            dma((2, 4)),
-            dma((4, 2, 8)),
-            dma((2, 8)),
-            dma((2, 4)),
-            dma((2, 2, 3)),
-            dma((2, 2, 3)),
-            dma((2, 7)),
-            dma((2, 7)),
-            dma((2, 4, 8)),
-            dma((2, 7)),
-            dma((2, 2, 4)),
-            dma((2, 4)),
-            dma((2, 4, 8)),
-        ],
-        compiler_params=pltpu.CompilerParams(
-            collective_id=0, has_side_effects=True, vmem_limit_bytes=56 << 20
-        ),
-        name="front",
-    )(tokens, table, wq_parts, time_table, *scales_in, up_parts, w_out, w_down, cot, time_index)
-
-
-class Scatter:
-    def __init__(self, head, blk, terms, near, joined, far, sems):
-        self.head, self.blk, self.core = head, blk, lax.rem(blk, 2)
-        self.terms, self.near, self.joined, self.far, self.sems = terms, near, joined, far, sems
-
-    def halves(self):
-        return send(
-            self.terms.at[:, :, 1 - self.core],
-            self.near,
-            self.sems.at[0, 0],
-            self.sems.at[1, 0],
-            self.head,
-            flip(self.blk, 1),
-        )
-
-    def chips(self, i):
-        peer = flip(self.blk, 2 * i)
-        return send(
-            self.joined.at[lax.div(peer, 2)],
-            self.far.at[i],
-            self.sems.at[0, i],
-            self.sems.at[1, i],
-            self.head,
-            peer,
-        )
-
-    def start(self):
-        self.halves().start()
-
-    def join(self):
-        self.halves().wait_recv()
-        for chip in range(4):
-            mine = self.terms[:, chip, pl.ds(self.core, 1)].astype(F32)
-            mine = mine.reshape(mine.shape[0], *mine.shape[2:])
-            self.joined[chip] = (mine + self.near[:, chip].astype(F32)).astype(BF)
-        for i in (3, 1, 2):
-            self.chips(i).start()
-
-    def total(self):
-        value = self.joined[lax.div(self.blk, 2)].astype(F32)
-        for i in range(1, 4):
-            self.chips(i).wait_recv()
-            value = value + self.far[i].astype(F32)
-        return value
-
-    def drain(self):
-        self.halves().wait_send()
-        for i in range(1, 4):
-            self.chips(i).wait_send()
-
-
-def sum_four(parts):
-    return (parts[0].astype(F32) + parts[1].astype(F32)) + (
-        parts[2].astype(F32) + parts[3].astype(F32)
-    )
-
-
-def fourth_kernel(
-    tiles, grad_rx, mixed, lse, outq, middle, grad_down, grad_up, grad_out,
-    back, output, down_own, up_own, out_own,
-    queries, grads, queries_t, grads_t, stats, keyt, dkv, dqt, bsend, oin, din, uin, usum, near, joined, far, osum, zin,
-    dvia, djoin, uvia, ujoin,
-    qsem, dsem, usem, vsem, osem, xsem, bsem,
-):
-    head, blk = lax.axis_index("head"), lax.axis_index("blk")
-    greet(head, blk, (1, 2, 3), range(1, 8))
-    scatter = Scatter(head, blk, grad_out, near, joined, far, osem)
+        value = contract_rows(attended[group], branch[...])
+        grad_out[group] = value.astype(BF).reshape(4, 2, 32, 1024)
+    scatter = Scatter(head, blk, grad_out, near, joined, far, osem_r)
     scatter.start()
-    dswap = Fold(head, blk, grad_down, dvia, djoin, din, dsem)
-    uswap = Fold(head, blk, grad_up, uvia, ujoin, uin, usem)
-    uswap.start()
-    dswap.start()
     outs = []
     for i in range(1, 4):
         peer = flip(blk, 2 * i)
         outs.append(
-            send(outq.at[lax.div(peer, 2)], oin.at[i], qsem.at[0, i], qsem.at[1, i], head, peer)
-        )
-        outs[-1].start()
-    vswap = Swap(head, blk, "blk", lambda i: usum.at[i], lambda i: up_own.at[i], vsem)
+            send(outq.at[lax.div(peer, 2)], oin.at[i], qsem_r.at[0, i], qsem_r.at[1, i], head, peer)
+        )
+    vswap = Swap(head, blk, "blk", lambda i: usum.at[i], lambda i: g_up.at[i], vsem)
     xswap = Swap(head, blk, "head", lambda i: osum.at[i], lambda i: zin.at[i], xsem)
     left = half_lane((256, 128))
     keyt[...] = jnp.transpose(tiles[:, :, 0:64, :].reshape(2048, 128))[:64]
@@ -1230,7 +1143,12 @@
             stats[2 * z + side] = jnp.concatenate([shift, delta, jnp.zeros((6, 256), F32)], axis=0)
         return carry
 
-    lax.fori_loop(0, 4, prepare, 0)
+    def ready(kz, carry):
+        backward.arrive(kz)
+        return prepare(flip_by(head, kz), carry)
+
+    scatter.join()
+    lax.fori_loop(0, 4, ready, 0)
     dqt[...] = jnp.zeros_like(dqt)
 
     def kv_move(z):
@@ -1240,7 +1158,7 @@
             "blk",
             lambda i: bsend.at[i, z, pl.ds(0, 64)],
             lambda i: back.at[i, z, pl.ds(0, 64)],
-            bsem.at[z],
+            bsem_r.at[z],
         )
 
     def keys_step(z, carry):
@@ -1275,20 +1193,24 @@
 
         @pl.when(z == 0)
         def _():
-            scatter.join()
+            for fold in folds:
+                fold.start_one(2)
 
         @pl.when(z == 1)
         def _():
-            uswap.relay()
-            dswap.relay()
+            for fold in folds:
+                fold.relay()
+            for copy in outs:
+                copy.start()
 
         @pl.when(z == 2)
         def _():
-            total = middle[...] + outq[lax.div(blk, 2)].astype(F32)
-            for i in range(1, 4):
-                outs[i - 1].wait_recv()
-                total = total + oin[i].astype(F32)
-            output[...] = total.astype(BF)
+            for fold in folds:
+
+                @pl.when(jnp.logical_not(fold.middle))
+                def _():
+                    fold.copy(1).start()
+
             osum[...] = scatter.total().astype(BF)
             xswap.start()
             zin[head] = osum[head]
@@ -1306,88 +1228,20 @@
         "blk",
         lambda i: bsend.at[i, :, pl.ds(64, 32)],
         lambda i: back.at[i, :, pl.ds(64, 32)],
-        bsem.at[4],
+        bsem_r.at[4],
     )
     qmove.start()
     back[blk] = bsend[blk]
-    uswap.arrive()
-    usum[...] = sum_four(uin).astype(BF)
-    vswap.start()
-    up_own[blk] = usum[blk]
-    dswap.arrive()
-    down_own[...] = sum_four(din)
-    xswap.arrive()
-    out_own[...] = sum_four(zin)
-    vswap.arrive()
+    picked = turned[pl.ds(pl.multiple_of((head * 8 + blk) * 8, 8), 8), :]
+    step_lane = lax.broadcasted_iota(jnp.int32, picked.shape, 1)
+    columns = [
+        jnp.sum(jnp.where(step_lane == tix[seq], picked, 0.0), axis=1, keepdims=True)
+        for seq in range(2)
+    ]
     for z in range(4):
         kv_move(z).arrive()
     qmove.arrive()
-    for z in range(4):
-        kv_move(z).drain()
-    for copy in outs:
-        copy.wait_send()
-    for copies in (dswap, scatter, uswap, vswap, xswap, qmove):
-        copies.drain()
-
-
-def phase_four_kernel(tiles, grad_rx, mixed, lse, outq, middle, grad_down, grad_up, grad_out):
-    dma = pltpu.SemaphoreType.DMA
-    return pl.pallas_call(
-        fourth_kernel,
-        out_shape=(
-            jax.ShapeDtypeStruct((8, 4, 96, 128), BF),
-            jax.ShapeDtypeStruct((128, 1024), BF),
-            jax.ShapeDtypeStruct((128, 1024), F32),
-            jax.ShapeDtypeStruct((8, 32, 512), BF),
-            jax.ShapeDtypeStruct((32, 1024), F32),
-        ),
-        in_specs=whole(9),
-        out_specs=whole(5),
-        scratch_shapes=[
-            pltpu.VMEM((8, 256, 128), BF),
-            pltpu.VMEM((8, 256, 128), BF),
-            pltpu.VMEM((8, 128, 256), BF),
-            pltpu.VMEM((8, 128, 256), BF),
-            pltpu.VMEM((8, 8, 256), F32),
-            pltpu.VMEM((64, 2048), BF),
-            pltpu.VMEM((2, 256, 128), F32),
-            pltpu.VMEM((8, 64, 256), F32),
-            pltpu.VMEM((8, 4, 96, 128), BF),
-            pltpu.VMEM((4, 128, 1024), BF),
-            pltpu.VMEM((4, 128, 1024), BF),
-            pltpu.VMEM((4, 8, 32, 512), BF),
-            pltpu.VMEM((8, 32, 512), BF),
-            pltpu.VMEM((4, 4, 32, 1024), BF),
-            pltpu.VMEM((4, 4, 32, 1024), BF),
-            pltpu.VMEM((4, 4, 32, 1024), BF),
-            pltpu.VMEM((4, 32, 1024), BF),
-            pltpu.VMEM((4, 32, 1024), BF),
-            pltpu.VMEM((128, 1024), BF),
-            pltpu.VMEM((128, 1024), BF),
-            pltpu.VMEM((8, 32, 512), BF),
-            pltpu.VMEM((8, 32, 512), BF),
-            dma((2, 4)),
-            dma((2, 4)),
-            dma((2, 4)),
-            dma((2, 8)),
-            dma((2, 4)),
-            dma((2, 4)),
-            dma((5, 2, 8)),
-        ],
-        compiler_params=pltpu.CompilerParams(
-            collective_id=3, has_side_effects=True, vmem_limit_bytes=56 << 20
-        ),
-        name="fourth",
-    )(tiles, grad_rx, mixed, lse, outq, middle, grad_down, grad_up, grad_out)
-def fifth_kernel(
-    back, tabg, normed, wq, tokg, scales, grad_middle, sums, ttab, tix,
-    grad_tokens, gq, grad_attn, grad_mlp,
-    gp, gnf, gnp, gvia, gjoin, gin, terms, near, joined, far, osum, turned, part, sums_in, parts,
-    gsem, osem, xsem, asem, bsem,
-):
-    head, blk = lax.axis_index("head"), lax.axis_index("blk")
-    greet(head, blk, (1, 2, 3), range(1, 8))
-    gswap = Fold(head, blk, gnp, gvia, gjoin, gin, gsem)
+    gswap = Fold(head, blk, gnp, gvia, gjoin, gin_r, gsem_r)
 
     def unturn(step, carry):
         at = flip(head, step)
@@ -1409,90 +1263,188 @@
                 )
                 query = query * both[0] + lane_swap(query) * both[1]
                 gp[at, rows, 512 + 128 * i : 640 + 128 * i] = query.astype(BF)
-        gnf[at] = contract_cols(gp[at], wq[...].reshape(1024, 768))
-        gnp[at] = gnf[at].astype(BF)
+        gnp[at] = contract_cols(gp[at], wq[...].reshape(1024, 768)).astype(BF)
         return carry
 
     for step in (3, 2, 1, 0):
         unturn(step, 0)
         if step == 3:
             gswap.start_far()
-        if step:
-            gswap.start_one(step)
+            gswap.start_one(3)
     for group in range(4):
         lanes = slice(256 * group, 256 * group + 256)
         value = contract_rows(normed[:, :, lanes].reshape(512, 256), gp[...].reshape(512, 768))
         terms[group] = value.astype(BF).reshape(4, 2, 32, 768)
-    scatter = Scatter(head, blk, terms, near, joined, far, osem)
-    scatter.start()
-    turned[...] = jnp.transpose(ttab[...])
-    picked = turned[pl.ds(pl.multiple_of((head * 8 + blk) * 8, 8), 8), :]
-    step_lane = lax.broadcasted_iota(jnp.int32, picked.shape, 1)
-    columns = [
-        jnp.sum(jnp.where(step_lane == tix[seq], picked, 0.0), axis=1, keepdims=True)
-        for seq in range(2)
-    ]
-    gswap.relay()
-    part[...] = jnp.concatenate(
+    scatter_q = Scatter(head, blk, terms, near_q, joined_q, far_q, osem_q)
+    scatter_q.start()
+    part_r[...] = jnp.concatenate(
         [jnp.zeros((2, 1024), F32), sums[0:2, :], jnp.zeros((4, 1024), F32)], axis=0
     )
 
-    def gather(at, carry):
+    def gather_r(at, carry):
         for seq in range(2):
             unit, _ = norm_stats(tokg[at, seq].astype(F32))
-            part[seq : seq + 1, :] += jnp.sum(
-                gnf[at, pl.ds(64 * seq, 64), :] * unit, axis=0, keepdims=True
+            part_r[seq : seq + 1, :] += jnp.sum(
+                gnp[at, pl.ds(64 * seq, 64), :].astype(F32) * unit, axis=0, keepdims=True
             )
         return carry
 
-    lax.fori_loop(0, 4, gather, 0)
-    one = Swap(head, blk, "blk", lambda i: part, lambda i: sums_in.at[i], asem)
-    one.start()
-    sums_in[blk] = part[...]
-    scatter.join()
-    one.arrive()
-    total = sums_in[0]
+    lax.fori_loop(0, 4, gather_r, 0)
+    one_r = Swap(head, blk, "blk", lambda i: part_r, lambda i: sums_in_r.at[i], asem_r)
+    one_r.start()
+    sums_in_r[blk] = part_r[...]
+    gswap.start_one(2)
+    gswap.relay()
+    gswap.start_one(1)
+    scatter_q.join()
+    uswap_r.arrive()
+    usum[...] = sum_four(uin).astype(BF)
+    vswap.start()
+    g_up[blk] = usum[blk]
+    one_r.arrive()
+    total = sums_in_r[0]
     for i in range(1, 8):
-        total = total + sums_in[i]
-    parts[head] = total
-    two = Swap(head, blk, "head", lambda i: parts.at[head], lambda i: parts.at[i], bsem)
-    two.start()
-    osum[...] = scatter.total().astype(BF)
-    xswap = Swap(head, blk, "head", lambda i: osum.at[i], lambda i: gq.at[i], xsem)
-    xswap.start()
-    gq[head] = osum[head]
-    two.arrive()
-    total = (parts[0] + parts[1]) + (parts[2] + parts[3])
+        total = total + sums_in_r[i]
+    parts_r[head] = total
+    two_r = Swap(head, blk, "head", lambda i: parts_r.at[head], lambda i: parts_r.at[i], csem_r)
+    two_r.start()
+    total = middle[...] + outq[lax.div(blk, 2)].astype(F32)
+    for i in range(1, 4):
+        outs[i - 1].wait_recv()
+        total = total + oin[i].astype(F32)
+    output[...] = total.astype(BF)
+    dfold.arrive()
+    g_down[...] = sum_four(din)
+    osum_q[...] = scatter_q.total().astype(BF)
+    xswap_q = Swap(head, blk, "head", lambda i: osum_q.at[i], lambda i: gq.at[i], xsem_q)
+    xswap_q.start()
+    gq[head] = osum_q[head]
+    xswap.arrive()
+    g_out[...] = sum_four(zin)
+    two_r.arrive()
+    total = (parts_r[0] + parts_r[1]) + (parts_r[2] + parts_r[3])
     grad_attn[...] = columns[0] * total[0:1] + columns[1] * total[1:2]
     grad_mlp[...] = columns[0] * total[2:3] + columns[1] * total[3:4]
     gswap.arrive()
     for seq in range(2):
         rows = slice(64 * seq, 64 * seq + 64)
-        grad = sum_four([gin[i, rows, :] for i in range(4)])
+        grad = sum_four([gin_r[i, rows, :] for i in range(4)])
         unit, spread = norm_stats(tokg[head, seq].astype(F32))
         grad_tokens[rows, :] = grad_middle[rows, :] + norm_back(
             unit, spread, grad, scales[seq : seq + 1, :]
         )
-    xswap.arrive()
-    for copies in (gswap, scatter, xswap, one, two):
+    vswap.arrive()
+    xswap_q.arrive()
+    for z in range(4):
+        kv_move(z).drain()
+    for copy in outs:
+        copy.wait_send()
+    for copies in (
+        scatter, uswap_r, dfold, vswap, xswap, qmove, gswap, scatter_q, xswap_q, one_r, two_r
+    ):
         copies.drain()
-
-
-def phase_five_kernel(back, tabg, normed, wq, tokg, scales, grad_middle, sums, ttab, tix):
+    for at in range(4):
+        move(at).drain()
+    for i in range(4):
+        for copy in halves(i):
+            copy.wait_send()
+        if i:
+            onward(i).wait_send()
+    for copies in (
+        zswap, line, tline, plane, one, two, uswap, oline,
+        uline, dline, oplane, cplane, everyone, nplane, backward,
+    ):
+        copies.drain()
+
+
+def whole(count):
+    return [pl.BlockSpec(memory_space=pltpu.VMEM)] * count
+
+
+def layer(*operands):
     dma = pltpu.SemaphoreType.DMA
+    shape = jax.ShapeDtypeStruct
     return pl.pallas_call(
-        fifth_kernel,
+        layer_kernel,
         out_shape=(
-            jax.ShapeDtypeStruct((128, 1024), F32),
-            jax.ShapeDtypeStruct((4, 32, 768), BF),
-            jax.ShapeDtypeStruct((8, 1024), F32),
-            jax.ShapeDtypeStruct((8, 1024), F32),
+            shape((128, 1024), BF),
+            shape((128, 1024), F32),
+            shape((8, 32, 512), BF),
+            shape((32, 1024), F32),
+            shape((128, 1024), F32),
+            shape((4, 32, 768), BF),
+            shape((8, 1024), F32),
+            shape((8, 1024), F32),
         ),
-        in_specs=whole(9) + [pl.BlockSpec(memory_space=pltpu.SMEM)],
-        out_specs=whole(4),
+        in_specs=whole(10) + [pl.BlockSpec(memory_space=pltpu.SMEM)],
+        out_specs=whole(8),
         scratch_shapes=[
+            pltpu.VMEM((4, 8, 96, 128), BF),
+            pltpu.VMEM((4, 128, 1024), BF),
+            pltpu.VMEM((4, 8, 32, 768), BF),
+            pltpu.VMEM((8, 1024), F32),
+            pltpu.VMEM((4, 64, 128), F32),
+            pltpu.VMEM((4, 2, 64, 1024), BF),
+            pltpu.VMEM((4, 128, 256), F32),
+            pltpu.VMEM((4, 8, 256), F32),
+            pltpu.VMEM((4, 8, 32, 128), BF),
+            pltpu.VMEM((128, 1024), F32),
+            pltpu.VMEM((128, 1024), F32),
+            pltpu.VMEM((4, 128, 1024), BF),
+            pltpu.VMEM((4, 128, 1024), BF),
+            pltpu.VMEM((4, 8, 32, 512), BF),
+            pltpu.VMEM((4, 4, 2, 32, 1024), BF),
+            pltpu.VMEM((8, 1024), F32),
+            pltpu.VMEM((4, 32, 768), BF),
+            pltpu.VMEM((256, 64), F32),
+            pltpu.VMEM((8, 1024), F32),
+            pltpu.VMEM((8, 8, 1024), F32),
+            pltpu.VMEM((4, 8, 1024), F32),
+            pltpu.VMEM((8, 4, 96, 128), BF),
+            pltpu.VMEM((8, 32, 512), BF),
+            pltpu.VMEM((4, 32, 1024), BF),
+            pltpu.VMEM((4, 8, 32, 512), BF),
+            pltpu.VMEM((4, 128, 1024), BF),
+            pltpu.VMEM((4, 8, 32, 1024), BF),
+            pltpu.VMEM((8, 128, 1024), BF),
+            pltpu.VMEM((128, 2048), BF),
+            pltpu.VMEM((2, 2048 // KEYS, KEYS, 256), F32),
+            pltpu.VMEM((4, 8, 32, 128), BF),
+            pltpu.VMEM((4, 8, 32, 128), BF),
+            pltpu.VMEM((4, 128, 256), BF),
+            pltpu.VMEM((8, 128, 1024), BF),
+            pltpu.VMEM((8, 128, 512), BF),
+            pltpu.VMEM((8, 128, 512), BF),
+            pltpu.VMEM((2, 4, 2, 128, 1024), BF),
+            pltpu.VMEM((2, 4, 128, 1024), BF),
+            pltpu.VMEM((4, 128, 1024), BF),
+            pltpu.VMEM((4, 128, 1024), BF),
+            pltpu.VMEM((4, 8, 32, 128), BF),
+            pltpu.VMEM((128, 1024), BF),
+            pltpu.VMEM((8, 256, 128), BF),
+            pltpu.VMEM((8, 256, 128), BF),
+            pltpu.VMEM((8, 128, 256), BF),
+            pltpu.VMEM((8, 128, 256), BF),
+            pltpu.VMEM((8, 8, 256), F32),
+            pltpu.VMEM((64, 2048), BF),
+            pltpu.VMEM((2, 256, 128), F32),
+            pltpu.VMEM((8, 64, 256), F32),
+            pltpu.VMEM((8, 4, 96, 128), BF),
+            pltpu.VMEM((8, 4, 96, 128), BF),
+            pltpu.VMEM((4, 128, 1024), BF),
+            pltpu.VMEM((4, 128, 1024), BF),
+            pltpu.VMEM((128, 1024), BF),
+            pltpu.VMEM((128, 1024), BF),
+            pltpu.VMEM((4, 8, 32, 512), BF),
+            pltpu.VMEM((8, 32, 512), BF),
+            pltpu.VMEM((8, 32, 512), BF),
+            pltpu.VMEM((8, 32, 512), BF),
+            pltpu.VMEM((4, 4, 32, 1024), BF),
+            pltpu.VMEM((4, 4, 32, 1024), BF),
+            pltpu.VMEM((4, 4, 32, 1024), BF),
+            pltpu.VMEM((4, 32, 1024), BF),
+            pltpu.VMEM((4, 32, 1024), BF),
             pltpu.VMEM((4, 128, 768), BF),
-            pltpu.VMEM((4, 128, 1024), F32),
             pltpu.VMEM((4, 128, 1024), BF),
             pltpu.VMEM((128, 1024), BF),
             pltpu.VMEM((128, 1024), BF),
@@ -1502,10 +1454,34 @@
             pltpu.VMEM((4, 4, 32, 768), BF),
             pltpu.VMEM((4, 4, 32, 768), BF),
             pltpu.VMEM((4, 32, 768), BF),
-            pltpu.VMEM((256, 64), F32),
             pltpu.VMEM((8, 1024), F32),
             pltpu.VMEM((8, 8, 1024), F32),
             pltpu.VMEM((4, 8, 1024), F32),
+            dma((2, 4)),
+            dma((2, 2, 3)),
+            dma((2, 2, 3)),
+            dma((2, 7)),
+            dma((2, 8)),
+            dma((2, 4)),
+            dma((4, 2, 8)),
+            dma((2, 8)),
+            dma((2, 4)),
+            dma((2, 2, 3)),
+            dma((2, 2, 3)),
+            dma((2, 7)),
+            dma((2, 7)),
+            dma((2, 4, 8)),
+            dma((2, 7)),
+            dma((2, 2, 4)),
+            dma((2, 4)),
+            dma((2, 4, 8)),
+            dma((2, 4)),
+            dma((2, 4)),
+            dma((2, 4)),
+            dma((2, 8)),
+            dma((2, 4)),
+            dma((2, 4)),
+            dma((5, 2, 8)),
             dma((2, 4)),
             dma((2, 4)),
             dma((2, 4)),
@@ -1513,10 +1489,12 @@
             dma((2, 4)),
         ],
         compiler_params=pltpu.CompilerParams(
-            collective_id=4, has_side_effects=True, vmem_limit_bytes=48 << 20
+            collective_id=0, has_side_effects=True, vmem_limit_bytes=VMEM_LIMIT
         ),
-        name="fifth",
-    )(back, tabg, normed, wq, tokg, scales, grad_middle, sums, ttab, tix)
+        name="layer",
+    )(*operands)
+
+
 def blocked(
     tokens,
     positions,
@@ -1538,35 +1516,9 @@
     wq_parts = jnp.concatenate([kv_cols, wide[:, 0].reshape(32, 4, 256)], axis=-1)
     wq_parts = jnp.swapaxes(wq_parts, 0, 1)
     up_parts = jnp.transpose(w_up.reshape(32, 4, 8, 128), (2, 0, 1, 3)).reshape(8, 32, 512)
-    (
-        tiles, normed, wq, scales, table_all, tokens_all, mixed, lse,
-        grad_rx, grad_middle, middle, outq, grad_down, grad_up, grad_out, sums,
-    ) = front(
-        tokens, table, wq_parts, time_table, (scale_attn, scale_mlp), up_parts, w_out,
+    output, down_own, up_own, out_own, grad_tokens, grad_wq, grad_attn, grad_mlp = layer(
+        tokens, table, wq_parts, time_table, scale_attn, scale_mlp, up_parts, w_out,
         w_down, cotangent.reshape(128, 1024), time_index,
-    )
-    back, output, down_own, up_own, out_own = phase_four_kernel(
-        tiles,
-        grad_rx,
-        mixed,
-        lse,
-        outq,
-        middle,
-        grad_down,
-        grad_up,
-        grad_out.reshape(4, 4, 2, 32, 1024),
-    )
-    grad_tokens, grad_wq, grad_attn, grad_mlp = phase_five_kernel(
-        back,
-        table_all,
-        normed,
-        wq,
-        tokens_all,
-        scales,
-        grad_middle,
-        sums,
-        time_table,
-        time_index,
     )
     kv_cols = grad_wq[:, :, :512].reshape(4, 32, 4, 2, 64)
     wide = jnp.stack(

time: 220 us -> 200 us (0.909)
  Pallas kernels: 204 us -> 183 us
    pallas_call x3 -> x1, Pallas kernels: 204 us -> 183 us  [layer(): pl.pallas_call(layer_kernel, out_shape=(shape((128, 1024), BF), shape((12...]
    unnamed x40 -> x30, local copies, waits for them, and re-layouts: 7.5 us -> 6.95 us
where the time goes in v6:
time: 200 us; the launch traced here: 199 us
  Pallas kernels  183 us (92%)
  local copies, waits for them, and re-layouts  13.7 us (7%)
    pallas_call x1, Pallas kernels, layer(): pl.pallas_call(layer_kernel, out_shape=(shape((128, 1024), BF), shape((12...  183 us
    unnamed x30, local copies, waits for them, and re-layouts  6.95 us

profile of v6, /device:TPU:0, one launch (start us, length us, event | category | flops | bytes accessed | tf_op | source)
XLA Modules:
  0.0 199.1 jit_solution(12239185862756845204)
XLA Ops:
  0.6 0.0 copy-start.9
  0.7 0.7 copy-done.9
  1.3 0.0 copy-start.3
  1.3 0.3 multiply_cosine_fusion
  1.6 0.7 pad_maximum_fusion.1.tab
  2.4 0.0 copy-done.3
  2.4 0.1 copy.55
  2.5 0.0 copy-start.5
  2.5 0.8 reshape.83.upp
  3.3 0.1 copy-done.5
  3.5 0.3 reshape.80
  3.7 0.1 fusion
  3.9 0.1 copy_bitcast_fusion.4
  4.0 0.1 pad_maximum_fusion
  4.0 0.2 copy.35
  4.2 0.2 reshape.81
  4.4 0.2 reshape.91
  4.6 0.7 maximum_bitcast_fusion.wqp
  5.3 182.7 %layer.1 = (bf16[128,1024]{1,0:T(8,128)(2,1)}, f32[128,1024]{1,0:T(8,128)}, bf16[8,32,512]{2,1,0:T(8,128)(2,1)}, f32[32,1024]{1,0:T(8,128)}, f32[128,1024]{1,0:T...) custom-call(bf16[2,64,1024]{2,1,0:T(8,128)(2,1)} %tok.1, ...), custom_call_target="tpu_custom_call" | custom-call | tf_op jit(solution)/shard_map/layer/pallas_call | solution.py:1367
  188.0 0.8 slice.44
  188.8 0.9 slice.45
  189.8 0.1 stack_reshape.3
  189.9 0.2 reshape.87
  190.1 0.4 fusion.1
  190.5 0.1 convert_bitcast_fusion
  190.7 0.5 copy.41
  191.2 0.0 copy-start.2
  191.2 1.3 reshape.88
  192.5 0.0 copy-done.2
  192.5 0.2 reshape.90
  192.7 0.3 copy.42
  193.0 0.0 copy-start.4
  193.0 1.1 copy.54
  194.1 0.0 copy-start.1
  194.1 0.0 copy-done.4
  194.1 0.7 copy.64
  194.8 0.4 copy-done.1
  195.3 0.0 copy-start.6
  195.3 0.0 copy-start
  195.3 0.8 copy.65
  196.1 0.2 copy-done.6
  196.3 0.7 copy.66
  196.9 0.0 copy-done
  196.9 0.0 copy-start.8
  196.9 0.8 copy.67
  197.7 0.0 copy-done.8
  197.7 0.0 copy-start.7
  197.7 0.6 copy.68
  198.3 0.2 copy-done.7
  198.5 0.6 copy.69
  (8 shorter events, 0.1 us)
Async XLA Ops:
  0.6 0.7 copy-start.9
  1.3 1.0 copy-start.3
  2.5 0.9 copy-start.5
  191.2 1.3 copy-start.2
  193.0 1.1 copy-start.4
  194.1 1.1 copy-start.1
  195.3 1.0 copy-start.6
  195.3 1.7 copy-start
  196.9 0.8 copy-start.8
  197.7 0.8 copy-start.7

commit v7 on v6

--- a/solution.py
+++ b/solution.py
@@ -477,6 +477,17 @@
         def _():
             self.copy(self.slot(at), at, up, k + 1).start()
 
+    def hop(self, k):
+        head = self.head
+
+        @pl.when(head >= k)
+        def _():
+            self.step(head - k)
+
+        @pl.when(head + k <= 3)
+        def _():
+            self.step(head + k)
+
     def drain(self):
         head = self.head
         for k in range(3):
@@ -792,8 +803,9 @@
 
 
 def layer_kernel(
-    tok, tab, wqp, ttab, sca, scm, upp, out_own, down_own, cot_own, tix,
-    output, g_down, g_up, g_out, grad_tokens, gq, grad_attn, grad_mlp,
+    tok, pos, freq, w_qkv, ttab, sca, scm, w_up, out_own, down_own, cot_own, tix,
+    output, grad_tokens, g_qkv, g_out, g_up, g_down, grad_attn, grad_mlp,
+    tab, wqp, upp, gq, up_own,
     tiles, normed, wq, scales, tabg, tokg, mixed, lse, grad_rx, grad_middle, middle, outq, grad_down,
     grad_up, grad_out, sums, wqz, turned, part, sums_in, parts, out_tiles, upz, outz, up, down, out, cots,
     kvt, scores, att, received, attended, n2g, act, gh, pairs, prx, gsend, gin, tsend, branch, queries,
@@ -805,6 +817,23 @@
 ):
     head, blk = lax.axis_index("head"), lax.axis_index("blk")
     core = lax.rem(blk, 2)
+    for group in range(4):
+        for i in range(2):
+            at = 256 * group + 128 * i
+            keys = w_qkv[:, 1024 + at : 1152 + at].astype(F32)
+            values = w_qkv[:, 2048 + at : 2176 + at].astype(F32)
+            for right in range(2):
+                lanes = slice(256 * i + 128 * right, 256 * i + 128 * right + 128)
+                wqp[group, :, lanes] = join_halves(keys, values, right).astype(BF)
+        wqp[group, :, 512:768] = w_qkv[:, 256 * group : 256 * group + 256]
+    angles = [freq[:, 0:64] * pos[seq : seq + 1, :].astype(F32) for seq in range(2)]
+    tab[...] = jnp.transpose(
+        jnp.concatenate([turn(angle) for angle in angles for turn in (jnp.cos, jnp.sin)], axis=0)
+    )
+    for i in range(8):
+        for group in range(4):
+            at = 128 * (8 * group + i)
+            upp[i, :, 128 * group : 128 * group + 128] = w_up[:, at : at + 128]
     greet_all(head, blk)
     zswap = Swap(head, blk, "head", lambda i: wqp.at[i], lambda i: wqz.at[i], zsem)
     zswap.start()
@@ -917,6 +946,8 @@
     for at in range(4):
         move(at).arrive()
     oplane.start()
+    uline.hop(1)
+    dline.start()
     kvt[...] = jnp.transpose(tiles[:, :, 0:64, :].reshape(2048, 128))
 
     def attend(step, carry):
@@ -930,14 +961,14 @@
             for c in range(2048 // KEYS):
                 keys = tiles[c // 2, 4 * (c % 2) : 4 * (c % 2) + 4, 0:64, :].reshape(KEYS, 128)
                 part = jnp.dot(keys, query, preferred_element_type=F32)
-                scores[side, c] = part
+                scores[c] = part
                 peak = jnp.max(part.reshape(KEYS // 8, 8, 256), axis=0)
                 top = peak if top is None else jnp.maximum(top, peak)
             top = jnp.max(top, axis=0, keepdims=True)
             total = jnp.zeros((8, 256), F32)
             mix = jnp.zeros((64, 256), F32)
             for c in range(2048 // KEYS):
-                weights = jnp.exp2((scores[side, c] - top) * EXP_SCALE)
+                weights = jnp.exp2((scores[c] - top) * EXP_SCALE)
                 total = total + group_rows(weights)
                 mix = mix + jnp.dot(
                     kvt[64:128, KEYS * c : KEYS * c + KEYS],
@@ -953,18 +984,10 @@
         att[z] = both.astype(BF).reshape(8, 32, 128)
         everyone.start(3 - step)
 
-        @pl.when(step == 0)
-        def _():
-            uline.step(line_order(head, jnp.int32(1)))
-
-        @pl.when(step == 1)
-        def _():
-            uline.step(line_order(head, jnp.int32(2)))
-
         @pl.when(step == 2)
         def _():
-            uline.step(line_order(head, jnp.int32(3)))
-            dline.start()
+            uline.hop(2)
+            dline.hop(1)
             for i in range(3):
                 oplane.forward(i)
             cplane.start()
@@ -974,7 +997,6 @@
     lse[...] = jnp.zeros_like(lse)
     lax.fori_loop(0, 4, attend, 0)
     received[head, blk] = att[head, blk]
-    dline.step(line_order(head, jnp.int32(1)))
     for i in range(-1, 3):
         oplane.arrive(i)
     middle[...] = tok[...].astype(F32).reshape(128, 1024)
@@ -999,10 +1021,11 @@
     nplane = Plane(head, blk, n2g.at[blk], lambda i: n2g.at[i], nsem)
     for i in (1, 2, 0):
         nplane.first[i].start()
-    dline.step(line_order(head, jnp.int32(2)))
+    uline.hop(3)
+    dline.hop(2)
     nplane.first[3].start()
     cplane.finish()
-    dline.step(line_order(head, jnp.int32(3)))
+    dline.hop(3)
     sibling = flip(blk, 1)
 
     def halves(i):
@@ -1117,7 +1140,7 @@
         outs.append(
             send(outq.at[lax.div(peer, 2)], oin.at[i], qsem_r.at[0, i], qsem_r.at[1, i], head, peer)
         )
-    vswap = Swap(head, blk, "blk", lambda i: usum.at[i], lambda i: g_up.at[i], vsem)
+    vswap = Swap(head, blk, "blk", lambda i: usum.at[i], lambda i: up_own.at[i], vsem)
     xswap = Swap(head, blk, "head", lambda i: osum.at[i], lambda i: zin.at[i], xsem)
     left = half_lane((256, 128))
     keyt[...] = jnp.transpose(tiles[:, :, 0:64, :].reshape(2048, 128))[:64]
@@ -1300,7 +1323,7 @@
     uswap_r.arrive()
     usum[...] = sum_four(uin).astype(BF)
     vswap.start()
-    g_up[blk] = usum[blk]
+    up_own[blk] = usum[blk]
     one_r.arrive()
     total = sums_in_r[0]
     for i in range(1, 8):
@@ -1334,7 +1357,20 @@
             unit, spread, grad, scales[seq : seq + 1, :]
         )
     vswap.arrive()
+    for i in range(8):
+        for group in range(4):
+            at = 128 * (8 * group + i)
+            g_up[:, at : at + 128] = up_own[i, :, 128 * group : 128 * group + 128].astype(F32)
     xswap_q.arrive()
+    for group in range(4):
+        for i in range(2):
+            first = gq[group, :, 256 * i : 256 * i + 128].astype(F32)
+            second = gq[group, :, 256 * i + 128 : 256 * i + 256].astype(F32)
+            at = 256 * group + 128 * i
+            for right in range(2):
+                lanes = slice(1024 + 1024 * right + at, 1152 + 1024 * right + at)
+                g_qkv[:, lanes] = join_halves(first, second, right)
+        g_qkv[:, 256 * group : 256 * group + 256] = gq[group, :, 512:768].astype(F32)
     for z in range(4):
         kv_move(z).drain()
     for copy in outs:
@@ -1369,16 +1405,21 @@
         out_shape=(
             shape((128, 1024), BF),
             shape((128, 1024), F32),
-            shape((8, 32, 512), BF),
+            shape((32, 3072), F32),
             shape((32, 1024), F32),
+            shape((32, 4096), F32),
             shape((128, 1024), F32),
-            shape((4, 32, 768), BF),
             shape((8, 1024), F32),
             shape((8, 1024), F32),
         ),
-        in_specs=whole(10) + [pl.BlockSpec(memory_space=pltpu.SMEM)],
+        in_specs=whole(11) + [pl.BlockSpec(memory_space=pltpu.SMEM)],
         out_specs=whole(8),
         scratch_shapes=[
+            pltpu.VMEM((64, 128), F32),
+            pltpu.VMEM((4, 32, 768), BF),
+            pltpu.VMEM((8, 32, 512), BF),
+            pltpu.VMEM((4, 32, 768), BF),
+            pltpu.VMEM((8, 32, 512), BF),
             pltpu.VMEM((4, 8, 96, 128), BF),
             pltpu.VMEM((4, 128, 1024), BF),
             pltpu.VMEM((4, 8, 32, 768), BF),
@@ -1408,7 +1449,7 @@
             pltpu.VMEM((4, 8, 32, 1024), BF),
             pltpu.VMEM((8, 128, 1024), BF),
             pltpu.VMEM((128, 2048), BF),
-            pltpu.VMEM((2, 2048 // KEYS, KEYS, 256), F32),
+            pltpu.VMEM((2048 // KEYS, KEYS, 256), F32),
             pltpu.VMEM((4, 8, 32, 128), BF),
             pltpu.VMEM((4, 8, 32, 128), BF),
             pltpu.VMEM((4, 128, 256), BF),
@@ -1495,6 +1536,38 @@
     )(*operands)
 
 
+def finish_kernel(*refs):
+    count = (len(refs) - 1) // 3
+    sems = refs[-1]
+    arrive = [
+        pltpu.make_async_copy(refs[i], refs[2 * count + i], sems.at[0, i]) for i in range(count)
+    ]
+    leave = [
+        pltpu.make_async_copy(refs[2 * count + i], refs[count + i], sems.at[1, i])
+        for i in range(count)
+    ]
+    for copy in arrive:
+        copy.start()
+    for i in range(count):
+        arrive[i].wait()
+        leave[i].start()
+    for copy in leave:
+        copy.wait()
+
+
+def finish(results):
+    spec = [pl.BlockSpec(memory_space=pl.ANY)] * len(results)
+    return pl.pallas_call(
+        finish_kernel,
+        out_shape=tuple(jax.ShapeDtypeStruct(x.shape, x.dtype) for x in results),
+        in_specs=spec,
+        out_specs=spec,
+        scratch_shapes=[pltpu.VMEM(x.shape, x.dtype) for x in results]
+        + [pltpu.SemaphoreType.DMA((2, len(results)))],
+        name="finish",
+    )(*results)
+
+
 def blocked(
     tokens,
     positions,
@@ -1508,35 +1581,24 @@
     scale_mlp,
     cotangent,
 ):
-    cosine, sine = rotary_tables(positions, HEAD_DIM)
-    cosine, sine = cosine[:, :, 0], sine[:, :, 0]
-    table = jnp.concatenate([cosine[0], sine[0], cosine[1], sine[1]], axis=-1)
-    wide = w_qkv.reshape(32, 3, 4, 4, 64)
-    kv_cols = jnp.stack([wide[:, 1], wide[:, 2]], axis=3).reshape(32, 4, 512)
-    wq_parts = jnp.concatenate([kv_cols, wide[:, 0].reshape(32, 4, 256)], axis=-1)
-    wq_parts = jnp.swapaxes(wq_parts, 0, 1)
-    up_parts = jnp.transpose(w_up.reshape(32, 4, 8, 128), (2, 0, 1, 3)).reshape(8, 32, 512)
-    output, down_own, up_own, out_own, grad_tokens, grad_wq, grad_attn, grad_mlp = layer(
-        tokens, table, wq_parts, time_table, scale_attn, scale_mlp, up_parts, w_out,
-        w_down, cotangent.reshape(128, 1024), time_index,
-    )
-    kv_cols = grad_wq[:, :, :512].reshape(4, 32, 4, 2, 64)
-    wide = jnp.stack(
-        [grad_wq[:, :, 512:].reshape(4, 32, 4, 64), kv_cols[:, :, :, 0], kv_cols[:, :, :, 1]],
-        axis=0,
-    )
-    qkv_own = jnp.transpose(wide, (2, 0, 1, 3, 4)).reshape(32, 3072).astype(F32)
-    up_own = jnp.transpose(up_own.reshape(8, 32, 4, 128), (1, 2, 0, 3)).reshape(32, 4096)
-    return (
-        output.reshape(2, 64, 1024),
-        grad_tokens.reshape(2, 64, 1024),
-        qkv_own,
-        out_own,
-        up_own.astype(F32),
-        down_own,
-        grad_attn,
-        grad_mlp,
-    )
+    half_dim = HEAD_DIM // 2
+    frequency = 10000.0 ** (-jnp.arange(half_dim, dtype=jnp.float32) / half_dim)
+    results = layer(
+        tokens,
+        positions,
+        jnp.broadcast_to(frequency[:, None], (half_dim, 128)),
+        w_qkv,
+        time_table,
+        scale_attn,
+        scale_mlp,
+        w_up,
+        w_out,
+        w_down,
+        cotangent.reshape(128, 1024),
+        time_index,
+    )
+    output, grad_tokens, *others = finish(results)
+    return (output.reshape(2, 64, 1024), grad_tokens.reshape(2, 64, 1024), *others)
 
 
 def solution(mesh):

time: 200 us -> 187 us (0.935)
  local copies, waits for them, and re-layouts: 13.7 us -> 0.68 us
  Pallas kernels: 183 us -> 185 us
    unnamed x30 -> x0, local copies, waits for them, and re-layouts: 6.95 us -> none
    pallas_call x0 -> x1, Pallas kernels: none -> 2.58 us  [finish(): pl.pallas_call(finish_kernel, out_shape=tuple((jax.ShapeDtypeStruct(x.sha...]
    convert_element_type x4 -> x0, local copies, waits for them, and re-layouts: 2.31 us -> none  [the longest x2 1.84 us: blocked(): qkv_own = jnp.transpose(wide, (2, 0, 1, 3, 4)).reshape(32, 3072).astype(F32)]
    slice x4 -> x0, local copies, waits for them, and re-layouts: 2.26 us -> none  [the longest x1 0.91 us: blocked(): kv_cols = grad_wq[:, :, :512].reshape(4, 32, 4, 2, 64)]
where the time goes in v7:
time: 187 us
  Pallas kernels  185 us (99%)
    pallas_call x1, Pallas kernels, layer(): pl.pallas_call(layer_kernel, out_shape=(shape((128, 1024), BF), shape((12...  183 us

profile of v7, /device:TPU:0, one launch (start us, length us, event | category | flops | bytes accessed | tf_op | source)
XLA Modules:
  0.0 186.6 jit_solution(8168068198108549788)
XLA Ops:
  0.6 0.7 broadcast_in_dim.2.freq
  1.3 182.5 %layer.1 = (bf16[128,1024]{1,0:T(8,128)(2,1)}, f32[128,1024]{1,0:T(8,128)}, f32[32,3072]{1,0:T(8,128)}, f32[32,1024]{1,0:T(8,128)}, f32[32,4096]{1,0:T(8,128)}, ...) custom-call(bf16[2,64,1024]{2,1,0:T(8,128)(2,1)} %tok.1, s32[2,64]{1,0:T(2,128)} %pos.1, ...), custom_call_target="tpu_custom_call" | custom-call | tf_op jit(solution)/shard_map/layer/pallas_call | solution.py:1403
  183.9 2.6 %finish.1 = (bf16[128,1024]{1,0:T(8,128)(2,1)}, f32[128,1024]{1,0:T(8,128)}, f32[32,3072]{1,0:T(8,128)}, f32[32,1024]{1,0:T(8,128)}, f32[32,4096]{1,0:T(8,128)},...) custom-call(bf16[128,1024]{1,0:T(8,128)(2,1)} %get-tuple-element.24.refs_0_, ...), custom_call_target="tpu_custom_call" | custom-call | tf_op jit(solution)/shard_map/finish/pallas_call | solution.py:1560
  (1 shorter events, 0.0 us)

commit v8 on v7

--- a/solution.py
+++ b/solution.py
@@ -434,6 +434,57 @@
 
     def drain(self):
         for copy in self.first + self.passed:
+            copy.wait_send()
+
+
+class Split:
+    def __init__(self, head, blk, own, slot, half, sems):
+        sibling, across, along, far = (flip(blk, k) for k in (1, 2, 4, 6))
+
+        def copy(source, target, i, peer):
+            return send(source, target, sems.at[0, i], sems.at[1, i], head, peer)
+
+        self.first = [
+            copy(own, slot(blk), 0, sibling),
+            copy(own, slot(blk), 1, across),
+            copy(own, slot(blk), 2, along),
+        ]
+        self.cross = [
+            copy(half(across, 1), half(across, 1), 3, along),
+            copy(half(along, 0), half(along, 0), 4, across),
+        ]
+        self.passed = [
+            copy(slot(peer), slot(peer), 5 + i, sibling)
+            for i, peer in enumerate((across, along, far))
+        ]
+
+    def start(self):
+        for i in (1, 2, 0):
+            self.first[i].start()
+
+    def forward(self, i):
+        if i < 2:
+            self.first[i + 1].wait_recv()
+            self.cross[i].start()
+        else:
+            for copy in self.cross:
+                copy.wait_recv()
+        self.passed[i].start()
+
+    def arrive(self, i):
+        if i < 0:
+            self.first[0].wait_recv()
+        else:
+            self.passed[i].wait_recv()
+
+    def finish(self):
+        for i in range(3):
+            self.forward(i)
+        for i in range(-1, 3):
+            self.arrive(i)
+
+    def drain(self):
+        for copy in self.first + self.cross + self.passed:
             copy.wait_send()
 
 
@@ -984,13 +1035,16 @@
         att[z] = both.astype(BF).reshape(8, 32, 128)
         everyone.start(3 - step)
 
+        @pl.when(step == 1)
+        def _():
+            cplane.start()
+
         @pl.when(step == 2)
         def _():
             uline.hop(2)
             dline.hop(1)
             for i in range(3):
                 oplane.forward(i)
-            cplane.start()
 
         return carry
 
@@ -1018,12 +1072,13 @@
         rows = slice(64 * seq, 64 * seq + 64)
         unit, _ = norm_stats(middle[rows, :])
         n2g[blk, rows, :] = (unit * scales[2 + seq : 3 + seq, :]).astype(BF)
-    nplane = Plane(head, blk, n2g.at[blk], lambda i: n2g.at[i], nsem)
+    nplane = Split(
+        head, blk, n2g.at[blk], lambda i: n2g.at[i], lambda i, h: n2g.at[i, pl.ds(64 * h, 64)], nsem
+    )
     for i in (1, 2, 0):
         nplane.first[i].start()
     uline.hop(3)
     dline.hop(2)
-    nplane.first[3].start()
     cplane.finish()
     dline.hop(3)
     sibling = flip(blk, 1)
@@ -1052,7 +1107,11 @@
         if i == 0:
             nplane.arrive(-1)
         else:
-            nplane.forward(i - 1)
+            if i == 1:
+                nplane.forward(0)
+                nplane.forward(1)
+            elif i == 3:
+                nplane.forward(2)
             if i > 1:
                 reduce(i - 1)
             nplane.arrive(i - 1)
@@ -1206,7 +1265,7 @@
             dqt[q] = dq
             return inner
 
-        lax.fori_loop(0, 8, query_step, 0)
+        lax.fori_loop(0, 8, query_step, 0, unroll=4)
         scale = jnp.where(left, SCORE_SCALE, 1.0)
         for c in range(2):
             bsend[4 * c : 4 * c + 4, pl.ds(z, 1), 0:64, :] = (
@@ -1286,20 +1345,23 @@
                 )
                 query = query * both[0] + lane_swap(query) * both[1]
                 gp[at, rows, 512 + 128 * i : 640 + 128 * i] = query.astype(BF)
-        gnp[at] = contract_cols(gp[at], wq[...].reshape(1024, 768)).astype(BF)
         return carry
 
     for step in (3, 2, 1, 0):
         unturn(step, 0)
-        if step == 3:
-            gswap.start_far()
-            gswap.start_one(3)
     for group in range(4):
         lanes = slice(256 * group, 256 * group + 256)
         value = contract_rows(normed[:, :, lanes].reshape(512, 256), gp[...].reshape(512, 768))
         terms[group] = value.astype(BF).reshape(4, 2, 32, 768)
     scatter_q = Scatter(head, blk, terms, near_q, joined_q, far_q, osem_q)
     scatter_q.start()
+    for step in (3, 2, 1, 0):
+        at = flip(head, step)
+        gnp[at] = contract_cols(gp[at], wq[...].reshape(1024, 768)).astype(BF)
+        if step == 3:
+            gswap.start_far()
+            gswap.start_one(3)
+    scatter_q.join()
     part_r[...] = jnp.concatenate(
         [jnp.zeros((2, 1024), F32), sums[0:2, :], jnp.zeros((4, 1024), F32)], axis=0
     )
@@ -1319,7 +1381,6 @@
     gswap.start_one(2)
     gswap.relay()
     gswap.start_one(1)
-    scatter_q.join()
     uswap_r.arrive()
     usum[...] = sum_four(uin).astype(BF)
     vswap.start()
@@ -1501,7 +1562,7 @@
             dma((2, 4)),
             dma((2, 2, 3)),
             dma((2, 2, 3)),
-            dma((2, 7)),
+            dma((2, 8)),
             dma((2, 8)),
             dma((2, 4)),
             dma((4, 2, 8)),
@@ -1509,10 +1570,10 @@
             dma((2, 4)),
             dma((2, 2, 3)),
             dma((2, 2, 3)),
-            dma((2, 7)),
-            dma((2, 7)),
+            dma((2, 8)),
+            dma((2, 8)),
             dma((2, 4, 8)),
-            dma((2, 7)),
+            dma((2, 8)),
             dma((2, 2, 4)),
             dma((2, 4)),
             dma((2, 4, 8)),

time: 187 us -> 183 us (0.979)
  Pallas kernels: 185 us -> 181 us
    pallas_call x1, Pallas kernels: 183 us -> 178 us  [layer(): pl.pallas_call(layer_kernel, out_shape=(shape((128, 1024), BF), shape((12...]
where the time goes in v8:
time: 183 us; the launch traced here: 182 us
  Pallas kernels  181 us (99%)
    pallas_call x1, Pallas kernels, layer(): pl.pallas_call(layer_kernel, out_shape=(shape((128, 1024), BF), shape((12...  178 us

profile of v8, /device:TPU:0, one launch (start us, length us, event | category | flops | bytes accessed | tf_op | source)
XLA Modules:
  0.0 182.4 jit_solution(3323112736281492110)
XLA Ops:
  0.6 0.7 broadcast_in_dim.2.freq
  1.3 178.3 %layer.1 = (bf16[128,1024]{1,0:T(8,128)(2,1)}, f32[128,1024]{1,0:T(8,128)}, f32[32,3072]{1,0:T(8,128)}, f32[32,1024]{1,0:T(8,128)}, f32[32,4096]{1,0:T(8,128)}, ...) custom-call(bf16[2,64,1024]{2,1,0:T(8,128)(2,1)} %tok.1, s32[2,64]{1,0:T(2,128)} %pos.1, ...), custom_call_target="tpu_custom_call" | custom-call | tf_op jit(solution)/shard_map/layer/pallas_call | solution.py:1464
  179.6 2.6 %finish.1 = (bf16[128,1024]{1,0:T(8,128)(2,1)}, f32[128,1024]{1,0:T(8,128)}, f32[32,3072]{1,0:T(8,128)}, f32[32,1024]{1,0:T(8,128)}, f32[32,4096]{1,0:T(8,128)},...) custom-call(bf16[128,1024]{1,0:T(8,128)(2,1)} %get-tuple-element.24.refs_0_, ...), custom_call_target="tpu_custom_call" | custom-call | tf_op jit(solution)/shard_map/finish/pallas_call | solution.py:1621
  (1 shorter events, 0.0 us)

commit v9 on v8

--- a/solution.py
+++ b/solution.py
@@ -786,7 +786,10 @@
                 pl.semaphore_signal(
                     barrier, inc=1, device_id=(flip(head, kz), flip(blk, k)), device_id_type=MESH
                 )
-    pl.semaphore_wait(barrier, 31)
+
+
+def all_here():
+    pl.semaphore_wait(pltpu.get_barrier_semaphore(), 31)
 
 
 def group_rows(value):
@@ -868,6 +871,7 @@
 ):
     head, blk = lax.axis_index("head"), lax.axis_index("blk")
     core = lax.rem(blk, 2)
+    greet_all(head, blk)
     for group in range(4):
         for i in range(2):
             at = 256 * group + 128 * i
@@ -885,13 +889,13 @@
         for group in range(4):
             at = 128 * (8 * group + i)
             upp[i, :, 128 * group : 128 * group + 128] = w_up[:, at : at + 128]
-    greet_all(head, blk)
+    all_here()
     zswap = Swap(head, blk, "head", lambda i: wqp.at[i], lambda i: wqz.at[i], zsem)
     zswap.start()
     line = Line(head, blk, tok, lambda i: tokg.at[i], lsem)
     tline = Line(head, blk, tab, lambda i: tabg.at[i], tsem)
+    line.start()
     tline.start()
-    line.start()
     uswap = Swap(head, blk, "blk", lambda i: upp.at[i], lambda i: upz.at[i], usem)
     oline = Reach(head, blk, out_own, lambda i: outz.at[i], osem)
     uline = Line(head, blk, upz, lambda i: up.at[i], usem2)
@@ -940,8 +944,8 @@
 
         @pl.when(step > 0)
         def _():
+            line.step(at)
             tline.step(at)
-            line.step(at)
 
         for seq in range(2):
             unit, _ = norm_stats(tokg[at, seq].astype(F32))

time: 183 us -> 182 us (level)
  no operation moved by 1% of the time
where the time goes in v9:
time: 182 us
  Pallas kernels  181 us (99%)
    pallas_call x1, Pallas kernels, layer(): pl.pallas_call(layer_kernel, out_shape=(shape((128, 1024), BF), shape((12...  178 us

profile of v9, /device:TPU:0, one launch (start us, length us, event | category | flops | bytes accessed | tf_op | source)
XLA Modules:
  0.0 182.2 jit_solution(16010722110933624341)
XLA Ops:
  0.6 0.7 broadcast_in_dim.2.freq
  1.3 178.1 %layer.1 = (bf16[128,1024]{1,0:T(8,128)(2,1)}, f32[128,1024]{1,0:T(8,128)}, f32[32,3072]{1,0:T(8,128)}, f32[32,1024]{1,0:T(8,128)}, f32[32,4096]{1,0:T(8,128)}, ...) custom-call(bf16[2,64,1024]{2,1,0:T(8,128)(2,1)} %tok.1, s32[2,64]{1,0:T(2,128)} %pos.1, ...), custom_call_target="tpu_custom_call" | custom-call | tf_op jit(solution)/shard_map/layer/pallas_call | solution.py:1468
  179.4 2.6 %finish.1 = (bf16[128,1024]{1,0:T(8,128)(2,1)}, f32[128,1024]{1,0:T(8,128)}, f32[32,3072]{1,0:T(8,128)}, f32[32,1024]{1,0:T(8,128)}, f32[32,4096]{1,0:T(8,128)},...) custom-call(bf16[128,1024]{1,0:T(8,128)(2,1)} %get-tuple-element.24.refs_0_, ...), custom_call_target="tpu_custom_call" | custom-call | tf_op jit(solution)/shard_map/finish/pallas_call | solution.py:1625
  (1 shorter events, 0.0 us)

commit v10 on v9

--- a/solution.py
+++ b/solution.py
@@ -1269,7 +1269,7 @@
             dqt[q] = dq
             return inner
 
-        lax.fori_loop(0, 8, query_step, 0, unroll=4)
+        lax.fori_loop(0, 8, query_step, 0, unroll=8)
         scale = jnp.where(left, SCORE_SCALE, 1.0)
         for c in range(2):
             bsend[4 * c : 4 * c + 4, pl.ds(z, 1), 0:64, :] = (

time: 182 us -> 182 us (level)
  no operation moved by 1% of the time
where the time goes in v10:
time: 182 us
  Pallas kernels  181 us (99%)
    pallas_call x1, Pallas kernels, layer(): pl.pallas_call(layer_kernel, out_shape=(shape((128, 1024), BF), shape((12...  178 us

profile of v10, /device:TPU:0, one launch (start us, length us, event | category | flops | bytes accessed | tf_op | source)
XLA Modules:
  0.0 182.2 jit_solution(14581723845555075941)
XLA Ops:
  0.6 0.7 broadcast_in_dim.2.freq
  1.3 178.1 %layer.1 = (bf16[128,1024]{1,0:T(8,128)(2,1)}, f32[128,1024]{1,0:T(8,128)}, f32[32,3072]{1,0:T(8,128)}, f32[32,1024]{1,0:T(8,128)}, f32[32,4096]{1,0:T(8,128)}, ...) custom-call(bf16[2,64,1024]{2,1,0:T(8,128)(2,1)} %tok.1, s32[2,64]{1,0:T(2,128)} %pos.1, ...), custom_call_target="tpu_custom_call" | custom-call | tf_op jit(solution)/shard_map/layer/pallas_call | solution.py:1468
  179.4 2.6 %finish.1 = (bf16[128,1024]{1,0:T(8,128)(2,1)}, f32[128,1024]{1,0:T(8,128)}, f32[32,3072]{1,0:T(8,128)}, f32[32,1024]{1,0:T(8,128)}, f32[32,4096]{1,0:T(8,128)},...) custom-call(bf16[128,1024]{1,0:T(8,128)(2,1)} %get-tuple-element.24.refs_0_, ...), custom_call_target="tpu_custom_call" | custom-call | tf_op jit(solution)/shard_map/finish/pallas_call | solution.py:1625
  (1 shorter events, 0.0 us)
